TPU v7x, 32 devices: a whole 2x2x4 slice. The times are simulated.
32 devices in a mesh: groups: 2 (over x), slab: 16 (over z, y, core).
Axes of the slice: x: 2, y: 2, z: 4, core: 2. Of those that a mesh axis runs over, the one named last changes fastest.
Arguments:
- flow_state: float32 [10, 128, 8192], P('groups', 'slab'), parts along dimension 0, may hold values from -6 to 6
- flow_speed: float32 [4, 128, 8192], P('groups', 'slab'), parts along dimension 0, may hold values from -1 to 1
- wall_cell: int32 [16384], P(('groups', 'slab')), parts along dimension 0, may hold values from 0 to 65535
- base_shift: float32 [6, 8192], P('groups', 'slab'), parts along dimension 0, may hold values from -30 to 30
- normals: float32 [6, 8192], P('groups', 'slab'), parts along dimension 0, may hold values from -3 to 3
- centres: float32 [6, 8192], P('groups', 'slab'), parts along dimension 0, as said below
- tile_blocks: int32 [32, 4], P('groups'), parts along dimension 0, may hold values from 0 to 15, as said below
- near_count: int32 [32], P('groups'), parts along dimension 0, may hold values from 1 to 1024, 8192 in all
- near_nodes: float32 [6, 16384], P('groups', 'slab'), parts along dimension 0, as said below
Outputs:
- new_flow: float32 [10, 128, 8192], P('groups', 'slab'), parts along dimension 0
- coefficients: float32 [6, 8192], P('groups', 'slab'), parts along dimension 0
- node_shift: float32 [6, 16384], P('groups', 'slab'), parts along dimension 0
There are 2 independent parts, one for each index of `groups`. A program takes and returns all parts, laid end to end along the dimension named above; each array names one. Nothing has to cross between parts.
Inputs may be any that keep to these rules, and one draw needn't show every extreme that they name: `centres`: centre c has its first two coordinates in [0, 1) and its third in [0.4 * (c // 512), 0.4 * (c // 512 + 1)). `tile_blocks`: each row lists 4 consecutive centre blocks in rising order. `near_count`: the counts sum to 8192 and the largest equals 1024. `near_nodes`: A node of block m has its first two coordinates in [0, 1) and its third in [0.4 * b, 0.4 * (b + 1)) for one block b listed in tile_blocks[m].
All inputs are finite; a program needn't handle non-finite values.
Results may differ from a plain program's by a relative error of at most 0.0003.
Values sent between devices are 32-bit elements; how exact they have to be, the bound alone decides.
No kernel may reach another device: no remote copies, remote signals or barrier semaphores. Data moves between devices by JAX's collectives and lax.ppermute only.
A program may use at most 64 MiB of HBM per device.

v0:
```python
import jax
import jax.numpy as jnp
from jax import lax
from jax.sharding import PartitionSpec as P

ITERS = 3


FLUX_STEP = 0.2
SUPPORT = 0.15
DIAG_SHIFT = 0.5


def padded_2(cells, sides, width):
    for axis, dim in sides:
        count = lax.axis_size(axis)
        ends = count - 1
        head = lax.slice_in_dim(cells, 0, width, axis=dim)
        tail = lax.slice_in_dim(cells, cells.shape[dim] - width, cells.shape[dim], axis=dim)
        cells = jnp.concatenate(
            [
                lax.ppermute(tail, axis, [(i, (i + 1) % count) for i in range(ends)]),
                cells,
                lax.ppermute(head, axis, [((i + 1) % count, i) for i in range(ends)]),
            ],
            axis=dim,
        )
    return cells


def wendland(squared):
    scaled = jnp.sqrt(squared) / SUPPORT
    inside = jnp.maximum(1.0 - scaled, 0.0)
    square_in = inside * inside
    return square_in * square_in * (4.0 * scaled + 1.0)


def kernel_table(sources, targets):
    diff_a = sources[0][:, None] - targets[0][None, :]
    diff_b = sources[1][:, None] - targets[1][None, :]
    diff_c = sources[2][:, None] - targets[2][None, :]
    return wendland(diff_a * diff_a + diff_b * diff_b + diff_c * diff_c)


def flux_update(padded_q, padded_w, flow_state, cycle_speed):
    face_w = 0.5 * (padded_w[:-1] + padded_w[1:])
    below_face = padded_q[:, :-1]
    above_face = padded_q[:, 1:]
    axial_flux = 0.5 * face_w * (below_face + above_face) - 0.5 * jnp.abs(face_w) * (
        above_face - below_face
    )
    following = jnp.roll(flow_state, -1, axis=2)
    cycle_w = 0.5 * (cycle_speed + jnp.roll(cycle_speed, -1, axis=1))
    cycle_flux = 0.5 * cycle_w * (flow_state + following) - 0.5 * jnp.abs(cycle_w) * (
        following - flow_state
    )
    change = axial_flux[:, 1:] - axial_flux[:, :-1] + (cycle_flux - jnp.roll(cycle_flux, 1, axis=2))
    return flow_state - FLUX_STEP * change


def norm_of(residual):
    return lax.psum(jnp.sum(residual * residual, axis=1), "slab")


def rim_of(direction, block_size):
    return padded_2(direction, (("slab", 1),), block_size)


def shards(
    flow_state,
    flow_speed,
    wall_cell,
    base_shift,
    normals,
    centres,
    tile_blocks,
    near_count,
    near_nodes,
):
    var_count = flow_state.shape[0]
    stacked = jnp.concatenate([flow_state, flow_speed[0:1]], axis=0)
    padded = padded_2(stacked, (("slab", 1),), 1)
    new_flow = flux_update(padded[:var_count], padded[var_count], flow_state, flow_speed[1])
    pressure = new_flow[4].reshape(-1)
    wall_load = jnp.take(pressure, wall_cell)
    right_side = base_shift + normals * wall_load[None, :]
    my_index = lax.axis_index("slab")
    block_size = centres.shape[1]
    ext_centres = padded_2(centres, (("slab", 1),), block_size)
    coefficients = jnp.zeros_like(right_side)
    residual = right_side
    search = right_side
    energy = norm_of(residual)
    for iteration in range(ITERS):
        ext_dir = rim_of(search, block_size)
        apply_kernel = kernel_table(ext_centres, centres)
        product = jnp.dot(
            ext_dir,
            apply_kernel,
            precision=lax.Precision.HIGHEST,
            preferred_element_type=jnp.float32,
        )
        matrix_image = product + DIAG_SHIFT * search
        step_len = energy / lax.psum(jnp.sum(search * matrix_image, axis=1), "slab")
        coefficients = coefficients + step_len[:, None] * search
        residual = residual - step_len[:, None] * matrix_image
        new_energy = norm_of(residual)
        search = residual + (new_energy / energy)[:, None] * search
        energy = new_energy
    all_centres, all_coef = (
        lax.all_gather(centres, "slab", axis=1, tiled=True),
        lax.all_gather(coefficients, "slab", axis=1, tiled=True),
    )
    slots = near_nodes.shape[1]
    tile_rows = min(512, slots)
    own_count = near_count[my_index]
    own_tiles = tile_blocks[my_index]

    def one_block(position, result):
        row_start = position * tile_rows
        chosen = lax.dynamic_slice_in_dim(near_nodes, row_start, tile_rows, 1)
        node_sum = jnp.zeros((3, tile_rows), jnp.float32)
        for listed in range(own_tiles.shape[0]):
            offset = own_tiles[listed] * block_size
            near_centres = lax.dynamic_slice_in_dim(all_centres, offset, block_size, 1)
            near_coef = lax.dynamic_slice_in_dim(all_coef, offset, block_size, 1)
            kernel = kernel_table(near_centres, chosen)
            node_sum = node_sum + jnp.dot(
                near_coef,
                kernel,
                precision=lax.Precision.HIGHEST,
                preferred_element_type=jnp.float32,
            )
        live_mask = row_start + lax.iota(jnp.int32, tile_rows) < own_count
        node_sum = jnp.where(live_mask[None, :], node_sum, 0.0)
        return lax.dynamic_update_slice_in_dim(result, node_sum, row_start, 1)

    node_shift = lax.fori_loop(
        0, (own_count + tile_rows - 1) // tile_rows, one_block, jnp.zeros((3, slots), jnp.float32)
    )
    return (new_flow, coefficients, node_shift)


def solution(mesh):
    in_specs = (
        P("groups", "slab", None),
        P("groups", "slab", None),
        P(("groups", "slab")),
        P("groups", "slab"),
        P("groups", "slab"),
        P("groups", "slab"),
        P("groups", None),
        P("groups"),
        P("groups", "slab"),
    )
    out_specs = (P("groups", "slab", None), P("groups", "slab"), P("groups", "slab"))
    return jax.shard_map(shards, mesh=mesh, in_specs=in_specs, out_specs=out_specs, check_vma=False)
```

profile of v0, /device:TPU:1, one launch (start us, length us, event | category | flops | bytes accessed | tf_op | source)
XLA Modules:
  0.0 264.5 jit_solution(9540581059896083584)
XLA Ops:
  0.7 4.7 %collective-permute-start.4 = (f32[3,512]{1,0:T(4,128)}, f32[3,512]{1,0:T(4,128)S(1)}, u32[]{:S(2)}, u32[]{:S(2)}) collective-permute-start(f32[3,512]{1,0:T(4,128)} %param.16), channel_id=1, source_target_pairs={{0,1},{1,2},{2,3},{3,4},{4,5},{5,6},{6,7},{7,8},{8,9},{9,10},{10,1... | collective-permute-start | bytes 18440 | tf_op jit(solution)/shard_map/ppermute | solution.py:22
  5.3 1.9 collective-permute-start.5
  10.6 3.6 %collective-permute-start = (f32[6,1,8192]{2,0,1:T(8,128)}, f32[6,1,8192]{2,0,1:T(8,128)}, u32[]{:S(2)}, u32[]{:S(2)}) collective-permute-start(f32[6,1,8192]{2,0,1:T(8,128)} %copy.23), channel_id=1, source_target_pairs={{0,1},{1,2},{2,3},{3,4},{4,5},{5,6},{6,7},{7,8},{8,9},{9,10},{10,1... | collective-permute-start | bytes 589832 | tf_op jit(solution)/shard_map/ppermute | solution.py:22
  15.1 1.9 collective-permute-start.1
  19.7 3.4 %collective-permute-done.1 = f32[6,1,8192]{2,0,1:T(8,128)} collective-permute-done((f32[6,1,8192]{2,0,1:T(8,128)}, f32[6,1,8192]{2,0,1:T(8,128)}, u32[]{:S(2)}, u32[]{:S(2)}) %collective-permute-start.1) | collective-permute-done | bytes 196640 | tf_op jit(solution)/shard_map/ppermute | solution.py:24
  25.8 3.1 %gather_fusion = f32[512]{0:T(512)S(1)} fusion(f32[65536]{0:T(1024)S(1)} %bitcast.89, s32[1024]{0:T(1024)S(1)} %pad_clamp_fusion), kind=kCustom, calls=%fused_computation | custom fusion | bytes 6144 | tf_op jit(solution)/shard_map/jit(_take)/gather | solution.py:85
  29.0 1.9 collective-permute-start.2
  30.9 2.4 collective-permute-start.3
  33.4 4.2 %collective-permute-done.3 = f32[3,512]{1,0:T(4,128)S(1)} collective-permute-done((f32[3,512]{1,0:T(4,128)S(1)}, f32[3,512]{1,0:T(4,128)S(1)}, u32[]{:S(2)}, u32[]{:S(2)}) %collective-permute-start.3) | collective-permute-done | bytes 6176 | tf_op jit(solution)/shard_map/ppermute | solution.py:24
  37.6 4.1 %multiply_reduce_fusion.3 = (f32[3]{0:T(128)S(1)}, f32[3]{0:T(128)S(1)}, f32[3,512]{1,0:T(4,128)S(1)}) fusion(f32[3,512]{1,0:T(4,128)S(1)} %multiply_add_fusion.3, f32[512]{0:T(512)S(1)} %bitcast.121, f32[1536]{0:T(1024)S(1)} %get-tuple-element.232, f32[512]{0:T(512)S(1)} %bitcast.118, f32[1536]{0:T(1024)S(1)} %get-tuple-element.233, ...), kind=kOutput, calls=%fused_computation.189 | convolution fusion | flops 40912888 | bytes 49176 | tf_op jit(solution)/shard_map/dot_general | solution.py:97
  41.7 26.4 %all-reduce = (f32[3]{0:T(128)S(1)}, f32[3]{0:T(128)S(1)}) all-reduce(f32[3]{0:T(128)S(1)} %get-tuple-element.235, f32[3]{0:T(128)S(1)} %get-tuple-element.234), channel_id=1, replica_groups=mesh['groups'=2,'slab'=16] {'slab'}, use_global_device_ids=true, to_apply=%region_1.2 | all-reduce | flops 6 | bytes 48 | tf_op jit(solution)/shard_map/psum | solution.py:62
  68.3 32.5 %psum.44 = f32[3]{0:T(128)S(1)} all-reduce(f32[3]{0:T(128)S(1)} %get-tuple-element.264), channel_id=1, replica_groups=mesh['groups'=2,'slab'=16] {'slab'}, use_global_device_ids=true, to_apply=%region_5.6 | all-reduce | flops 3 | bytes 24 | tf_op jit(solution)/shard_map/psum | solution.py:62
  100.8 1.9 collective-permute-start.6
  102.7 2.4 collective-permute-start.7
  105.1 19.1 %all_gather.6 = f32[3,8192]{1,0:T(4,128)S(1)} all-gather(f32[3,512]{1,0:T(4,128)S(1)} %copy-done.3), channel_id=1, replica_groups=mesh['groups'=2,'slab'=16] {'slab'}, dimensions={1}, use_global_device_ids=true | all-gather | bytes 104448 | tf_op jit(solution)/shard_map/all_gather | solution.py:111
  126.8 4.1 %multiply_reduce_fusion.1 = (f32[3]{0:T(128)S(1)}, f32[3,512]{1,0:T(4,128)S(1)}) fusion(f32[3,512]{1,0:T(4,128)S(1)} %multiply_add_fusion.2, f32[512]{0:T(512)S(1)} %bitcast.122, f32[1536]{0:T(1024)S(1)} %get-tuple-element.232, f32[512]{0:T(512)S(1)} %bitcast.119, f32[1536]{0:T(1024)S(1)} %get-tuple-element.233, f32[512]{0:T(512)S(1)} %bitcast.116, ...), kind=kOutput, calls=%fused_computation.185 | convolution fusion | flops 40909820 | bytes 49164 | tf_op jit(solution)/shard_map/dot_general | solution.py:97
  130.9 29.0 %psum.45 = f32[3]{0:T(128)S(1)} all-reduce(f32[3]{0:T(128)S(1)} %get-tuple-element.310), channel_id=1, replica_groups=mesh['groups'=2,'slab'=16] {'slab'}, use_global_device_ids=true, to_apply=%region_7.8 | all-reduce | flops 3 | bytes 24 | tf_op jit(solution)/shard_map/psum | solution.py:104
  160.1 29.8 %psum.46 = f32[3]{0:T(128)S(1)} all-reduce(f32[3]{0:T(128)S(1)} %multiply_reduce_fusion), channel_id=1, replica_groups=mesh['groups'=2,'slab'=16] {'slab'}, use_global_device_ids=true, to_apply=%region_9.10 | all-reduce | flops 3 | bytes 24 | tf_op jit(solution)/shard_map/psum | solution.py:62
  190.0 1.9 collective-permute-start.8
  191.9 2.4 collective-permute-start.9
  196.9 4.1 %fusion.138 = f32[3]{0:T(128)S(1)} fusion(f32[3,512]{1,0:T(4,128)S(1)} %multiply_add_fusion.1, f32[512]{0:T(512)S(1)} %bitcast.123, f32[1536]{0:T(1024)S(1)} %get-tuple-element.232, f32[512]{0:T(512)S(1)} %bitcast.120, f32[1536]{0:T(1024)S(1)} %get-tuple-element.233, f32[512]{0:T(512)S(1)} %bitcast.117, f32[1536]{0:T(1024)S(1)} %get-tuple-element.231, ...), kind=kOutput, calls=%fused_computation.154 | convolution fusion | flops 40909820 | bytes 43020 | tf_op jit(solution)/shard_map/dot_general | solution.py:97
  201.0 27.4 %psum.47 = f32[3]{0:T(128)S(1)} all-reduce(f32[3]{0:T(128)S(1)} %fusion.138), channel_id=1, replica_groups=mesh['groups'=2,'slab'=16] {'slab'}, use_global_device_ids=true, to_apply=%region_11.12 | all-reduce | flops 3 | bytes 24 | tf_op jit(solution)/shard_map/psum | solution.py:104
  228.5 19.9 %all_gather.7 = f32[3,8192]{1,0:T(4,128)S(1)} all-gather(f32[3,512]{1,0:T(4,128)S(1)} %multiply_add_fusion), channel_id=1, replica_groups=mesh['groups'=2,'slab'=16] {'slab'}, dimensions={1}, use_global_device_ids=true | all-gather | bytes 104448 | tf_op jit(solution)/shard_map/all_gather | solution.py:112
  248.4 15.5 %while.13 = (s32[]{:T(128)}, f32[3,1024]{1,0:T(4,128)S(1)}, s32[]{:T(128)}, s32[]{:T(128)}, f32[3,512]{1,0:T(4,128)S(1)}, /*index=5*/f32[3,1024]{1,0:T(4,128)}, ...) while((s32[]{:T(128)}, f32[3,1024]{1,0:T(4,128)S(1)}, ...), condition=%wide.region_13.14_spmd, body=%wide.region_12.13_spmd.sunk | while | flops 54533128 | bytes 185611 | solution.py:138
  249.6 1.5 fusion.200
  251.1 1.5 convolution_add_fusion.5
  252.6 1.5 convolution_add_fusion.6
  254.8 1.5 fusion.202
  257.2 1.5 fusion.200
  258.7 1.5 convolution_add_fusion.5
  260.2 1.5 convolution_add_fusion.6
  262.4 1.5 fusion.202
  (81 shorter events, 15.8 us)
Async XLA Ops:
  0.6 16.8 %copy-start = (s32[16,4]{0,1:T(4,128)S(1)}, s32[16,4]{0,1:T(4,128)}, u32[]{:S(2)}) copy-start(s32[16,4]{0,1:T(4,128)} %param.17) | copy-start | bytes 772
  0.6 8.9 %copy-start.1 = (f32[5,8,8192]{2,1,0:T(8,128)S(1)}, f32[5,8,8192]{2,1,0:T(8,128)}, u32[]{:S(2)}) copy-start(f32[5,8,8192]{2,1,0:T(8,128)} %param.11) | copy-start | bytes 3932164
  0.7 17.8 %collective-permute-start.4 = (f32[3,512]{1,0:T(4,128)}, f32[3,512]{1,0:T(4,128)S(1)}, u32[]{:S(2)}, u32[]{:S(2)}) collective-permute-start(f32[3,512]{1,0:T(4,128)} %param.16), channel_id=1, source_target_pairs={{0,1},{1,2},{2,3},{3,4},{4,5},{5,6},{6,7},{7,8},{8,9},{9,10},{10,1... | collective-permute-start | bytes 18440 | tf_op jit(solution)/shard_map/ppermute | solution.py:22
  5.3 13.2 %collective-permute-start.5 = (f32[3,512]{1,0:T(4,128)}, f32[3,512]{1,0:T(4,128)S(1)}, u32[]{:S(2)}, u32[]{:S(2)}) collective-permute-start(f32[3,512]{1,0:T(4,128)} %param.16), channel_id=1, source_target_pairs={{1,0},{2,1},{3,2},{4,3},{5,4},{6,5},{7,6},{8,7},{9,8},{10,9},{11,1... | collective-permute-start | bytes 18440 | tf_op jit(solution)/shard_map/ppermute | solution.py:24
  9.5 7.9 %copy-start.3 = (f32[3,512]{1,0:T(4,128)S(1)}, f32[3,512]{1,0:T(4,128)}, u32[]{:S(2)}) copy-start(f32[3,512]{1,0:T(4,128)} %param.16) | copy-start | bytes 18436
  9.5 7.9 %copy-start.6 = (s32[512]{0:T(512)S(1)}, s32[512]{0:T(512)}, u32[]{:S(2)}) copy-start(s32[512]{0:T(512)} %param.13) | copy-start | bytes 6148
  9.5 8.6 %slice-start = ((f32[5,8,8192]{2,1,0:T(8,128)}), f32[5,8,1]{2,1,0:T(8,128)S(1)}, s32[]{:S(2)}) async-start(f32[5,8,8192]{2,1,0:T(8,128)} %param.11), calls=%async_computation | async-start | bytes 40960 | tf_op jit(solution)/shard_map/jit(_roll_static)/slice | solution.py:52
  10.6 7.9 %collective-permute-start = (f32[6,1,8192]{2,0,1:T(8,128)}, f32[6,1,8192]{2,0,1:T(8,128)}, u32[]{:S(2)}, u32[]{:S(2)}) collective-permute-start(f32[6,1,8192]{2,0,1:T(8,128)} %copy.23), channel_id=1, source_target_pairs={{0,1},{1,2},{2,3},{3,4},{4,5},{5,6},{6,7},{7,8},{8,9},{9,10},{10,1... | collective-permute-start | bytes 589832 | tf_op jit(solution)/shard_map/ppermute | solution.py:22
  15.1 8.0 %collective-permute-start.1 = (f32[6,1,8192]{2,0,1:T(8,128)}, f32[6,1,8192]{2,0,1:T(8,128)}, u32[]{:S(2)}, u32[]{:S(2)}) collective-permute-start(f32[6,1,8192]{2,0,1:T(8,128)} %copy.25), channel_id=1, source_target_pairs={{1,0},{2,1},{3,2},{4,3},{5,4},{6,5},{7,6},{8,7},{9,8},{10,9},{11,1... | collective-permute-start | bytes 589832 | tf_op jit(solution)/shard_map/ppermute | solution.py:24
  25.7 16.0 %copy-start.2 = (f32[5,8,8192]{2,1,0:T(8,128)}, f32[5,8,8192]{2,1,0:T(8,128)S(1)}, u32[]{:S(2)}) copy-start(f32[5,8,8192]{2,1,0:T(8,128)S(1)} %fusion.133) | copy-start | bytes 3932164
  25.7 3.3 %copy-start.7 = (f32[3,512]{1,0:T(4,128)S(1)}, f32[3,512]{1,0:T(4,128)}, u32[]{:S(2)}) copy-start(f32[3,512]{1,0:T(4,128)} %param.14) | copy-start | bytes 18436
  25.7 3.3 %copy-start.8 = (f32[3,512]{1,0:T(4,128)S(1)}, f32[3,512]{1,0:T(4,128)}, u32[]{:S(2)}) copy-start(f32[3,512]{1,0:T(4,128)} %param.15) | copy-start | bytes 18436
  29.0 4.4 %collective-permute-start.2 = (f32[3,512]{1,0:T(4,128)S(1)}, f32[3,512]{1,0:T(4,128)S(1)}, u32[]{:S(2)}, u32[]{:S(2)}) collective-permute-start(f32[3,512]{1,0:T(4,128)S(1)} %multiply_add_fusion.3), channel_id=1, source_target_pairs={{0,1},{1,2},{2,3},{3,4},{4,5},{5,6},{6,7},{7,8},{8,9},{9,10},{10,1... | collective-permute-start | bytes 18440 | tf_op jit(solution)/shard_map/ppermute | solution.py:22
  30.9 6.7 %collective-permute-start.3 = (f32[3,512]{1,0:T(4,128)S(1)}, f32[3,512]{1,0:T(4,128)S(1)}, u32[]{:S(2)}, u32[]{:S(2)}) collective-permute-start(f32[3,512]{1,0:T(4,128)S(1)} %multiply_add_fusion.3), channel_id=1, source_target_pairs={{1,0},{2,1},{3,2},{4,3},{5,4},{6,5},{7,6},{8,7},{9,8},{10,9},{11,1... | collective-permute-start | bytes 18440 | tf_op jit(solution)/shard_map/ppermute | solution.py:24
  100.8 26.0 %collective-permute-start.6 = (f32[3,512]{1,0:T(4,128)S(1)}, f32[3,512]{1,0:T(4,128)S(1)}, u32[]{:S(2)}, u32[]{:S(2)}) collective-permute-start(f32[3,512]{1,0:T(4,128)S(1)} %multiply_add_fusion.2), channel_id=1, source_target_pairs={{0,1},{1,2},{2,3},{3,4},{4,5},{5,6},{6,7},{7,8},{8,9},{9,10},{10,1... | collective-permute-start | bytes 18440 | tf_op jit(solution)/shard_map/ppermute | solution.py:22
  102.7 24.1 %collective-permute-start.7 = (f32[3,512]{1,0:T(4,128)S(1)}, f32[3,512]{1,0:T(4,128)S(1)}, u32[]{:S(2)}, u32[]{:S(2)}) collective-permute-start(f32[3,512]{1,0:T(4,128)S(1)} %multiply_add_fusion.2), channel_id=1, source_target_pairs={{1,0},{2,1},{3,2},{4,3},{5,4},{6,5},{7,6},{8,7},{9,8},{10,9},{11,1... | collective-permute-start | bytes 18440 | tf_op jit(solution)/shard_map/ppermute | solution.py:24
  126.8 67.6 %copy-start.9 = (s32[16]{0:T(128)S(1)}, s32[16]{0:T(128)}, u32[]{:S(2)}) copy-start(s32[16]{0:T(128)} %param.18) | copy-start | bytes 196
  190.0 5.8 %collective-permute-start.8 = (f32[3,512]{1,0:T(4,128)S(1)}, f32[3,512]{1,0:T(4,128)S(1)}, u32[]{:S(2)}, u32[]{:S(2)}) collective-permute-start(f32[3,512]{1,0:T(4,128)S(1)} %multiply_add_fusion.1), channel_id=1, source_target_pairs={{0,1},{1,2},{2,3},{3,4},{4,5},{5,6},{6,7},{7,8},{8,9},{9,10},{10,1... | collective-permute-start | bytes 18440 | tf_op jit(solution)/shard_map/ppermute | solution.py:22
  191.9 5.0 %collective-permute-start.9 = (f32[3,512]{1,0:T(4,128)S(1)}, f32[3,512]{1,0:T(4,128)S(1)}, u32[]{:S(2)}, u32[]{:S(2)}) collective-permute-start(f32[3,512]{1,0:T(4,128)S(1)} %multiply_add_fusion.1), channel_id=1, source_target_pairs={{1,0},{2,1},{3,2},{4,3},{5,4},{6,5},{7,6},{8,7},{9,8},{10,9},{11,1... | collective-permute-start | bytes 18440 | tf_op jit(solution)/shard_map/ppermute | solution.py:24
  228.5 19.9 %copy-start.4 = (f32[3,512]{1,0:T(4,128)}, f32[3,512]{1,0:T(4,128)S(1)}, u32[]{:S(2)}) copy-start(f32[3,512]{1,0:T(4,128)S(1)} %multiply_add_fusion) | copy-start | bytes 18436
  263.9 0.6 copy-start.5
where the time goes:
time: 265 us
  blocking collectives  184 us (69%)
  starting transfers between devices  25.1 us (9%)
  matrix products  24.2 us (9%)
  local copies, waits for them, and re-layouts  12.7 us (5%)
  waiting for transfers between devices  8.73 us (3%)
  other arithmetic  5.13 us (2%)
  between operations  4.3 us (2%)
    psum x3, blocking collectives, norm_of(): return lax.psum(jnp.sum(residual * residual, axis=1), 'slab')  88.7 us
    psum x2, blocking collectives, shards(): step_len = energy / lax.psum(jnp.sum(search * matrix_image, axis=1), 'slab')  56.4 us
    all_gather x1, blocking collectives, shards(): lax.all_gather(coefficients, 'slab', axis=1, tiled=True)  19.9 us
    all_gather x1, blocking collectives, shards(): lax.all_gather(centres, 'slab', axis=1, tiled=True)  19.1 us
    ppermute x5, starting transfers between devices, padded_2(): lax.ppermute(tail, axis, [(i, (i + 1) % count) for i in range(ends)])  14 us
    dot_general x3, matrix products, shards(): jnp.dot(ext_dir, apply_kernel, precision=lax.Precision.HIGHEST, preferred...  12.2 us
    dot_general x8, matrix products, one_block(): jnp.dot(near_coef, kernel, precision=lax.Precision.HIGHEST, preferred_ele...  12 us
    ppermute x5, starting transfers between devices, padded_2(): lax.ppermute(head, axis, [((i + 1) % count, i) for i in range(ends)])  11 us
  transfers between devices with their start and end apart: 10, of which 3 were waited for; matrix products, arithmetic and copies ran while one was open for 3% of the time, Pallas kernels for 0%

commit v1 on v0

v1 whole, which is shorter than its diff:
```python
import functools

import jax
import jax.numpy as jnp
from jax import lax
from jax.experimental import pallas as pl
from jax.experimental.pallas import tpu as pltpu
from jax.sharding import Mesh
from jax.sharding import PartitionSpec as P

FLUX_STEP = 0.2
SUPPORT = 0.15
DIAG_SHIFT = 0.5
CENTRE_SHIFT = DIAG_SHIFT + 1.0
TINY = 1e-30
F32 = jnp.float32
BF16 = jnp.bfloat16
SLAB = ("chip", "core")
VMEM = pl.BlockSpec(memory_space=pltpu.VMEM)
SMEM = pl.BlockSpec(memory_space=pltpu.SMEM)
ANY = pl.BlockSpec(memory_space=pl.ANY)


def halves(values):
    high = values.astype(BF16)
    return high, (values - high.astype(F32)).astype(BF16)


def wendland(squared):
    scaled = squared * lax.rsqrt(jnp.maximum(squared, TINY))
    inside = jnp.maximum(1.0 - scaled, 0.0)
    square_in = inside * inside
    return square_in * square_in * (4.0 * scaled + 1.0)


def distances(columns, rows, width):
    total = None
    for axis in range(3):
        diff = columns[:, axis : axis + 1] - rows[axis : axis + 1, :]
        total = diff * diff if total is None else total + diff * diff
    return total


def doubled(values):
    high, low = halves(values)
    return jnp.concatenate([high, low], axis=0)


def edge_kernel(core_ref, q_ref, w_ref, a_ref, b_ref, sems):
    count = q_ref.shape[0]
    last = q_ref.shape[1] - 1

    def move(row_a, row_b):
        copies = [
            pltpu.make_async_copy(q_ref.at[:, row_a], a_ref.at[pl.ds(0, count)], sems.at[0]),
            pltpu.make_async_copy(q_ref.at[:, row_b], b_ref.at[pl.ds(0, count)], sems.at[1]),
            pltpu.make_async_copy(w_ref.at[pl.ds(0, 1), row_a], a_ref.at[pl.ds(count, 1)], sems.at[2]),
            pltpu.make_async_copy(w_ref.at[pl.ds(0, 1), row_b], b_ref.at[pl.ds(count, 1)], sems.at[3]),
        ]
        for copy in copies:
            copy.start()
        for copy in copies:
            copy.wait()

    @pl.when(core_ref[1] == 0)
    def _():
        move(last, 0)

    @pl.when(core_ref[1] != 0)
    def _():
        move(0, last)


def edge_rows(place, flow_state, flow_speed):
    count, _, plane = flow_state.shape
    rows = jax.ShapeDtypeStruct((count + 1, plane), F32)
    return pl.pallas_call(
        edge_kernel,
        out_shape=(rows, rows),
        in_specs=[SMEM, ANY, ANY],
        out_specs=(VMEM, VMEM),
        scratch_shapes=[pltpu.SemaphoreType.DMA((4,))],
        name="edge_rows",
    )(place, flow_state, flow_speed)


def flux_kernel(
    place_ref, q_ref, w_ref, a_ref, b_ref, cell_ref, base_ref, normal_ref, centre_ref, new_ref, out_ref
):
    count, rows, plane = q_ref.shape
    width = 512
    even = place_ref[1] == 0
    pressure = 4
    rate = 0.5 * FLUX_STEP

    def chunk(step, _):
        here = pl.multiple_of(step * width, 128)
        left = pl.multiple_of(lax.rem(here + plane - 128, plane), 128)
        right = pl.multiple_of(lax.rem(here + width, plane), 128)
        below = jnp.where(even, b_ref[:, pl.ds(here, width)], a_ref[:, pl.ds(here, width)])
        above = jnp.where(even, a_ref[:, pl.ds(here, width)], b_ref[:, pl.ds(here, width)])
        row = lax.broadcasted_iota(jnp.int32, (rows, width), 0)

        def axial(values, index):
            down = jnp.where(row == 0, below[index : index + 1], pltpu.roll(values, 1, 0))
            up = jnp.where(row == rows - 1, above[index : index + 1], pltpu.roll(values, rows - 1, 0))
            return down, up

        def cyclic(ref, index):
            values = ref[index, :, pl.ds(here, width)]
            wide = jnp.concatenate(
                [ref[index, :, pl.ds(left, 128)], values, ref[index, :, pl.ds(right, 128)]], axis=1
            )
            before = pltpu.roll(wide, 1, 1)[:, 128 : 128 + width]
            after = pltpu.roll(wide, width + 255, 1)[:, 128 : 128 + width]
            return values, before, after

        w = w_ref[0, :, pl.ds(here, width)]
        w_down, w_up = axial(w, count)
        face_low = rate * (w_down + w)
        face_high = rate * (w + w_up)
        speed, speed_before, speed_after = cyclic(w_ref, 1)
        face_left = rate * (speed_before + speed)
        face_right = rate * (speed + speed_after)
        low_in = jnp.maximum(face_low, 0.0)
        high_out = jnp.minimum(face_high, 0.0)
        left_in = jnp.maximum(face_left, 0.0)
        right_out = jnp.minimum(face_right, 0.0)
        keep = 1.0 - (
            (jnp.maximum(face_high, 0.0) - jnp.minimum(face_low, 0.0))
            + (jnp.maximum(face_right, 0.0) - jnp.minimum(face_left, 0.0))
        )
        for index in range(count):
            values, before, after = cyclic(q_ref, index)
            down, up = axial(values, index)
            new_ref[index, :, pl.ds(here, width)] = (
                keep * values + low_in * down - high_out * up + left_in * before - right_out * after
            )
        return 0

    lax.fori_loop(0, plane // width, chunk, 0)

    cells = cell_ref[...]
    lanes = plane // 128
    cell_row = cells // plane
    column = cells - cell_row * plane
    group = column // 128
    lane = column - group * 128
    stacked = jnp.concatenate(
        [new_ref[pressure, :, index * 128 : index * 128 + 128] for index in range(lanes)], axis=0
    )
    place = group * rows + cell_row
    centres = cells.shape[1]
    chosen = (lax.broadcasted_iota(jnp.int32, (rows * lanes, centres), 0) == place).astype(F32)
    picked = lax.dot_general(
        stacked,
        chosen,
        (((0,), (0,)), ((), ())),
        precision=lax.Precision.HIGHEST,
        preferred_element_type=F32,
    )
    load = jnp.sum(
        jnp.where(lax.broadcasted_iota(jnp.int32, (128, centres), 0) == lane, picked, 0.0), axis=0, keepdims=True
    )
    out_ref[...] = jnp.concatenate(
        [
            base_ref[...] + normal_ref[...] * load,
            centre_ref[...] * (1.0 / SUPPORT),
            jnp.zeros((2, centres), F32),
        ],
        axis=0,
    )


def flux_and_right_side(place, flow_state, flow_speed, from_a, from_b, wall_cell, base_shift, normals, centres):
    return pl.pallas_call(
        flux_kernel,
        out_shape=(
            jax.ShapeDtypeStruct(flow_state.shape, F32),
            jax.ShapeDtypeStruct((8, centres.shape[1]), F32),
        ),
        in_specs=[SMEM] + [VMEM] * 8,
        out_specs=(VMEM, VMEM),
        name="flux",
    )(place, flow_state, flow_speed, from_a, from_b, wall_cell.reshape(1, -1), base_shift, normals, centres)


def block_of(mine_ref, other_ref, block, core):
    chip = lax.div(block, 2)
    own = lax.rem(block, 2) == core
    return jnp.where(own, mine_ref[chip], other_ref[chip])


def apply_table(values, table, transposed):
    size = table.shape[1]
    lhs = doubled(values)
    if transposed:
        both = lax.dot_general(lhs, table, (((1,), (1,)), ((), ())), preferred_element_type=F32)
        both = both[:, :size] + both[:, size:]
    else:
        both = jnp.dot(jnp.concatenate([lhs, lhs], axis=1), table, preferred_element_type=F32)
    return both[:8] + both[8:]


def powers_kernel(count, place_ref, mine_ref, other_ref, out_ref, blocks, columns, tables):
    size = mine_ref.shape[2]
    chip, core = place_ref[0], place_ref[1]
    me = chip * 2 + core
    rows = 64
    value_row = lax.broadcasted_iota(jnp.int32, (8, size), 0) < 3

    live = []
    for slot in range(6):
        block = me + slot - 2
        valid = jnp.logical_and(block >= 0, block < count)
        live.append(valid)
        data = block_of(mine_ref, other_ref, jnp.clip(block, 0, count - 1), core)
        blocks[slot] = data
        columns[slot] = data.T

    def build(index, source, target, diagonal):
        def part(step, _):
            start = pl.multiple_of(step * rows, rows)
            table = wendland(
                distances(columns[source, pl.ds(start, rows), 3:6], blocks[target, 3:6], size)
            )
            if diagonal:
                same = lax.broadcasted_iota(jnp.int32, (rows, size), 0) + start == lax.broadcasted_iota(
                    jnp.int32, (rows, size), 1
                )
                table = jnp.where(same, 0.0, table)
            high, low = halves(table)
            tables[index, pl.ds(start, rows)] = high
            tables[index, pl.ds(pl.multiple_of(start + size, rows), rows)] = low
            return 0

        lax.fori_loop(0, size // rows, part, 0)

    def diagonal(step, _):
        build(step, step + 1, step + 1, True)
        return 0

    def pair(step, _):
        build(step + 4, step, step + 1, False)
        return 0

    lax.fori_loop(0, 4, diagonal, 0)
    lax.fori_loop(0, 5, pair, 0)

    def power(values, slots):
        result = {}
        for slot in slots:
            total = apply_table(values[slot], tables[slot - 1], False)
            total = total + apply_table(values[slot - 1], tables[slot + 3], False)
            total = total + apply_table(values[slot + 1], tables[slot + 4], True)
            result[slot] = jnp.where(live[slot], total, 0.0)
        return result

    zeroth = {
        slot: jnp.where(jnp.logical_and(value_row, live[slot]), blocks[slot], 0.0) for slot in range(6)
    }
    first = power(zeroth, range(1, 5))
    second = power(first, range(2, 4))
    own = apply_table(second[2], tables[1], False)
    beside = apply_table(second[3], tables[6], True)

    def inner(left, right):
        return jnp.sum(left * right, axis=1, keepdims=True)

    moments = [
        inner(zeroth[2], zeroth[2]),
        inner(zeroth[2], first[2]),
        inner(first[2], first[2]),
        inner(first[2], second[2]),
        inner(second[2], second[2]),
        inner(second[2], own + 2.0 * beside),
    ]
    lane = lax.broadcasted_iota(jnp.int32, (8, 128), 1)
    packed = jnp.zeros((8, 128), F32)
    for index, moment in enumerate(moments):
        packed = jnp.where(lane == index, moment, packed)
    out_ref[:, :size] = jnp.concatenate([first[2][:3], second[2][:3], jnp.zeros((2, size), F32)], axis=0)
    out_ref[:, size:] = packed


def powers(place, mine, other, count):
    size = mine.shape[2]
    return pl.pallas_call(
        functools.partial(powers_kernel, count),
        out_shape=jax.ShapeDtypeStruct((8, size + 128), F32),
        in_specs=[SMEM, VMEM, VMEM],
        out_specs=VMEM,
        scratch_shapes=[
            pltpu.VMEM((6, 8, size), F32),
            pltpu.VMEM((6, size, 8), F32),
            pltpu.VMEM((9, 2 * size, size), BF16),
        ],
        name="powers",
    )(place, mine, other)


def ratio(top, bottom):
    safe = bottom > 0.0
    return jnp.where(safe, top / jnp.where(safe, bottom, 1.0), 0.0)


def weights_of(moments):
    def inner(left, right):
        total = None
        for i, a in enumerate(left):
            for j, c in enumerate(right):
                term = a * c * moments[i + j]
                total = term if total is None else total + term
        return total

    one = jnp.ones_like(moments[0])
    residual, search = [one], [one]
    coefficients = [0.0 * one] * 3
    energy = moments[0]
    for step in range(3):
        image = [CENTRE_SHIFT * value for value in search] + [0.0 * one]
        for index, value in enumerate(search):
            image[index + 1] = image[index + 1] + value
        length = ratio(energy, inner(search, image))
        for index, value in enumerate(search):
            coefficients[index] = coefficients[index] + length * value
        if step == 2:
            break
        longer = residual + [0.0 * one]
        residual = [value - length * other for value, other in zip(longer, image)]
        fresh = jnp.maximum(inner(residual, residual), 0.0)
        scale = ratio(fresh, energy)
        search = [
            value + scale * (search[index] if index < len(search) else 0.0)
            for index, value in enumerate(residual)
        ]
        energy = fresh
    return coefficients


def near_kernel(
    place_ref, tile_ref, count_ref, mine_ref, other_ref, mine_power, other_power, nodes_ref, coef_ref, shift_ref, columns, tables
):
    size = mine_ref.shape[2]
    slots = nodes_ref.shape[1]
    chips = mine_ref.shape[0]
    chip, core = place_ref[0], place_ref[1]
    me = chip * 2 + core
    listed = tile_ref.shape[1]
    rows = 64
    width = min(512, slots)

    summed = mine_power[0, :, size:] + other_power[0, :, size:]
    for index in range(1, chips):
        summed = summed + (mine_power[index, :, size:] + other_power[index, :, size:])
    moments = [summed[:, index : index + 1] for index in range(6)]
    weights = weights_of(moments)

    def coefficients_of(block):
        data = block_of(mine_ref, other_ref, block, core)
        power = block_of(mine_power, other_power, block, core)[:, :size]
        values = weights[0] * data + weights[1] * power + weights[2] * pltpu.roll(power, 5, 0)
        keep = lax.broadcasted_iota(jnp.int32, (8, size), 0) < 3
        return data, jnp.where(keep, values, 0.0)

    coef_ref[...] = coefficients_of(me)[1][:3]
    lhs = []
    for index in range(listed):
        data, values = coefficients_of(tile_ref[me, index])
        columns[index] = data.T
        both = doubled(values)
        lhs.append(jnp.concatenate([both, both], axis=1))

    live = count_ref[me]
    for tile in range(slots // width):
        points = nodes_ref[:, tile * width : (tile + 1) * width] * (1.0 / SUPPORT)
        total = jnp.zeros((16, width), F32)
        for index in range(listed):

            def part(step, _, index=index, points=points):
                start = pl.multiple_of(step * rows, rows)
                table = wendland(distances(columns[index, pl.ds(start, rows), 3:6], points, width))
                high, low = halves(table)
                tables[index % 2, pl.ds(start, rows)] = high
                tables[index % 2, pl.ds(pl.multiple_of(start + size, rows), rows)] = low
                return 0

            lax.fori_loop(0, size // rows, part, 0)
            total = total + jnp.dot(lhs[index], tables[index % 2], preferred_element_type=F32)
        slot = lax.broadcasted_iota(jnp.int32, (3, width), 1) + tile * width
        shift_ref[:, tile * width : (tile + 1) * width] = jnp.where(slot < live, total[:3] + total[8:11], 0.0)


def near_body(place, tile_blocks, near_count, mine, other, mine_power, other_power, near_nodes):
    size = mine.shape[2]
    width = min(512, near_nodes.shape[1])
    return pl.pallas_call(
        near_kernel,
        out_shape=(
            jax.ShapeDtypeStruct((3, size), F32),
            jax.ShapeDtypeStruct(near_nodes.shape, F32),
        ),
        in_specs=[SMEM, SMEM, SMEM] + [VMEM] * 5,
        out_specs=(VMEM, VMEM),
        scratch_shapes=[
            pltpu.VMEM((tile_blocks.shape[1], size, 8), F32),
            pltpu.VMEM((2, 2 * size, width), BF16),
        ],
        name="near_body",
    )(place, tile_blocks, near_count, mine, other, mine_power, other_power, near_nodes)


def gathered(values, count, partner):
    chips = count // 2
    mine = lax.all_to_all(jnp.broadcast_to(values[None], (chips,) + values.shape), "chip", 0, 0)
    return mine, lax.ppermute(mine, SLAB, partner)


def shards(
    count,
    flow_state,
    flow_speed,
    wall_cell,
    base_shift,
    normals,
    centres,
    tile_blocks,
    near_count,
    near_nodes,
):
    place = jnp.stack([lax.axis_index("chip"), lax.axis_index("core")]).astype(jnp.int32)
    partner = [(i, i ^ 1) for i in range(count)]
    across = [(i, i + 1) for i in range(1, count - 1, 2)]
    across = across + [(j, i) for i, j in across]
    send_a, send_b = edge_rows(place, flow_state, flow_speed)
    from_a = lax.ppermute(send_a, SLAB, partner)
    from_b = lax.ppermute(send_b, SLAB, across)
    new_flow, packed = flux_and_right_side(
        place, flow_state, flow_speed, from_a, from_b, wall_cell, base_shift, normals, centres
    )
    mine, other = gathered(packed, count, partner)
    mine_power, other_power = gathered(powers(place, mine, other, count), count, partner)
    coefficients, node_shift = near_body(
        place, tile_blocks, near_count, mine, other, mine_power, other_power, near_nodes
    )
    return new_flow, coefficients, node_shift


def solution(mesh):
    groups, count = mesh.shape["groups"], mesh.shape["slab"]
    split = Mesh(mesh.devices.reshape(groups, count // 2, 2), ("groups",) + SLAB)
    in_specs = (
        P("groups", SLAB, None),
        P("groups", SLAB, None),
        P(("groups",) + SLAB),
        P("groups", SLAB),
        P("groups", SLAB),
        P("groups", SLAB),
        P("groups", None),
        P("groups"),
        P("groups", SLAB),
    )
    out_specs = (P("groups", SLAB, None), P("groups", SLAB), P("groups", SLAB))
    return jax.shard_map(
        functools.partial(shards, count), mesh=split, in_specs=in_specs, out_specs=out_specs, check_vma=False
    )
```

time: 265 us -> 83.8 us (0.32)
  blocking collectives: 184 us -> 21 us
  Pallas kernels: 0 us -> 40.9 us
  matrix products: 24.2 us -> 0 us
  starting transfers between devices: 25.1 us -> 8 us
  local copies, waits for them, and re-layouts: 12.7 us -> 4.15 us
  other arithmetic: 5.13 us -> 0.65 us
  between operations: 4.3 us -> 0.69 us
    psum x5 -> x0, blocking collectives: 145 us -> none  [the longest x3 88.7 us: norm_of(): return lax.psum(jnp.sum(residual * residual, axis=1), 'slab')]
    pallas_call x0 -> x4, Pallas kernels: none -> 40.9 us  [the longest x1 18.5 us: powers(): pl.pallas_call(functools.partial(powers_kernel, count), out_shape=jax.Sha...]
    all_gather x2 -> x0, blocking collectives: 39 us -> none  [the longest x1 19.9 us: shards(): lax.all_gather(coefficients, 'slab', axis=1, tiled=True)]
    dot_general x11 -> x0, matrix products: 24.2 us -> none  [the longest x3 12.2 us: shards(): jnp.dot(ext_dir, apply_kernel, precision=lax.Precision.HIGHEST, preferred...]
    all_to_all x0 -> x2, blocking collectives: none -> 21 us  [gathered(): lax.all_to_all(jnp.broadcast_to(values[None], (chips,) + values.shape), '...]
    ppermute x10 -> x4, starting transfers between devices: 25.1 us -> 8 us  [the longest x1 4.51 us: shards(): from_b = lax.ppermute(send_b, SLAB, across)]
    slice x15 -> x0, local copies, waits for them, and re-layouts: 4.61 us -> none  [the longest x8 1.89 us: kernel_table(): diff_a = sources[0][:, None] - targets[0][None, :]]
    gather x1 -> x0, local copies, waits for them, and re-layouts: 3.14 us -> none  [shards(): wall_load = jnp.take(pressure, wall_cell)]
  transfers between devices with their start and end apart: 10 -> 4, of which waited for: 3 -> 3; matrix products, arithmetic and copies ran while one was open for 3% -> 1% of each run, Pallas kernels for 0% -> 0%
where the time goes in v1:
time: 83.8 us; the launch traced here: 83.1 us
  Pallas kernels  40.9 us (49%)
  blocking collectives  21 us (25%)
  starting transfers between devices  8 us (10%)
  waiting for transfers between devices  7.74 us (9%)
  local copies, waits for them, and re-layouts  4.15 us (5%)
    all_to_all x2, blocking collectives, gathered(): lax.all_to_all(jnp.broadcast_to(values[None], (chips,) + values.shape), '...  21 us
    pallas_call x1, Pallas kernels, powers(): pl.pallas_call(functools.partial(powers_kernel, count), out_shape=jax.Sha...  18.5 us
    pallas_call x1, Pallas kernels, near_body(): pl.pallas_call(near_kernel, out_shape=(jax.ShapeDtypeStruct((3, size), F3...  14.6 us
    ppermute x1, waiting for transfers between devices, shards(): from_b = lax.ppermute(send_b, SLAB, across)  6.4 us
    pallas_call x1, Pallas kernels, flux_and_right_side(): pl.pallas_call(flux_kernel, out_shape=(jax.ShapeDtypeStruct(flow_state.sh...  5.22 us
    ppermute x1, starting transfers between devices, shards(): from_b = lax.ppermute(send_b, SLAB, across)  4.51 us
    ppermute x2, starting transfers between devices, gathered(): return (mine, lax.ppermute(mine, SLAB, partner))  3.42 us
    unnamed x15, local copies, waits for them, and re-layouts  2.68 us
  transfers between devices with their start and end apart: 4, of which 3 were waited for; matrix products, arithmetic and copies ran while one was open for 1% of the time, Pallas kernels for 0%

profile of v1, /device:TPU:1, one launch (start us, length us, event | category | flops | bytes accessed | tf_op | source)
XLA Modules:
  0.0 83.1 jit_solution(2150366257327060123)
XLA Ops:
  0.6 0.6 pad_add_fusion.core_ref.place_ref
  1.3 2.5 %edge_rows.1 = (f32[6,8192]{1,0:T(8,128)}, f32[6,8192]{1,0:T(8,128)}) custom-call(s32[2]{0:T(128)} %pad_add_fusion.core_ref.place_ref, f32[5,8,8192]{2,1,0:T(8,128)} %q_ref.3, f32[2,8,8192]{2,1,0:T(8,128)} %w_ref.3), custom_call_target="tpu_custom_call" | custom-call | tf_op jit(solution)/shard_map/edge_rows/pallas_call | solution.py:77
  3.8 0.1 collective-permute-start
  3.9 4.5 %collective-permute-start.1 = (f32[6,8192]{1,0:T(8,128)}, f32[6,8192]{1,0:T(8,128)S(1)}, u32[]{:S(2)}, u32[]{:S(2)}) collective-permute-start(f32[6,8192]{1,0:T(8,128)} %get-tuple-element.10), channel_id=1, source_target_pairs={{1,2},{3,4},{5,6},{7,8},{9,10},{11,12},{13,14},{2,1},{4,3},{6,5},{... | collective-permute-start | bytes 589832 | tf_op jit(solution)/shard_map/ppermute | solution.py:437
  8.4 0.0 collective-permute-done.a_ref
  8.4 0.0 copy-start.3
  8.4 6.4 %collective-permute-done.1.b_ref = f32[6,8192]{1,0:T(8,128)S(1)} collective-permute-done((f32[6,8192]{1,0:T(8,128)}, f32[6,8192]{1,0:T(8,128)S(1)}, u32[]{:S(2)}, u32[]{:S(2)}) %collective-permute-start.1) | collective-permute-done | bytes 196640 | tf_op jit(solution)/shard_map/ppermute | solution.py:437
  14.8 0.0 copy-start.4
  14.8 0.0 copy-done.3
  14.8 0.7 copy-done.4
  15.5 0.0 copy-start.6
  15.5 5.2 %flux.1 = (f32[5,8,8192]{2,1,0:T(8,128)}, f32[8,512]{1,0:T(8,128)}) custom-call(s32[2]{0:T(128)} %pad_add_fusion.core_ref.place_ref, f32[5,8,8192]{2,1,0:T(8,128)} %q_ref.3, f32[2,8,8192]{2,1,0:T(8,128)} %w_ref.3, f32[6,8192]{1,0:T(8,128)} %copy-done.3, f32[6,8192]{1,0:T(8,128)} %copy-done.4, s32[1,512]{1,0:T(1,128)} %bitcast.3, f32[3,512]{1,0:T(4,128)} %base_ref.1, ...), custom_call_target="tpu_custom_call" | custom-call | tf_op jit(solution)/shard_map/flux/pallas_call | solution.py:176
  20.7 0.7 broadcast_in_dim.4
  21.5 12.0 %all_to_all.10.mine_ref = f32[8,8,512]{2,1,0:T(8,128)S(1)} all-to-all(f32[8,8,512]{2,1,0:T(8,128)S(1)} %broadcast_in_dim.4), channel_id=1, replica_groups=mesh['groups'=2,'chip'=8,'core'=2] {'chip'}, dimensions={0} | all-to-all | bytes 262144 | tf_op jit(solution)/shard_map/all_to_all | solution.py:415
  33.4 0.0 copy-start
  33.4 1.6 %collective-permute-start.2 = (f32[8,8,512]{2,1,0:T(8,128)S(1)}, f32[8,8,512]{2,1,0:T(8,128)S(1)}, u32[]{:S(2)}, u32[]{:S(2)}) collective-permute-start(f32[8,8,512]{2,1,0:T(8,128)S(1)} %all_to_all.10.mine_ref), channel_id=1, source_target_pairs={{0,1},{1,0},{2,3},{3,2},{4,5},{5,4},{6,7},{7,6},{8,9},{9,8},{10,11... | collective-permute-start | bytes 393224 | tf_op jit(solution)/shard_map/ppermute | solution.py:416
  35.0 1.0 %collective-permute-done.2.other_ref = f32[8,8,512]{2,1,0:T(8,128)S(1)} collective-permute-done((f32[8,8,512]{2,1,0:T(8,128)S(1)}, f32[8,8,512]{2,1,0:T(8,128)S(1)}, u32[]{:S(2)}, u32[]{:S(2)}) %collective-permute-start.2) | collective-permute-done | bytes 131104 | tf_op jit(solution)/shard_map/ppermute | solution.py:416
  36.0 0.0 copy-done
  36.0 0.0 copy-start.2
  36.0 0.6 copy-done.2
  36.7 18.5 %powers.1 = f32[8,640]{1,0:T(8,128)} custom-call(s32[2]{0:T(128)} %pad_add_fusion.core_ref.place_ref, f32[8,8,512]{2,1,0:T(8,128)} %copy-done, f32[8,8,512]{2,1,0:T(8,128)} %copy-done.2), custom_call_target="tpu_custom_call" | custom-call | tf_op jit(solution)/shard_map/powers/pallas_call | solution.py:288
  55.2 0.7 broadcast_in_dim.5
  55.9 9.0 %all_to_all.11.mine_power = f32[8,8,640]{2,1,0:T(8,128)S(1)} all-to-all(f32[8,8,640]{2,1,0:T(8,128)S(1)} %broadcast_in_dim.5), channel_id=1, replica_groups=mesh['groups'=2,'chip'=8,'core'=2] {'chip'}, dimensions={0} | all-to-all | bytes 327680 | tf_op jit(solution)/shard_map/all_to_all | solution.py:415
  64.9 0.0 copy-start.1
  64.9 1.8 %collective-permute-start.3 = (f32[8,8,640]{2,1,0:T(8,128)S(1)}, f32[8,8,640]{2,1,0:T(8,128)S(1)}, u32[]{:S(2)}, u32[]{:S(2)}) collective-permute-start(f32[8,8,640]{2,1,0:T(8,128)S(1)} %all_to_all.11.mine_power), channel_id=1, source_target_pairs={{0,1},{1,0},{2,3},{3,2},{4,5},{5,4},{6,7},{7,6},{8,9},{9,8},{10,11... | collective-permute-start | bytes 491528 | tf_op jit(solution)/shard_map/ppermute | solution.py:416
  66.8 0.0 copy-done.6
  66.8 0.7 copy.12.tile_ref
  67.4 0.3 collective-permute-done.3.other_power
  67.8 0.0 copy-done.1
  67.8 0.0 copy-start.5
  67.8 0.6 copy-done.5
  68.5 14.6 %near_body.1 = (f32[3,512]{1,0:T(4,128)}, f32[3,1024]{1,0:T(4,128)}) custom-call(s32[2]{0:T(128)} %pad_add_fusion.core_ref.place_ref, s32[16,4]{1,0:T(8,128)} %copy.12.tile_ref, s32[16]{0:T(128)} %count_ref.1, f32[8,8,512]{2,1,0:T(8,128)} %copy-done, f32[8,8,512]{2,1,0:T(8,128)} %copy-done.2, f32[8,8,640]{2,1,0:T(8,128)} %copy-done.1, ...), custom_call_target="tpu_custom_call" | custom-call | tf_op jit(solution)/shard_map/near_body/pallas_call | solution.py:397
Async XLA Ops:
  3.8 4.6 %collective-permute-start = (f32[6,8192]{1,0:T(8,128)}, f32[6,8192]{1,0:T(8,128)S(1)}, u32[]{:S(2)}, u32[]{:S(2)}) collective-permute-start(f32[6,8192]{1,0:T(8,128)} %get-tuple-element.9), channel_id=1, source_target_pairs={{0,1},{1,0},{2,3},{3,2},{4,5},{5,4},{6,7},{7,6},{8,9},{9,8},{10,11... | collective-permute-start | bytes 589832 | tf_op jit(solution)/shard_map/ppermute | solution.py:436
  3.9 10.9 %collective-permute-start.1 = (f32[6,8192]{1,0:T(8,128)}, f32[6,8192]{1,0:T(8,128)S(1)}, u32[]{:S(2)}, u32[]{:S(2)}) collective-permute-start(f32[6,8192]{1,0:T(8,128)} %get-tuple-element.10), channel_id=1, source_target_pairs={{1,2},{3,4},{5,6},{7,8},{9,10},{11,12},{13,14},{2,1},{4,3},{6,5},{... | collective-permute-start | bytes 589832 | tf_op jit(solution)/shard_map/ppermute | solution.py:437
  8.4 6.4 %copy-start.3 = (f32[6,8192]{1,0:T(8,128)}, f32[6,8192]{1,0:T(8,128)S(1)}, u32[]{:S(2)}) copy-start(f32[6,8192]{1,0:T(8,128)S(1)} %collective-permute-done.a_ref) | copy-start | bytes 589828
  14.8 0.7 copy-start.4
  15.5 51.3 %copy-start.6 = (s32[16,4]{0,1:T(4,128)S(1)}, s32[16,4]{0,1:T(4,128)}, u32[]{:S(2)}) copy-start(s32[16,4]{0,1:T(4,128)} %param.15) | copy-start | bytes 772
  33.4 2.6 %copy-start = (f32[8,8,512]{2,1,0:T(8,128)}, f32[8,8,512]{2,1,0:T(8,128)S(1)}, u32[]{:S(2)}) copy-start(f32[8,8,512]{2,1,0:T(8,128)S(1)} %all_to_all.10.mine_ref) | copy-start | bytes 393220
  33.4 2.6 %collective-permute-start.2 = (f32[8,8,512]{2,1,0:T(8,128)S(1)}, f32[8,8,512]{2,1,0:T(8,128)S(1)}, u32[]{:S(2)}, u32[]{:S(2)}) collective-permute-start(f32[8,8,512]{2,1,0:T(8,128)S(1)} %all_to_all.10.mine_ref), channel_id=1, source_target_pairs={{0,1},{1,0},{2,3},{3,2},{4,5},{5,4},{6,7},{7,6},{8,9},{9,8},{10,11... | collective-permute-start | bytes 393224 | tf_op jit(solution)/shard_map/ppermute | solution.py:416
  36.0 0.6 copy-start.2
  64.9 2.9 %copy-start.1 = (f32[8,8,640]{2,1,0:T(8,128)}, f32[8,8,640]{2,1,0:T(8,128)S(1)}, u32[]{:S(2)}) copy-start(f32[8,8,640]{2,1,0:T(8,128)S(1)} %all_to_all.11.mine_power) | copy-start | bytes 491524
  64.9 2.9 %collective-permute-start.3 = (f32[8,8,640]{2,1,0:T(8,128)S(1)}, f32[8,8,640]{2,1,0:T(8,128)S(1)}, u32[]{:S(2)}, u32[]{:S(2)}) collective-permute-start(f32[8,8,640]{2,1,0:T(8,128)S(1)} %all_to_all.11.mine_power), channel_id=1, source_target_pairs={{0,1},{1,0},{2,3},{3,2},{4,5},{5,4},{6,7},{7,6},{8,9},{9,8},{10,11... | collective-permute-start | bytes 491528 | tf_op jit(solution)/shard_map/ppermute | solution.py:416
  67.8 0.7 copy-start.5

commit v2 on v1

v2 whole, which is shorter than its diff:
```python
import functools

import jax
import jax.numpy as jnp
from jax import lax
from jax.experimental import pallas as pl
from jax.experimental.pallas import tpu as pltpu
from jax.sharding import Mesh
from jax.sharding import PartitionSpec as P

FLUX_STEP = 0.2
SUPPORT = 0.15
DIAG_SHIFT = 0.5
CENTRE_SHIFT = DIAG_SHIFT + 1.0
TINY = 1e-12
DEPTH = 0.4
CHUNK = 128
MARGIN = 1e-3
BIG_LIMIT = 48 * 1024 * 1024
SMALL_LIMIT = 16 * 1024 * 1024
F32 = jnp.float32
BF16 = jnp.bfloat16
SLAB = ("chip", "core")
VMEM = pl.BlockSpec(memory_space=pltpu.VMEM)
SMEM = pl.BlockSpec(memory_space=pltpu.SMEM)
ANY = pl.BlockSpec(memory_space=pl.ANY)


def parts(values):
    first = values.astype(BF16).astype(F32)
    rest = values - first
    second = rest.astype(BF16).astype(F32)
    return first, second, rest - second


def doubled(values):
    high = values.astype(BF16)
    return jnp.concatenate([high, (values - high.astype(F32)).astype(BF16)], axis=0)


def sides(points):
    count = points.shape[1]
    squares = jnp.sum(points * points, axis=0, keepdims=True)
    one = jnp.ones((1, count), F32)
    zero = jnp.zeros((3, count), F32)
    a, b, c = parts(jnp.concatenate([points, squares, one, zero], axis=0))
    d, e, f = parts(jnp.concatenate([-2.0 * points, one, squares, zero], axis=0))
    return jnp.concatenate([a, a, b, a, c, b], axis=0), jnp.concatenate([d, e, d, f, d, e], axis=0)


def quarter_kernel(sources, targets):
    squared = jnp.maximum(jnp.dot(sources, targets, preferred_element_type=F32), TINY)
    inside = jnp.maximum(1.0 - squared * lax.rsqrt(squared), 0.0)
    square_in = inside * inside
    return square_in * square_in * (1.25 - inside)


def local_points(raw, origin):
    x = (raw[0:2] - 0.5) * (1.0 / SUPPORT)
    return jnp.concatenate([x, (raw[2:3] - origin) * (1.0 / SUPPORT)], axis=0)


def rank_of(values):
    count = values.shape[1]
    column = jnp.broadcast_to(values, (8, count)).T[:, 0:1]
    result = []
    for tile in range(count // CHUNK):
        mine = values[:, tile * CHUNK : (tile + 1) * CHUNK]
        total = jnp.zeros((8, CHUNK), F32)
        for chunk in range(count // CHUNK):
            other = column[chunk * CHUNK : (chunk + 1) * CHUNK]
            if chunk < tile:
                before = other <= mine
            elif chunk > tile:
                before = other < mine
            else:
                above = lax.broadcasted_iota(jnp.int32, (CHUNK, CHUNK), 0) < lax.broadcasted_iota(
                    jnp.int32, (CHUNK, CHUNK), 1
                )
                before = jnp.logical_or(other < mine, jnp.logical_and(other == mine, above))
            ones = jnp.where(before, 1.0, 0.0)
            for group in range(CHUNK // 8):
                total = total + ones[group * 8 : group * 8 + 8]
        result.append(jnp.sum(total, axis=0, keepdims=True))
    return jnp.concatenate(result, axis=1)


def moved(values, table, back):
    rows = values.shape[0]
    stacked = jnp.concatenate(parts(values), axis=0).astype(BF16)
    both = lax.dot_general(
        stacked, table, (((1,), (0 if back else 1,)), ((), ())), preferred_element_type=F32
    )
    return (both[:rows] + both[rows : 2 * rows]) + both[2 * rows :]


def chunk_bounds(source_z, target_z, width, low_ref, high_ref):
    chunks = source_z.shape[1] // CHUNK
    tiles = target_z.shape[1] // width

    def edges(values, size, pieces):
        rows = jnp.concatenate([values[:, i * size : (i + 1) * size] for i in range(pieces)], axis=0)
        return jnp.min(rows, axis=1, keepdims=True), jnp.max(rows, axis=1, keepdims=True)

    source_low, source_high = edges(source_z, CHUNK, chunks)
    target_low, target_high = edges(target_z, width, tiles)
    index = lax.broadcasted_iota(jnp.int32, (chunks, 1), 0).astype(F32)
    for tile in range(tiles):
        near = jnp.logical_and(
            source_high >= target_low[tile : tile + 1] - (1.0 + MARGIN),
            source_low <= target_high[tile : tile + 1] + (1.0 + MARGIN),
        )
        low_ref[tile] = jnp.min(jnp.where(near, index, float(chunks))).astype(jnp.int32)
        high_ref[tile] = jnp.max(jnp.where(near, index + 1.0, 0.0)).astype(jnp.int32)


def order_kernel(base_ref, normal_ref, centre_ref, cell_ref, nodes_ref, out_ref, centre_table, nodes_out, node_table):
    def table_of(ref, rank):
        count = rank.shape[1]
        rows = 128
        for start in range(0, count, rows):
            row = lax.broadcasted_iota(jnp.int32, (rows, count), 0).astype(F32) + float(start)
            ref[start : start + rows] = jnp.where(row == rank, 1.0, 0.0).astype(BF16)

    count = centre_ref.shape[1]
    table_of(centre_table, rank_of(centre_ref[2:3]))
    values = jnp.concatenate(
        [
            base_ref[...],
            normal_ref[...],
            centre_ref[...],
            cell_ref[...].astype(F32),
            jnp.zeros((6, count), F32),
        ],
        axis=0,
    )
    out_ref[...] = moved(values, centre_table[...], False)
    table_of(node_table, rank_of(nodes_ref[2:3]))
    nodes = jnp.concatenate([nodes_ref[...], jnp.zeros((5, nodes_ref.shape[1]), F32)], axis=0)
    nodes_out[...] = moved(nodes, node_table[...], False)


def ordered(base_shift, normals, centres, wall_cell, near_nodes):
    count, slots = centres.shape[1], near_nodes.shape[1]
    return pl.pallas_call(
        order_kernel,
        out_shape=(
            jax.ShapeDtypeStruct((16, count), F32),
            jax.ShapeDtypeStruct((count, count), BF16),
            jax.ShapeDtypeStruct((8, slots), F32),
            jax.ShapeDtypeStruct((slots, slots), BF16),
        ),
        in_specs=[VMEM] * 5,
        out_specs=(VMEM,) * 4,
        compiler_params=pltpu.CompilerParams(vmem_limit_bytes=SMALL_LIMIT),
        cost_estimate=pl.CostEstimate(flops=8_000_000, bytes_accessed=4_000_000, transcendentals=0),
        name="order",
    )(base_shift, normals, centres, wall_cell.reshape(1, -1), near_nodes)


def edge_kernel(q_ref, w_ref, a_ref, b_ref, sems):
    count = q_ref.shape[0]
    last = q_ref.shape[1] - 1
    core = lax.axis_index("core")

    def move(row_a, row_b):
        copies = [
            pltpu.make_async_copy(q_ref.at[:, row_a], a_ref.at[pl.ds(0, count)], sems.at[0]),
            pltpu.make_async_copy(q_ref.at[:, row_b], b_ref.at[pl.ds(0, count)], sems.at[1]),
            pltpu.make_async_copy(w_ref.at[pl.ds(0, 1), row_a], a_ref.at[pl.ds(count, 1)], sems.at[2]),
            pltpu.make_async_copy(w_ref.at[pl.ds(0, 1), row_b], b_ref.at[pl.ds(count, 1)], sems.at[3]),
        ]
        for copy in copies:
            copy.start()
        for copy in copies:
            copy.wait()

    @pl.when(core == 0)
    def _():
        move(last, 0)

    @pl.when(core != 0)
    def _():
        move(0, last)


def edge_rows(flow_state, flow_speed):
    count, _, plane = flow_state.shape
    rows = jax.ShapeDtypeStruct((count + 1, plane), F32)
    return pl.pallas_call(
        edge_kernel,
        out_shape=(rows, rows),
        in_specs=[ANY, ANY],
        out_specs=(VMEM, VMEM),
        scratch_shapes=[pltpu.SemaphoreType.DMA((4,))],
        compiler_params=pltpu.CompilerParams(vmem_limit_bytes=SMALL_LIMIT),
        name="edge_rows",
    )(flow_state, flow_speed)


def flux_kernel(
    q_ref, w_ref, a_ref, b_ref, sorted_ref, new_ref, out_ref
):
    count, rows, plane = q_ref.shape
    width = 512
    even = lax.axis_index("core") == 0
    pressure = 4
    rate = 0.5 * FLUX_STEP

    def chunk(step, _):
        here = pl.multiple_of(step * width, 128)
        left = pl.multiple_of(lax.rem(here + plane - 128, plane), 128)
        right = pl.multiple_of(lax.rem(here + width, plane), 128)
        below = jnp.where(even, b_ref[:, pl.ds(here, width)], a_ref[:, pl.ds(here, width)])
        above = jnp.where(even, a_ref[:, pl.ds(here, width)], b_ref[:, pl.ds(here, width)])
        row = lax.broadcasted_iota(jnp.int32, (rows, width), 0)

        def axial(values, index):
            down = jnp.where(row == 0, below[index : index + 1], pltpu.roll(values, 1, 0))
            up = jnp.where(row == rows - 1, above[index : index + 1], pltpu.roll(values, rows - 1, 0))
            return down, up

        def cyclic(ref, index):
            values = ref[index, :, pl.ds(here, width)]
            wide = jnp.concatenate(
                [ref[index, :, pl.ds(left, 128)], values, ref[index, :, pl.ds(right, 128)]], axis=1
            )
            before = pltpu.roll(wide, 1, 1)[:, 128 : 128 + width]
            after = pltpu.roll(wide, width + 255, 1)[:, 128 : 128 + width]
            return values, before, after

        w = w_ref[0, :, pl.ds(here, width)]
        w_down, w_up = axial(w, count)
        face_low = rate * (w_down + w)
        face_high = rate * (w + w_up)
        speed, speed_before, speed_after = cyclic(w_ref, 1)
        face_left = rate * (speed_before + speed)
        face_right = rate * (speed + speed_after)
        low_in = jnp.maximum(face_low, 0.0)
        high_out = jnp.minimum(face_high, 0.0)
        left_in = jnp.maximum(face_left, 0.0)
        right_out = jnp.minimum(face_right, 0.0)
        keep = 1.0 - (
            (jnp.maximum(face_high, 0.0) - jnp.minimum(face_low, 0.0))
            + (jnp.maximum(face_right, 0.0) - jnp.minimum(face_left, 0.0))
        )
        for index in range(count):
            values, before, after = cyclic(q_ref, index)
            down, up = axial(values, index)
            new_ref[index, :, pl.ds(here, width)] = (
                keep * values + low_in * down - high_out * up + left_in * before - right_out * after
            )
        return 0

    lax.fori_loop(0, plane // width, chunk, 0)

    cells = sorted_ref[9:10].astype(jnp.int32)
    lanes = plane // 128
    cell_row = cells // plane
    column = cells - cell_row * plane
    group = column // 128
    lane = column - group * 128
    stacked = jnp.concatenate(
        [new_ref[pressure, :, index * 128 : index * 128 + 128] for index in range(lanes)], axis=0
    )
    place = group * rows + cell_row
    centres = cells.shape[1]
    chosen = (lax.broadcasted_iota(jnp.int32, (rows * lanes, centres), 0) == place).astype(F32).astype(BF16)
    pieces = jnp.concatenate(parts(stacked), axis=1).astype(BF16)
    both = lax.dot_general(pieces, chosen, (((0,), (0,)), ((), ())), preferred_element_type=F32)
    picked = (both[:128] + both[128:256]) + both[256:]
    load = jnp.sum(
        jnp.where(lax.broadcasted_iota(jnp.int32, (128, centres), 0) == lane, picked, 0.0), axis=0, keepdims=True
    )
    packed = jnp.concatenate(
        [sorted_ref[0:3] + sorted_ref[3:6] * load, sorted_ref[6:9], jnp.zeros((2, centres), F32)], axis=0
    )
    for chip in range(out_ref.shape[0]):
        out_ref[chip] = packed


def flux_and_right_side(chips, flow_state, flow_speed, from_a, from_b, in_order):
    return pl.pallas_call(
        flux_kernel,
        out_shape=(
            jax.ShapeDtypeStruct(flow_state.shape, F32),
            jax.ShapeDtypeStruct((chips, 8, in_order.shape[1]), F32),
        ),
        in_specs=[VMEM] * 5,
        out_specs=(VMEM, VMEM),
        compiler_params=pltpu.CompilerParams(vmem_limit_bytes=SMALL_LIMIT),
        name="flux",
    )(flow_state, flow_speed, from_a, from_b, in_order)


def block_of(mine_ref, other_ref, block, core):
    chip = lax.div(block, 2)
    own = lax.rem(block, 2) == core
    return jnp.where(own, mine_ref[chip], other_ref[chip])


def powers_kernel(
    count, mine_ref, other_ref, out_ref, source_side, target_side, vector, tables, low_ref, high_ref
):
    size = mine_ref.shape[2]
    chip, core = lax.axis_index("chip"), lax.axis_index("core")
    me = chip * 2 + core
    slots, width, reach = 6, 256, 6
    span = reach * CHUNK
    total = slots * size
    origin = lax.div(me * 2, 5).astype(F32)
    value_row = lax.broadcasted_iota(jnp.int32, (8, size), 0) < 3

    live, zeroth, third = [], [], []
    for slot in range(slots):
        block = me + slot - 2
        valid = jnp.logical_and(block >= 0, block < count)
        live.append(valid)
        data = block_of(mine_ref, other_ref, jnp.clip(block, 0, count - 1), core)
        zeroth.append(jnp.where(jnp.logical_and(value_row, valid), data, 0.0))
        middle = (block.astype(F32) + 0.5) * DEPTH
        raw = jnp.concatenate([data[3:5], jnp.where(valid, data[5:6], middle)], axis=0)
        points = local_points(raw, origin)
        third.append(points[2:3])
        source, target = sides(points)
        source_side[slot * size : (slot + 1) * size] = source.T.astype(BF16)
        target_side[:, slot * size : (slot + 1) * size] = target.astype(BF16)
    far = (lax.broadcasted_iota(jnp.int32, (span, 48), 1) == 3).astype(F32) * 4096.0
    source_side[total:] = far.astype(BF16)
    vector[:, total:] = jnp.zeros((16, span), BF16)
    heights = jnp.concatenate(third, axis=1)
    chunk_bounds(heights, heights[:, size : 5 * size], width, low_ref, high_ref)
    tiles = 4 * size // width

    def steps_of(tile):
        return lax.div(high_ref[tile] - low_ref[tile] + (reach - 1), reach)

    def build_tile(tile, _):
        lanes = pl.ds(pl.multiple_of(tile * width + size, width), width)
        targets = target_side[:, lanes]

        def build(step, _):
            chunk = low_ref[tile] + step * reach
            rows = pl.ds(pl.multiple_of(chunk * CHUNK, CHUNK), span)
            table = quarter_kernel(source_side[rows], targets)
            high = table.astype(BF16)
            tables[tile, step, :span] = high
            tables[tile, step, span:] = (table - high.astype(F32)).astype(BF16)
            for piece in range(width // CHUNK):
                place = (tile * width + size) // CHUNK + piece - chunk

                @pl.when(jnp.logical_and(place >= 0, place < reach))
                def _(place=place, piece=piece):
                    same = lax.broadcasted_iota(jnp.int32, (CHUNK, CHUNK), 0) == lax.broadcasted_iota(
                        jnp.int32, (CHUNK, CHUNK), 1
                    )
                    for half in range(2):
                        at = pl.ds(pl.multiple_of(place * CHUNK + half * span, CHUNK), CHUNK)
                        columns = slice(piece * CHUNK, (piece + 1) * CHUNK)
                        old = tables[tile, step, at, columns].astype(F32)
                        tables[tile, step, at, columns] = jnp.where(same, 0.0, old).astype(BF16)

            return 0

        lax.fori_loop(0, steps_of(tile), build, 0)
        return 0

    lax.fori_loop(0, tiles, build_tile, 0)

    def applied(tile):
        def one(step):
            lanes = pl.ds(pl.multiple_of((low_ref[tile] + step * reach) * CHUNK, CHUNK), span)
            window = vector[:, lanes]
            return jnp.dot(
                jnp.concatenate([window, window], axis=1), tables[tile, step], preferred_element_type=F32
            )

        both = lax.fori_loop(1, steps_of(tile), lambda step, old: old + one(step), one(0))
        return 4.0 * (both[:8] + both[8:])

    def power(slot):
        first = (slot - 1) * size // width
        values = jnp.concatenate([applied(first + i) for i in range(size // width)], axis=1)
        return jnp.where(live[slot], values, 0.0)

    def hold(values, slot):
        vector[:, slot * size : (slot + 1) * size] = doubled(values)

    for slot in range(slots):
        hold(zeroth[slot], slot)
    first = {slot: power(slot) for slot in range(1, 5)}
    for slot in range(1, 5):
        hold(first[slot], slot)
    second = {slot: power(slot) for slot in range(2, 4)}
    hold(jnp.zeros((8, size), F32), 1)
    hold(second[2], 2)
    hold(2.0 * second[3], 3)
    last = power(2)

    def inner(left, right):
        return jnp.sum(left * right, axis=1, keepdims=True)

    moments = [
        inner(zeroth[2], zeroth[2]),
        inner(zeroth[2], first[2]),
        inner(first[2], first[2]),
        inner(first[2], second[2]),
        inner(second[2], second[2]),
        inner(second[2], last),
    ]
    lane = lax.broadcasted_iota(jnp.int32, (8, 128), 1)
    packed = jnp.zeros((8, 128), F32)
    for index, moment in enumerate(moments):
        packed = jnp.where(lane == index, moment, packed)
    values = jnp.concatenate([first[2][:3], second[2][:3], jnp.zeros((2, size), F32)], axis=0)
    for index in range(out_ref.shape[0]):
        out_ref[index, :, :size] = values
        out_ref[index, :, size:] = packed


def powers(mine, other, count):
    chips, _, size = mine.shape
    tiles = 4 * size // 256
    steps = (6 * size // CHUNK + 5) // 6
    return pl.pallas_call(
        functools.partial(powers_kernel, count),
        out_shape=jax.ShapeDtypeStruct((chips, 8, size + 128), F32),
        in_specs=[VMEM, VMEM],
        out_specs=VMEM,
        scratch_shapes=[
            pltpu.VMEM((6 * size + 6 * CHUNK, 48), BF16),
            pltpu.VMEM((48, 6 * size), BF16),
            pltpu.VMEM((16, 6 * size + 6 * CHUNK), BF16),
            pltpu.VMEM((tiles, steps, 12 * CHUNK, 256), BF16),
            pltpu.SMEM((tiles,), jnp.int32),
            pltpu.SMEM((tiles,), jnp.int32),
        ],
        compiler_params=pltpu.CompilerParams(vmem_limit_bytes=BIG_LIMIT),
        name="powers",
    )(mine, other)


def ratio(top, bottom):
    safe = bottom > 0.0
    return jnp.where(safe, top / jnp.where(safe, bottom, 1.0), 0.0)


def weights_of(moments):
    def inner(left, right):
        total = None
        for i, a in enumerate(left):
            for j, c in enumerate(right):
                term = a * c * moments[i + j]
                total = term if total is None else total + term
        return total

    one = jnp.ones_like(moments[0])
    residual, search = [one], [one]
    coefficients = [0.0 * one] * 3
    energy = moments[0]
    for step in range(3):
        image = [CENTRE_SHIFT * value for value in search] + [0.0 * one]
        for index, value in enumerate(search):
            image[index + 1] = image[index + 1] + value
        length = ratio(energy, inner(search, image))
        for index, value in enumerate(search):
            coefficients[index] = coefficients[index] + length * value
        if step == 2:
            break
        longer = residual + [0.0 * one]
        residual = [value - length * other for value, other in zip(longer, image)]
        fresh = jnp.maximum(inner(residual, residual), 0.0)
        scale = ratio(fresh, energy)
        search = [
            value + scale * (search[index] if index < len(search) else 0.0)
            for index, value in enumerate(residual)
        ]
        energy = fresh
    return coefficients


def near_kernel(
    tile_ref, count_ref, mine_ref, other_ref, mine_power, other_power, nodes_ref, centre_hbm, node_hbm,
    coef_ref, shift_ref,
    source_side, target_side, vector, result, centre_table, node_table, sems, low_ref, high_ref,
):
    size = mine_ref.shape[2]
    slots = nodes_ref.shape[1]
    chips = mine_ref.shape[0]
    core = lax.axis_index("core")
    me = lax.axis_index("chip") * 2 + core
    listed = tile_ref.shape[0] // count_ref.shape[0]
    width, reach = 256, 4
    span = reach * CHUNK
    total = listed * size
    copies = [
        pltpu.make_async_copy(centre_hbm, centre_table, sems.at[0]),
        pltpu.make_async_copy(node_hbm, node_table, sems.at[1]),
    ]
    for copy in copies:
        copy.start()

    summed = mine_power[0, :, size:] + other_power[0, :, size:]
    for index in range(1, chips):
        summed = summed + (mine_power[index, :, size:] + other_power[index, :, size:])
    weights = weights_of([summed[:, index : index + 1] for index in range(6)])

    def coefficients_of(block):
        data = block_of(mine_ref, other_ref, block, core)
        power = block_of(mine_power, other_power, block, core)[:, :size]
        values = weights[0] * data + weights[1] * power + weights[2] * pltpu.roll(power, 5, 0)
        keep = lax.broadcasted_iota(jnp.int32, (8, size), 0) < 3
        return data, jnp.where(keep, values, 0.0)

    origin = lax.div((tile_ref[me * listed] + 2) * 2, 5).astype(F32)
    third = []
    for index in range(listed):
        data, values = coefficients_of(tile_ref[me * listed + index])
        points = local_points(data[3:6], origin)
        third.append(points[2:3])
        source, _ = sides(points)
        source_side[index * size : (index + 1) * size] = source.T.astype(BF16)
        vector[:, index * size : (index + 1) * size] = doubled(values)
    far = (lax.broadcasted_iota(jnp.int32, (span, 48), 1) == 3).astype(F32) * 4096.0
    source_side[total:] = far.astype(BF16)
    vector[:, total:] = jnp.zeros((16, span), BF16)
    points = local_points(nodes_ref[0:3], origin)
    _, target = sides(points)
    target_side[...] = target.astype(BF16)
    chunk_bounds(jnp.concatenate(third, axis=1), points[2:3], width, low_ref, high_ref)

    def node_tile(tile, _):
        lanes = pl.ds(pl.multiple_of(tile * width, width), width)
        targets = target_side[:, lanes]

        def one(step, old):
            start = pl.multiple_of((low_ref[tile] + step * reach) * CHUNK, CHUNK)
            table = quarter_kernel(source_side[pl.ds(start, span)], targets)
            window = vector[:, pl.ds(start, span)]
            return old + jnp.dot(
                jnp.concatenate([window, window], axis=1), doubled(table), preferred_element_type=F32
            )

        steps = lax.div(high_ref[tile] - low_ref[tile] + (reach - 1), reach)
        both = lax.fori_loop(0, steps, one, jnp.zeros((16, width), F32))
        result[:, lanes] = 4.0 * (both[:8] + both[8:])
        return 0

    lax.fori_loop(0, slots // width, node_tile, 0)
    for copy in copies:
        copy.wait()
    coef_ref[...] = moved(coefficients_of(me)[1], centre_table[...], True)[:3]
    slot = lax.broadcasted_iota(jnp.int32, (3, slots), 1)
    shift_ref[...] = jnp.where(slot < count_ref[me], moved(result[...], node_table[...], True)[:3], 0.0)


def near_body(tile_blocks, near_count, mine, other, mine_power, other_power, nodes, centre_table, node_table):
    size = mine.shape[2]
    slots = nodes.shape[1]
    total = tile_blocks.shape[1] * size
    return pl.pallas_call(
        near_kernel,
        out_shape=(
            jax.ShapeDtypeStruct((3, size), F32),
            jax.ShapeDtypeStruct((3, slots), F32),
        ),
        in_specs=[SMEM, SMEM] + [VMEM] * 5 + [ANY, ANY],
        out_specs=(VMEM, VMEM),
        scratch_shapes=[
            pltpu.VMEM((total + 4 * CHUNK, 48), BF16),
            pltpu.VMEM((48, slots), BF16),
            pltpu.VMEM((16, total + 4 * CHUNK), BF16),
            pltpu.VMEM((8, slots), F32),
            pltpu.VMEM((size, size), BF16),
            pltpu.VMEM((slots, slots), BF16),
            pltpu.SemaphoreType.DMA((2,)),
            pltpu.SMEM((slots // 256,), jnp.int32),
            pltpu.SMEM((slots // 256,), jnp.int32),
        ],
        compiler_params=pltpu.CompilerParams(vmem_limit_bytes=SMALL_LIMIT),
        name="near_body",
    )(tile_blocks.reshape(-1), near_count, mine, other, mine_power, other_power, nodes, centre_table, node_table)


def gathered(values, count, partner):
    mine = lax.all_to_all(values, "chip", 0, 0)
    return mine, lax.ppermute(mine, SLAB, partner)


def shards(
    count,
    flow_state,
    flow_speed,
    wall_cell,
    base_shift,
    normals,
    centres,
    tile_blocks,
    near_count,
    near_nodes,
):
    partner = [(i, i ^ 1) for i in range(count)]
    across = [(i, i + 1) for i in range(1, count - 1, 2)]
    across = across + [(j, i) for i, j in across]
    send_a, send_b = edge_rows(flow_state, flow_speed)
    from_a = lax.ppermute(send_a, SLAB, partner)
    from_b = lax.ppermute(send_b, SLAB, across)
    in_order, centre_table, nodes, node_table = ordered(base_shift, normals, centres, wall_cell, near_nodes)
    new_flow, packed = flux_and_right_side(count // 2, flow_state, flow_speed, from_a, from_b, in_order)
    mine, other = gathered(packed, count, partner)
    mine_power, other_power = gathered(powers(mine, other, count), count, partner)
    coefficients, node_shift = near_body(
        tile_blocks, near_count, mine, other, mine_power, other_power, nodes, centre_table, node_table
    )
    return new_flow, coefficients, node_shift


def solution(mesh):
    groups, count = mesh.shape["groups"], mesh.shape["slab"]
    split = Mesh(mesh.devices.reshape(groups, count // 2, 2), ("groups",) + SLAB)
    in_specs = (
        P("groups", SLAB, None),
        P("groups", SLAB, None),
        P(("groups",) + SLAB),
        P("groups", SLAB),
        P("groups", SLAB),
        P("groups", SLAB),
        P("groups", None),
        P("groups"),
        P("groups", SLAB),
    )
    out_specs = (P("groups", SLAB, None), P("groups", SLAB), P("groups", SLAB))
    return jax.shard_map(
        functools.partial(shards, count), mesh=split, in_specs=in_specs, out_specs=out_specs, check_vma=False
    )
```

time: 83.8 us -> 58.9 us (0.70)
  Pallas kernels: 40.9 us -> 20.1 us
  waiting for transfers between devices: 7.74 us -> 5.81 us
  local copies, waits for them, and re-layouts: 4.15 us -> 2.55 us
    pallas_call x1, Pallas kernels: 18.5 us -> 8 us  [powers(): pl.pallas_call(functools.partial(powers_kernel, count), out_shape=jax.Sha...]
    pallas_call x1, Pallas kernels: 14.6 us -> 6.52 us  [near_body(): pl.pallas_call(near_kernel, out_shape=(jax.ShapeDtypeStruct((3, size), F3...]
    ppermute x1, waiting for transfers between devices: 6.4 us -> 3.97 us  [shards(): from_b = lax.ppermute(send_b, SLAB, across)]
    pallas_call x1, Pallas kernels: 5.22 us -> 3.22 us  [flux_and_right_side(): pl.pallas_call(flux_kernel, out_shape=(jax.ShapeDtypeStruct(flow_state.sh...]
    broadcast_in_dim x2 -> x0, local copies, waits for them, and re-layouts: 1.46 us -> none  [gathered(): jnp.broadcast_to(values[None], (chips,) + values.shape)]
    unnamed x15 -> x21, local copies, waits for them, and re-layouts: 2.68 us -> 2.46 us
    pallas_call x1 -> x2, Pallas kernels: 2.51 us -> 2.39 us  [the longest x1 2.06 us: ordered(): pl.pallas_call(order_kernel, out_shape=(jax.ShapeDtypeStruct((16, count),...]
  transfers between devices with their start and end apart: 4 -> 4, of which waited for: 3 -> 3; matrix products, arithmetic and copies ran while one was open for 1% -> 0% of each run, Pallas kernels for 0% -> 4%
where the time goes in v2:
time: 58.9 us; the launch traced here: 58.3 us
  blocking collectives  20.8 us (35%)
  Pallas kernels  20.1 us (34%)
  starting transfers between devices  8.29 us (14%)
  waiting for transfers between devices  5.81 us (10%)
  local copies, waits for them, and re-layouts  2.55 us (4%)
  between operations  0.75 us (1%)
    all_to_all x2, blocking collectives, gathered(): mine = lax.all_to_all(values, 'chip', 0, 0)  20.8 us
    pallas_call x1, Pallas kernels, powers(): pl.pallas_call(functools.partial(powers_kernel, count), out_shape=jax.Sha...  8 us
    pallas_call x1, Pallas kernels, near_body(): pl.pallas_call(near_kernel, out_shape=(jax.ShapeDtypeStruct((3, size), F3...  6.52 us
    ppermute x1, starting transfers between devices, shards(): from_b = lax.ppermute(send_b, SLAB, across)  4.65 us
    ppermute x1, waiting for transfers between devices, shards(): from_b = lax.ppermute(send_b, SLAB, across)  3.97 us
    ppermute x2, starting transfers between devices, gathered(): return (mine, lax.ppermute(mine, SLAB, partner))  3.56 us
    pallas_call x1, Pallas kernels, flux_and_right_side(): pl.pallas_call(flux_kernel, out_shape=(jax.ShapeDtypeStruct(flow_state.sh...  3.22 us
    unnamed x21, local copies, waits for them, and re-layouts  2.46 us
  transfers between devices with their start and end apart: 4, of which 3 were waited for; matrix products, arithmetic and copies ran while one was open for 0% of the time, Pallas kernels for 4%

profile of v2, /device:TPU:1, one launch (start us, length us, event | category | flops | bytes accessed | tf_op | source)
XLA Modules:
  0.0 58.3 jit_solution(9798896470774949112)
XLA Ops:
  0.6 0.0 copy-start
  0.6 1.3 %copy-done = f32[5,8,8192]{2,1,0:T(8,128)S(1)} copy-done((f32[5,8,8192]{2,1,0:T(8,128)S(1)}, f32[5,8,8192]{2,1,0:T(8,128)}, u32[]{:S(2)}) %copy-start) | copy-done | bytes 1310744
  1.9 0.0 copy-start.2
  2.0 1.0 %copy-done.2 = f32[2,8,8192]{2,1,0:T(8,128)S(1)} copy-done((f32[2,8,8192]{2,1,0:T(8,128)S(1)}, f32[2,8,8192]{2,1,0:T(8,128)}, u32[]{:S(2)}) %copy-start.2) | copy-done | bytes 524312
  3.0 0.0 copy-start.3
  3.0 0.0 copy-start.7
  3.0 0.0 copy-start.1
  3.0 0.3 edge_rows.1
  3.4 0.1 collective-permute-start
  3.4 4.7 %collective-permute-start.1 = (f32[6,8192]{1,0:T(8,128)S(1)}, f32[6,8192]{1,0:T(8,128)S(1)}, u32[]{:S(2)}, u32[]{:S(2)}) collective-permute-start(f32[6,8192]{1,0:T(8,128)S(1)} %get-tuple-element.14), channel_id=1, source_target_pairs={{1,2},{3,4},{5,6},{7,8},{9,10},{11,12},{13,14},{2,1},{4,3},{6,5},{... | collective-permute-start | bytes 589832 | tf_op jit(solution)/shard_map/ppermute | solution.py:607
  8.1 0.0 copy-done.3
  8.1 0.0 copy-done.4
  8.1 0.0 copy-done.5
  8.1 0.0 copy-done.6
  8.1 0.0 copy-done.7
  8.2 2.1 %order.1 = (f32[16,512]{1,0:T(8,128)S(1)}, bf16[512,512]{1,0:T(8,128)(2,1)S(1)}, f32[8,1024]{1,0:T(8,128)S(1)}, bf16[1024,1024]{1,0:T(8,128)(2,1)S(1)}) custom-call(f32[3,512]{1,0:T(4,128)S(1)} %copy-done.4, f32[3,512]{1,0:T(4,128)S(1)} %copy-done.5, f32[3,512]{1,0:T(4,128)S(1)} %copy-done.6, s32[1,512]{1,0:T(1,128)S(1)} %bitcast.1, f32[3,1024]{1,0:T(4,128)S(1)} %copy-done.3), custom_call_target="tpu_custom_call" | custom-call | flops 8000000 | bytes 4000000 | tf_op jit(solution)/shard_map/order/pallas_call | solution.py:145
  10.2 0.0 collective-permute-done.a_ref
  10.2 4.0 %collective-permute-done.1.b_ref = f32[6,8192]{1,0:T(8,128)S(1)} collective-permute-done((f32[6,8192]{1,0:T(8,128)S(1)}, f32[6,8192]{1,0:T(8,128)S(1)}, u32[]{:S(2)}, u32[]{:S(2)}) %collective-permute-start.1) | collective-permute-done | bytes 196640 | tf_op jit(solution)/shard_map/ppermute | solution.py:607
  14.2 0.0 copy-done.1
  14.2 3.2 %flux.1 = (f32[5,8,8192]{2,1,0:T(8,128)}, f32[8,8,512]{2,1,0:T(8,128)S(1)}) custom-call(f32[5,8,8192]{2,1,0:T(8,128)S(1)} %copy-done.1, f32[2,8,8192]{2,1,0:T(8,128)S(1)} %copy-done.2, f32[6,8192]{1,0:T(8,128)S(1)} %collective-permute-done.a_ref, f32[6,8192]{1,0:T(8,128)S(1)} %collective-permute-done.1.b_ref, f32[16,512]{1,0:T(8,128)S(1)} %get-tuple-element.15.sorted_ref), custom_call_target="tpu_custom_call" | custom-call | tf_op jit(solution)/shard_map/flux/pallas_call | solution.py:283
  17.4 11.8 %all_to_all.10.mine_ref = f32[8,8,512]{2,1,0:T(8,128)S(1)} all-to-all(f32[8,8,512]{2,1,0:T(8,128)S(1)} %get-tuple-element.17), channel_id=1, replica_groups=mesh['groups'=2,'chip'=8,'core'=2] {'chip'}, dimensions={0} | all-to-all | bytes 262144 | tf_op jit(solution)/shard_map/all_to_all | solution.py:586
  29.2 1.7 %collective-permute-start.2 = (f32[8,8,512]{2,1,0:T(8,128)S(1)}, f32[8,8,512]{2,1,0:T(8,128)S(1)}, u32[]{:S(2)}, u32[]{:S(2)}) collective-permute-start(f32[8,8,512]{2,1,0:T(8,128)S(1)} %all_to_all.10.mine_ref), channel_id=1, source_target_pairs={{0,1},{1,0},{2,3},{3,2},{4,5},{5,4},{6,7},{7,6},{8,9},{9,8},{10,11... | collective-permute-start | bytes 393224 | tf_op jit(solution)/shard_map/ppermute | solution.py:587
  31.0 1.0 %collective-permute-done.2.other_ref = f32[8,8,512]{2,1,0:T(8,128)S(1)} collective-permute-done((f32[8,8,512]{2,1,0:T(8,128)S(1)}, f32[8,8,512]{2,1,0:T(8,128)S(1)}, u32[]{:S(2)}, u32[]{:S(2)}) %collective-permute-start.2) | collective-permute-done | bytes 131104 | tf_op jit(solution)/shard_map/ppermute | solution.py:587
  31.9 8.0 %powers.1 = f32[8,8,640]{2,1,0:T(8,128)S(1)} custom-call(f32[8,8,512]{2,1,0:T(8,128)S(1)} %all_to_all.10.mine_ref, f32[8,8,512]{2,1,0:T(8,128)S(1)} %collective-permute-done.2.other_ref), custom_call_target="tpu_custom_call" | custom-call | tf_op jit(solution)/shard_map/powers/pallas_call | solution.py:425
  39.9 9.0 %all_to_all.11.mine_power = f32[8,8,640]{2,1,0:T(8,128)S(1)} all-to-all(f32[8,8,640]{2,1,0:T(8,128)S(1)} %powers.1), channel_id=1, replica_groups=mesh['groups'=2,'chip'=8,'core'=2] {'chip'}, dimensions={0} | all-to-all | bytes 327680 | tf_op jit(solution)/shard_map/all_to_all | solution.py:586
  48.9 1.8 %collective-permute-start.3 = (f32[8,8,640]{2,1,0:T(8,128)S(1)}, f32[8,8,640]{2,1,0:T(8,128)S(1)}, u32[]{:S(2)}, u32[]{:S(2)}) collective-permute-start(f32[8,8,640]{2,1,0:T(8,128)S(1)} %all_to_all.11.mine_power), channel_id=1, source_target_pairs={{0,1},{1,0},{2,3},{3,2},{4,5},{5,4},{6,7},{7,6},{8,9},{9,8},{10,11... | collective-permute-start | bytes 491528 | tf_op jit(solution)/shard_map/ppermute | solution.py:587
  50.8 0.0 copy-done.9
  50.8 0.1 copy.13
  50.8 0.1 reshape.13.tile_ref
  50.9 0.9 %collective-permute-done.3.other_power = f32[8,8,640]{2,1,0:T(8,128)S(1)} collective-permute-done((f32[8,8,640]{2,1,0:T(8,128)S(1)}, f32[8,8,640]{2,1,0:T(8,128)S(1)}, u32[]{:S(2)}, u32[]{:S(2)}) %collective-permute-start.3) | collective-permute-done | bytes 163872 | tf_op jit(solution)/shard_map/ppermute | solution.py:587
  51.8 0.0 copy-done.8
  51.8 6.5 %near_body.1 = (f32[3,512]{1,0:T(4,128)}, f32[3,1024]{1,0:T(4,128)}) custom-call(s32[64]{0:T(128)S(1)} %reshape.13.tile_ref, s32[16]{0:T(128)S(1)} %copy-done.8, f32[8,8,512]{2,1,0:T(8,128)S(1)} %all_to_all.10.mine_ref, f32[8,8,512]{2,1,0:T(8,128)S(1)} %collective-permute-done.2.other_ref, f32[8,8,640]{2,1,0:T(8,128)S(1)} %all_to_all.11.mine_power, ...), custom_call_target="tpu_custom_call" | custom-call | tf_op jit(solution)/shard_map/near_body/pallas_call | solution.py:561
  (5 shorter events, 0.0 us)
Async XLA Ops:
  0.6 1.3 %copy-start = (f32[5,8,8192]{2,1,0:T(8,128)S(1)}, f32[5,8,8192]{2,1,0:T(8,128)}, u32[]{:S(2)}) copy-start(f32[5,8,8192]{2,1,0:T(8,128)} %q_ref.3) | copy-start | bytes 3932164
  1.9 1.0 %copy-start.2 = (f32[2,8,8192]{2,1,0:T(8,128)S(1)}, f32[2,8,8192]{2,1,0:T(8,128)}, u32[]{:S(2)}) copy-start(f32[2,8,8192]{2,1,0:T(8,128)} %w_ref.3) | copy-start | bytes 1572868
  3.0 5.1 %copy-start.3 = (f32[3,1024]{1,0:T(4,128)S(1)}, f32[3,1024]{1,0:T(4,128)}, u32[]{:S(2)}) copy-start(f32[3,1024]{1,0:T(4,128)} %nodes_ref.1) | copy-start | bytes 36868
  3.0 5.1 %copy-start.4 = (f32[3,512]{1,0:T(4,128)S(1)}, f32[3,512]{1,0:T(4,128)}, u32[]{:S(2)}) copy-start(f32[3,512]{1,0:T(4,128)} %base_ref.1) | copy-start | bytes 18436
  3.0 5.1 %copy-start.5 = (f32[3,512]{1,0:T(4,128)S(1)}, f32[3,512]{1,0:T(4,128)}, u32[]{:S(2)}) copy-start(f32[3,512]{1,0:T(4,128)} %normal_ref.1) | copy-start | bytes 18436
  3.0 5.1 %copy-start.6 = (f32[3,512]{1,0:T(4,128)S(1)}, f32[3,512]{1,0:T(4,128)}, u32[]{:S(2)}) copy-start(f32[3,512]{1,0:T(4,128)} %centre_ref.1) | copy-start | bytes 18436
  3.0 5.1 %copy-start.7 = (s32[512]{0:T(512)S(1)}, s32[512]{0:T(512)}, u32[]{:S(2)}) copy-start(s32[512]{0:T(512)} %param.11) | copy-start | bytes 6148
  3.0 11.2 %copy-start.1 = (f32[5,8,8192]{2,1,0:T(8,128)S(1)}, f32[5,8,8192]{2,1,0:T(8,128)}, u32[]{:S(2)}) copy-start(f32[5,8,8192]{2,1,0:T(8,128)} %q_ref.3) | copy-start | bytes 3932164
  3.4 6.9 %collective-permute-start = (f32[6,8192]{1,0:T(8,128)S(1)}, f32[6,8192]{1,0:T(8,128)S(1)}, u32[]{:S(2)}, u32[]{:S(2)}) collective-permute-start(f32[6,8192]{1,0:T(8,128)S(1)} %get-tuple-element.13), channel_id=1, source_target_pairs={{0,1},{1,0},{2,3},{3,2},{4,5},{5,4},{6,7},{7,6},{8,9},{9,8},{10,11... | collective-permute-start | bytes 589832 | tf_op jit(solution)/shard_map/ppermute | solution.py:606
  3.4 10.8 %collective-permute-start.1 = (f32[6,8192]{1,0:T(8,128)S(1)}, f32[6,8192]{1,0:T(8,128)S(1)}, u32[]{:S(2)}, u32[]{:S(2)}) collective-permute-start(f32[6,8192]{1,0:T(8,128)S(1)} %get-tuple-element.14), channel_id=1, source_target_pairs={{1,2},{3,4},{5,6},{7,8},{9,10},{11,12},{13,14},{2,1},{4,3},{6,5},{... | collective-permute-start | bytes 589832 | tf_op jit(solution)/shard_map/ppermute | solution.py:607
  14.2 36.6 %copy-start.9 = (s32[16,4]{0,1:T(4,128)S(1)}, s32[16,4]{0,1:T(4,128)}, u32[]{:S(2)}) copy-start(s32[16,4]{0,1:T(4,128)} %param.15) | copy-start | bytes 772
  14.2 37.6 %copy-start.8 = (s32[16]{0:T(128)S(1)}, s32[16]{0:T(128)}, u32[]{:S(2)}) copy-start(s32[16]{0:T(128)} %count_ref.1) | copy-start | bytes 196
  29.2 2.7 %collective-permute-start.2 = (f32[8,8,512]{2,1,0:T(8,128)S(1)}, f32[8,8,512]{2,1,0:T(8,128)S(1)}, u32[]{:S(2)}, u32[]{:S(2)}) collective-permute-start(f32[8,8,512]{2,1,0:T(8,128)S(1)} %all_to_all.10.mine_ref), channel_id=1, source_target_pairs={{0,1},{1,0},{2,3},{3,2},{4,5},{5,4},{6,7},{7,6},{8,9},{9,8},{10,11... | collective-permute-start | bytes 393224 | tf_op jit(solution)/shard_map/ppermute | solution.py:587
  48.9 2.9 %collective-permute-start.3 = (f32[8,8,640]{2,1,0:T(8,128)S(1)}, f32[8,8,640]{2,1,0:T(8,128)S(1)}, u32[]{:S(2)}, u32[]{:S(2)}) collective-permute-start(f32[8,8,640]{2,1,0:T(8,128)S(1)} %all_to_all.11.mine_power), channel_id=1, source_target_pairs={{0,1},{1,0},{2,3},{3,2},{4,5},{5,4},{6,7},{7,6},{8,9},{9,8},{10,11... | collective-permute-start | bytes 491528 | tf_op jit(solution)/shard_map/ppermute | solution.py:587

commit v3 on v2

--- a/solution.py
+++ b/solution.py
@@ -23,7 +23,7 @@
 SLAB = ("chip", "core")
 VMEM = pl.BlockSpec(memory_space=pltpu.VMEM)
 SMEM = pl.BlockSpec(memory_space=pltpu.SMEM)
-ANY = pl.BlockSpec(memory_space=pl.ANY)
+HBM = pl.BlockSpec(memory_space=pltpu.HBM)
 
 
 def parts(values):
@@ -158,30 +158,31 @@
     )(base_shift, normals, centres, wall_cell.reshape(1, -1), near_nodes)
 
 
-def edge_kernel(q_ref, w_ref, a_ref, b_ref, sems):
-    count = q_ref.shape[0]
-    last = q_ref.shape[1] - 1
+def edge_kernel(q_hbm, w_hbm, a_ref, b_ref, q_ref, w_ref, sems):
+    count, rows, _ = q_ref.shape
+    copies = [pltpu.make_async_copy(w_hbm.at[index], w_ref.at[index], sems.at[index]) for index in range(2)]
+    copies += [
+        pltpu.make_async_copy(q_hbm.at[index], q_ref.at[index], sems.at[2 + index]) for index in range(count)
+    ]
+    for copy in copies:
+        copy.start()
     core = lax.axis_index("core")
+    for copy in copies:
+        copy.wait()
 
     def move(row_a, row_b):
-        copies = [
-            pltpu.make_async_copy(q_ref.at[:, row_a], a_ref.at[pl.ds(0, count)], sems.at[0]),
-            pltpu.make_async_copy(q_ref.at[:, row_b], b_ref.at[pl.ds(0, count)], sems.at[1]),
-            pltpu.make_async_copy(w_ref.at[pl.ds(0, 1), row_a], a_ref.at[pl.ds(count, 1)], sems.at[2]),
-            pltpu.make_async_copy(w_ref.at[pl.ds(0, 1), row_b], b_ref.at[pl.ds(count, 1)], sems.at[3]),
-        ]
-        for copy in copies:
-            copy.start()
-        for copy in copies:
-            copy.wait()
+        for target, row in ((a_ref, row_a), (b_ref, row_b)):
+            for index in range(count):
+                target[index : index + 1] = q_ref[index, row : row + 1]
+            target[count : count + 1] = w_ref[0, row : row + 1]
 
     @pl.when(core == 0)
     def _():
-        move(last, 0)
+        move(rows - 1, 0)
 
     @pl.when(core != 0)
     def _():
-        move(0, last)
+        move(0, rows - 1)
 
 
 def edge_rows(flow_state, flow_speed):
@@ -189,36 +190,51 @@
     rows = jax.ShapeDtypeStruct((count + 1, plane), F32)
     return pl.pallas_call(
         edge_kernel,
-        out_shape=(rows, rows),
-        in_specs=[ANY, ANY],
-        out_specs=(VMEM, VMEM),
-        scratch_shapes=[pltpu.SemaphoreType.DMA((4,))],
+        out_shape=(
+            rows,
+            rows,
+            jax.ShapeDtypeStruct(flow_state.shape, F32),
+            jax.ShapeDtypeStruct(flow_speed.shape, F32),
+        ),
+        in_specs=[HBM, HBM],
+        out_specs=(VMEM,) * 4,
+        scratch_shapes=[pltpu.SemaphoreType.DMA((count + 2,))],
         compiler_params=pltpu.CompilerParams(vmem_limit_bytes=SMALL_LIMIT),
         name="edge_rows",
     )(flow_state, flow_speed)
 
 
-def flux_kernel(
-    q_ref, w_ref, a_ref, b_ref, sorted_ref, new_ref, out_ref
-):
+RATE = 0.5 * FLUX_STEP
+PRESSURE = 4
+
+
+def picked(stacked, chosen, lane):
+    high, middle, low = parts(stacked)
+    pieces = jnp.concatenate([high, middle, low], axis=1).astype(BF16)
+    both = lax.dot_general(pieces, chosen, (((0,), (0,)), ((), ())), preferred_element_type=F32)
+    value = (both[:128] + both[128:256]) + both[256:]
+    here = lax.broadcasted_iota(jnp.int32, value.shape, 0) == lane
+    return jnp.sum(jnp.where(here, value, 0.0), axis=0, keepdims=True)
+
+
+def stacked_lanes(values):
+    return jnp.concatenate([values[:, i : i + 128] for i in range(0, values.shape[1], 128)], axis=0)
+
+
+def inner_kernel(q_ref, w_ref, sorted_ref, new_hbm, low_ref, high_ref, out_ref, chosen_ref, new_ref, sems):
     count, rows, plane = q_ref.shape
     width = 512
-    even = lax.axis_index("core") == 0
-    pressure = 4
-    rate = 0.5 * FLUX_STEP
+    steps = plane // width
+    row = lax.broadcasted_iota(jnp.int32, (rows, width), 0)
+
+    def copy_of(step):
+        lanes = pl.ds(pl.multiple_of(step * width, width), width)
+        return pltpu.make_async_copy(new_ref.at[:, :, lanes], new_hbm.at[:, :, lanes], sems.at[step])
 
     def chunk(step, _):
         here = pl.multiple_of(step * width, 128)
         left = pl.multiple_of(lax.rem(here + plane - 128, plane), 128)
         right = pl.multiple_of(lax.rem(here + width, plane), 128)
-        below = jnp.where(even, b_ref[:, pl.ds(here, width)], a_ref[:, pl.ds(here, width)])
-        above = jnp.where(even, a_ref[:, pl.ds(here, width)], b_ref[:, pl.ds(here, width)])
-        row = lax.broadcasted_iota(jnp.int32, (rows, width), 0)
-
-        def axial(values, index):
-            down = jnp.where(row == 0, below[index : index + 1], pltpu.roll(values, 1, 0))
-            up = jnp.where(row == rows - 1, above[index : index + 1], pltpu.roll(values, rows - 1, 0))
-            return down, up
 
         def cyclic(ref, index):
             values = ref[index, :, pl.ds(here, width)]
@@ -230,12 +246,11 @@
             return values, before, after
 
         w = w_ref[0, :, pl.ds(here, width)]
-        w_down, w_up = axial(w, count)
-        face_low = rate * (w_down + w)
-        face_high = rate * (w + w_up)
+        face_low = jnp.where(row == 0, 0.0, RATE * (pltpu.roll(w, 1, 0) + w))
+        face_high = jnp.where(row == rows - 1, 0.0, RATE * (w + pltpu.roll(w, rows - 1, 0)))
         speed, speed_before, speed_after = cyclic(w_ref, 1)
-        face_left = rate * (speed_before + speed)
-        face_right = rate * (speed + speed_after)
+        face_left = RATE * (speed_before + speed)
+        face_right = RATE * (speed + speed_after)
         low_in = jnp.maximum(face_low, 0.0)
         high_out = jnp.minimum(face_high, 0.0)
         left_in = jnp.maximum(face_left, 0.0)
@@ -246,51 +261,110 @@
         )
         for index in range(count):
             values, before, after = cyclic(q_ref, index)
-            down, up = axial(values, index)
-            new_ref[index, :, pl.ds(here, width)] = (
-                keep * values + low_in * down - high_out * up + left_in * before - right_out * after
+            new = (
+                keep * values
+                + low_in * pltpu.roll(values, 1, 0)
+                - high_out * pltpu.roll(values, rows - 1, 0)
+                + left_in * before
+                - right_out * after
             )
+            new_ref[index, :, pl.ds(here, width)] = new
+            low_ref[index : index + 1, pl.ds(here, width)] = new[0:1]
+            high_ref[index : index + 1, pl.ds(here, width)] = new[rows - 1 : rows]
+        copy_of(step).start()
         return 0
 
-    lax.fori_loop(0, plane // width, chunk, 0)
+    lax.fori_loop(0, steps, chunk, 0)
 
     cells = sorted_ref[9:10].astype(jnp.int32)
-    lanes = plane // 128
     cell_row = cells // plane
     column = cells - cell_row * plane
     group = column // 128
     lane = column - group * 128
-    stacked = jnp.concatenate(
-        [new_ref[pressure, :, index * 128 : index * 128 + 128] for index in range(lanes)], axis=0
-    )
     place = group * rows + cell_row
     centres = cells.shape[1]
+    lanes = plane // 128
     chosen = (lax.broadcasted_iota(jnp.int32, (rows * lanes, centres), 0) == place).astype(F32).astype(BF16)
-    pieces = jnp.concatenate(parts(stacked), axis=1).astype(BF16)
-    both = lax.dot_general(pieces, chosen, (((0,), (0,)), ((), ())), preferred_element_type=F32)
-    picked = (both[:128] + both[128:256]) + both[256:]
-    load = jnp.sum(
-        jnp.where(lax.broadcasted_iota(jnp.int32, (128, centres), 0) == lane, picked, 0.0), axis=0, keepdims=True
+    chosen_ref[...] = chosen
+    load = picked(stacked_lanes(new_ref[PRESSURE]), chosen, lane)
+    out_ref[...] = jnp.concatenate(
+        [
+            sorted_ref[0:3] + sorted_ref[3:6] * load,
+            sorted_ref[3:9],
+            lane.astype(F32),
+            jnp.zeros((6, centres), F32),
+        ],
+        axis=0,
     )
-    packed = jnp.concatenate(
-        [sorted_ref[0:3] + sorted_ref[3:6] * load, sorted_ref[6:9], jnp.zeros((2, centres), F32)], axis=0
-    )
+    for step in range(steps):
+        copy_of(step).wait()
+
+
+def inner_flux(flow_state, flow_speed, in_order):
+    count, rows, plane = flow_state.shape
+    centres = in_order.shape[1]
+    edge = jax.ShapeDtypeStruct((count, plane), F32)
+    return pl.pallas_call(
+        inner_kernel,
+        out_shape=(
+            jax.ShapeDtypeStruct(flow_state.shape, F32),
+            edge,
+            edge,
+            jax.ShapeDtypeStruct((16, centres), F32),
+            jax.ShapeDtypeStruct((rows * plane // 128, centres), BF16),
+        ),
+        in_specs=[VMEM] * 3,
+        out_specs=(HBM, VMEM, VMEM, VMEM, VMEM),
+        scratch_shapes=[pltpu.VMEM(flow_state.shape, F32), pltpu.SemaphoreType.DMA((plane // 512,))],
+        compiler_params=pltpu.CompilerParams(vmem_limit_bytes=SMALL_LIMIT),
+        cost_estimate=pl.CostEstimate(flops=20_000_000, bytes_accessed=4_000_000, transcendentals=0),
+        name="inner_flux",
+    )(flow_state, flow_speed, in_order)
+
+
+def outer_kernel(
+    send_a, send_b, from_a, from_b, low_ref, high_ref, base_ref, chosen_ref, out_ref, new_low, new_high, both_ref
+):
+    count, plane = low_ref.shape
+    rows = both_ref.shape[0]
+    even = lax.axis_index("core") == 0
+    own_low = jnp.where(even, send_b[...], send_a[...])
+    own_high = jnp.where(even, send_a[...], send_b[...])
+    below = jnp.where(even, from_b[...], from_a[...])
+    above = jnp.where(even, from_a[...], from_b[...])
+
+    def flux(first, second):
+        face = RATE * (first[count : count + 1] + second[count : count + 1])
+        return jnp.maximum(face, 0.0) * first[:count] + jnp.minimum(face, 0.0) * second[:count]
+
+    low = flux(below, own_low)
+    high = flux(own_high, above)
+    new_low[...] = low_ref[...] + low
+    new_high[...] = high_ref[...] - high
+    row = lax.broadcasted_iota(jnp.int32, (rows, plane), 0)
+    zero = jnp.zeros((rows, plane), F32)
+    added = jnp.where(row == 0, low[PRESSURE : PRESSURE + 1], zero)
+    added = added - jnp.where(row == rows - 1, high[PRESSURE : PRESSURE + 1], zero)
+    both_ref[...] = added
+    base = base_ref[...]
+    load = picked(stacked_lanes(both_ref[...]), chosen_ref[...], base[9:10].astype(jnp.int32))
+    centres = base.shape[1]
+    packed = jnp.concatenate([base[0:3] + base[3:6] * load, base[6:9], jnp.zeros((2, centres), F32)], axis=0)
     for chip in range(out_ref.shape[0]):
         out_ref[chip] = packed
 
 
-def flux_and_right_side(chips, flow_state, flow_speed, from_a, from_b, in_order):
+def right_side(chips, rows, send_a, send_b, from_a, from_b, low, high, base, chosen):
+    edge = jax.ShapeDtypeStruct(low.shape, F32)
     return pl.pallas_call(
-        flux_kernel,
-        out_shape=(
-            jax.ShapeDtypeStruct(flow_state.shape, F32),
-            jax.ShapeDtypeStruct((chips, 8, in_order.shape[1]), F32),
-        ),
-        in_specs=[VMEM] * 5,
-        out_specs=(VMEM, VMEM),
+        outer_kernel,
+        out_shape=(jax.ShapeDtypeStruct((chips, 8, base.shape[1]), F32), edge, edge),
+        in_specs=[VMEM] * 8,
+        out_specs=(VMEM,) * 3,
+        scratch_shapes=[pltpu.VMEM((rows, low.shape[1]), F32)],
         compiler_params=pltpu.CompilerParams(vmem_limit_bytes=SMALL_LIMIT),
-        name="flux",
-    )(flow_state, flow_speed, from_a, from_b, in_order)
+        name="outer_flux",
+    )(send_a, send_b, from_a, from_b, low, high, base, chosen)
 
 
 def block_of(mine_ref, other_ref, block, core):
@@ -300,8 +374,17 @@
 
 
 def powers_kernel(
-    count, mine_ref, other_ref, out_ref, source_side, target_side, vector, tables, low_ref, high_ref
+    count, mine_ref, other_ref, new_low, new_high, new_in, out_ref, new_out,
+    source_side, target_side, vector, image, tables, low_ref, high_ref, sems,
 ):
+    del new_in
+    rows_per_block = new_out.shape[1]
+    copies = [
+        pltpu.make_async_copy(new_low, new_out.at[:, 0], sems.at[0]),
+        pltpu.make_async_copy(new_high, new_out.at[:, rows_per_block - 1], sems.at[1]),
+    ]
+    for copy in copies:
+        copy.start()
     size = mine_ref.shape[2]
     chip, core = lax.axis_index("chip"), lax.axis_index("core")
     me = chip * 2 + core
@@ -335,67 +418,98 @@
     def steps_of(tile):
         return lax.div(high_ref[tile] - low_ref[tile] + (reach - 1), reach)
 
-    def build_tile(tile, _):
+    most = steps_of(0)
+    for tile in range(1, tiles):
+        most = jnp.maximum(most, steps_of(tile))
+    same = lax.broadcasted_iota(jnp.int32, (CHUNK, CHUNK), 0) == lax.broadcasted_iota(
+        jnp.int32, (CHUNK, CHUNK), 1
+    )
+
+    def build(tile, step):
         lanes = pl.ds(pl.multiple_of(tile * width + size, width), width)
-        targets = target_side[:, lanes]
-
-        def build(step, _):
-            chunk = low_ref[tile] + step * reach
-            rows = pl.ds(pl.multiple_of(chunk * CHUNK, CHUNK), span)
-            table = quarter_kernel(source_side[rows], targets)
-            high = table.astype(BF16)
-            tables[tile, step, :span] = high
-            tables[tile, step, span:] = (table - high.astype(F32)).astype(BF16)
-            for piece in range(width // CHUNK):
-                place = (tile * width + size) // CHUNK + piece - chunk
-
-                @pl.when(jnp.logical_and(place >= 0, place < reach))
-                def _(place=place, piece=piece):
-                    same = lax.broadcasted_iota(jnp.int32, (CHUNK, CHUNK), 0) == lax.broadcasted_iota(
-                        jnp.int32, (CHUNK, CHUNK), 1
-                    )
-                    for half in range(2):
-                        at = pl.ds(pl.multiple_of(place * CHUNK + half * span, CHUNK), CHUNK)
-                        columns = slice(piece * CHUNK, (piece + 1) * CHUNK)
-                        old = tables[tile, step, at, columns].astype(F32)
-                        tables[tile, step, at, columns] = jnp.where(same, 0.0, old).astype(BF16)
-
-            return 0
-
-        lax.fori_loop(0, steps_of(tile), build, 0)
-        return 0
-
-    lax.fori_loop(0, tiles, build_tile, 0)
-
-    def applied(tile):
-        def one(step):
-            lanes = pl.ds(pl.multiple_of((low_ref[tile] + step * reach) * CHUNK, CHUNK), span)
-            window = vector[:, lanes]
-            return jnp.dot(
-                jnp.concatenate([window, window], axis=1), tables[tile, step], preferred_element_type=F32
-            )
-
-        both = lax.fori_loop(1, steps_of(tile), lambda step, old: old + one(step), one(0))
-        return 4.0 * (both[:8] + both[8:])
-
-    def power(slot):
-        first = (slot - 1) * size // width
-        values = jnp.concatenate([applied(first + i) for i in range(size // width)], axis=1)
-        return jnp.where(live[slot], values, 0.0)
+        chunk = low_ref[tile] + step * reach
+        rows = pl.ds(pl.multiple_of(chunk * CHUNK, CHUNK), span)
+        table = quarter_kernel(source_side[rows], target_side[:, lanes])
+        high = table.astype(BF16)
+        tables[tile, step, :span] = high
+        tables[tile, step, span:] = (table - high.astype(F32)).astype(BF16)
+        for piece in range(width // CHUNK):
+            place = (tile * width + size) // CHUNK + piece - chunk
+            inside = jnp.logical_and(place >= 0, place < reach)
+            place = jnp.clip(place, 0, reach - 1)
+            for half in range(2):
+                at = pl.ds(pl.multiple_of(place * CHUNK + half * span, CHUNK), CHUNK)
+                columns = slice(piece * CHUNK, (piece + 1) * CHUNK)
+                old = tables[tile, step, at, columns]
+                tables[tile, step, at, columns] = jnp.where(jnp.logical_and(same, inside), 0.0, old.astype(F32)).astype(BF16)
+
+    def one(tile, step):
+        lanes = pl.ds(pl.multiple_of((low_ref[tile] + step * reach) * CHUNK, CHUNK), span)
+        window = vector[:, lanes]
+        return jnp.dot(jnp.concatenate([window, window], axis=1), tables[tile, step], preferred_element_type=F32)
+
+    def lanes_of(tile):
+        return pl.ds(pl.multiple_of(tile * width, width), width)
+
+    def further(first, last):
+        @pl.when(most > 1)
+        def _():
+            def of_tile(tile, _):
+                def add(step, _):
+                    image[:, lanes_of(tile)] += one(tile, step)
+                    return 0
+
+                return lax.fori_loop(1, steps_of(tile), add, 0)
+
+            lax.fori_loop(first, last, of_tile, 0)
+
+    def image_of(slot):
+        both = image[:, (slot - 1) * size : slot * size]
+        return jnp.where(live[slot], 4.0 * (both[:8] + both[8:]), 0.0)
+
+    def power(slots):
+        first, last = (slots[0] - 1) * size // width, slots[-1] * size // width
+        for tile in range(first, last):
+            image[:, tile * width : (tile + 1) * width] = one(tile, 0)
+        further(first, last)
+        return {slot: image_of(slot) for slot in slots}
 
     def hold(values, slot):
         vector[:, slot * size : (slot + 1) * size] = doubled(values)
 
     for slot in range(slots):
         hold(zeroth[slot], slot)
-    first = {slot: power(slot) for slot in range(1, 5)}
+
+    def tile_step(tile, _):
+        before = jnp.maximum(tile - 1, 0)
+        image[:, lanes_of(before)] = one(before, 0)
+        build(tile, 0)
+        return 0
+
+    build(0, 0)
+    lax.fori_loop(1, tiles, tile_step, 0)
+    image[:, (tiles - 1) * width : tiles * width] = one(tiles - 1, 0)
+
+    @pl.when(most > 1)
+    def _():
+        def of_tile(tile, _):
+            def more(step, _):
+                build(tile, step)
+                return 0
+
+            return lax.fori_loop(1, steps_of(tile), more, 0)
+
+        lax.fori_loop(0, tiles, of_tile, 0)
+
+    further(0, tiles)
+    first = {slot: image_of(slot) for slot in range(1, 5)}
     for slot in range(1, 5):
         hold(first[slot], slot)
-    second = {slot: power(slot) for slot in range(2, 4)}
+    second = power([2, 3])
     hold(jnp.zeros((8, size), F32), 1)
     hold(second[2], 2)
     hold(2.0 * second[3], 3)
-    last = power(2)
+    last = power([2])[2]
 
     def inner(left, right):
         return jnp.sum(left * right, axis=1, keepdims=True)
@@ -416,28 +530,36 @@
     for index in range(out_ref.shape[0]):
         out_ref[index, :, :size] = values
         out_ref[index, :, size:] = packed
-
-
-def powers(mine, other, count):
+    for copy in copies:
+        copy.wait()
+
+
+def powers(mine, other, new_low, new_high, new_flow, count):
     chips, _, size = mine.shape
     tiles = 4 * size // 256
     steps = (6 * size // CHUNK + 5) // 6
     return pl.pallas_call(
         functools.partial(powers_kernel, count),
-        out_shape=jax.ShapeDtypeStruct((chips, 8, size + 128), F32),
-        in_specs=[VMEM, VMEM],
-        out_specs=VMEM,
+        out_shape=(
+            jax.ShapeDtypeStruct((chips, 8, size + 128), F32),
+            jax.ShapeDtypeStruct(new_flow.shape, F32),
+        ),
+        in_specs=[VMEM] * 4 + [HBM],
+        out_specs=(VMEM, HBM),
         scratch_shapes=[
             pltpu.VMEM((6 * size + 6 * CHUNK, 48), BF16),
             pltpu.VMEM((48, 6 * size), BF16),
             pltpu.VMEM((16, 6 * size + 6 * CHUNK), BF16),
+            pltpu.VMEM((16, 4 * size), F32),
             pltpu.VMEM((tiles, steps, 12 * CHUNK, 256), BF16),
             pltpu.SMEM((tiles,), jnp.int32),
             pltpu.SMEM((tiles,), jnp.int32),
+            pltpu.SemaphoreType.DMA((2,)),
         ],
+        input_output_aliases={4: 1},
         compiler_params=pltpu.CompilerParams(vmem_limit_bytes=BIG_LIMIT),
         name="powers",
-    )(mine, other)
+    )(mine, other, new_low, new_high, new_flow)
 
 
 def ratio(top, bottom):
@@ -479,26 +601,64 @@
     return coefficients
 
 
+REACH = 7
+
+
+def points_kernel(tile_ref, mine_ref, other_ref, nodes_ref, source_ref, target_ref, low_ref, high_ref):
+    size = mine_ref.shape[2]
+    core = lax.axis_index("core")
+    me = lax.axis_index("chip") * 2 + core
+    listed = tile_ref.shape[0] // (2 * mine_ref.shape[0])
+    origin = lax.div((tile_ref[me * listed] + 2) * 2, 5).astype(F32)
+    third = []
+    for index in range(listed):
+        data = block_of(mine_ref, other_ref, tile_ref[me * listed + index], core)
+        points = local_points(data[3:6], origin)
+        third.append(points[2:3])
+        source, _ = sides(points)
+        source_ref[index * size : (index + 1) * size] = source.T.astype(BF16)
+    span = REACH * CHUNK
+    far = (lax.broadcasted_iota(jnp.int32, (span, 48), 1) == 3).astype(F32) * 4096.0
+    source_ref[listed * size :] = far.astype(BF16)
+    points = local_points(nodes_ref[0:3], origin)
+    _, target = sides(points)
+    target_ref[...] = target.astype(BF16)
+    chunk_bounds(jnp.concatenate(third, axis=1), points[2:3], CHUNK, low_ref, high_ref)
+
+
+def near_points(tiles, listed, mine, other, nodes):
+    size = mine.shape[2]
+    slots = nodes.shape[1]
+    bounds = jax.ShapeDtypeStruct((slots // CHUNK,), jnp.int32)
+    return pl.pallas_call(
+        points_kernel,
+        out_shape=(
+            jax.ShapeDtypeStruct((listed * size + REACH * CHUNK, 48), BF16),
+            jax.ShapeDtypeStruct((48, slots), BF16),
+            bounds,
+            bounds,
+        ),
+        in_specs=[SMEM] + [VMEM] * 3,
+        out_specs=(VMEM, VMEM, SMEM, SMEM),
+        compiler_params=pltpu.CompilerParams(vmem_limit_bytes=SMALL_LIMIT),
+        cost_estimate=pl.CostEstimate(flops=1_000_000, bytes_accessed=1_000_000, transcendentals=0),
+        name="near_points",
+    )(tiles, mine, other, nodes)
+
+
 def near_kernel(
-    tile_ref, count_ref, mine_ref, other_ref, mine_power, other_power, nodes_ref, centre_hbm, node_hbm,
-    coef_ref, shift_ref,
-    source_side, target_side, vector, result, centre_table, node_table, sems, low_ref, high_ref,
+    tile_ref, count_ref, low_ref, high_ref, mine_ref, other_ref, mine_power, other_power, source_side, target_side,
+    centre_table, node_table, coef_ref, shift_ref, vector, result,
 ):
     size = mine_ref.shape[2]
-    slots = nodes_ref.shape[1]
+    slots = target_side.shape[1]
     chips = mine_ref.shape[0]
     core = lax.axis_index("core")
     me = lax.axis_index("chip") * 2 + core
     listed = tile_ref.shape[0] // count_ref.shape[0]
-    width, reach = 256, 4
-    span = reach * CHUNK
+    width = CHUNK
+    span = REACH * CHUNK
     total = listed * size
-    copies = [
-        pltpu.make_async_copy(centre_hbm, centre_table, sems.at[0]),
-        pltpu.make_async_copy(node_hbm, node_table, sems.at[1]),
-    ]
-    for copy in copies:
-        copy.start()
 
     summed = mine_power[0, :, size:] + other_power[0, :, size:]
     for index in range(1, chips):
@@ -510,76 +670,55 @@
         power = block_of(mine_power, other_power, block, core)[:, :size]
         values = weights[0] * data + weights[1] * power + weights[2] * pltpu.roll(power, 5, 0)
         keep = lax.broadcasted_iota(jnp.int32, (8, size), 0) < 3
-        return data, jnp.where(keep, values, 0.0)
-
-    origin = lax.div((tile_ref[me * listed] + 2) * 2, 5).astype(F32)
-    third = []
+        return jnp.where(keep, values, 0.0)
+
     for index in range(listed):
-        data, values = coefficients_of(tile_ref[me * listed + index])
-        points = local_points(data[3:6], origin)
-        third.append(points[2:3])
-        source, _ = sides(points)
-        source_side[index * size : (index + 1) * size] = source.T.astype(BF16)
+        values = coefficients_of(tile_ref[me * listed + index])
         vector[:, index * size : (index + 1) * size] = doubled(values)
-    far = (lax.broadcasted_iota(jnp.int32, (span, 48), 1) == 3).astype(F32) * 4096.0
-    source_side[total:] = far.astype(BF16)
     vector[:, total:] = jnp.zeros((16, span), BF16)
-    points = local_points(nodes_ref[0:3], origin)
-    _, target = sides(points)
-    target_side[...] = target.astype(BF16)
-    chunk_bounds(jnp.concatenate(third, axis=1), points[2:3], width, low_ref, high_ref)
 
     def node_tile(tile, _):
         lanes = pl.ds(pl.multiple_of(tile * width, width), width)
         targets = target_side[:, lanes]
 
         def one(step, old):
-            start = pl.multiple_of((low_ref[tile] + step * reach) * CHUNK, CHUNK)
+            start = pl.multiple_of((low_ref[tile] + step * REACH) * CHUNK, CHUNK)
             table = quarter_kernel(source_side[pl.ds(start, span)], targets)
             window = vector[:, pl.ds(start, span)]
             return old + jnp.dot(
                 jnp.concatenate([window, window], axis=1), doubled(table), preferred_element_type=F32
             )
 
-        steps = lax.div(high_ref[tile] - low_ref[tile] + (reach - 1), reach)
+        steps = lax.div(high_ref[tile] - low_ref[tile] + (REACH - 1), REACH)
         both = lax.fori_loop(0, steps, one, jnp.zeros((16, width), F32))
         result[:, lanes] = 4.0 * (both[:8] + both[8:])
         return 0
 
     lax.fori_loop(0, slots // width, node_tile, 0)
-    for copy in copies:
-        copy.wait()
-    coef_ref[...] = moved(coefficients_of(me)[1], centre_table[...], True)[:3]
+    coef_ref[...] = moved(coefficients_of(me), centre_table[...], True)[:3]
     slot = lax.broadcasted_iota(jnp.int32, (3, slots), 1)
     shift_ref[...] = jnp.where(slot < count_ref[me], moved(result[...], node_table[...], True)[:3], 0.0)
 
 
-def near_body(tile_blocks, near_count, mine, other, mine_power, other_power, nodes, centre_table, node_table):
+def near_body(tiles, listed, near_count, low, high, mine, other, mine_power, other_power, sources, targets, centre_table, node_table):
     size = mine.shape[2]
-    slots = nodes.shape[1]
-    total = tile_blocks.shape[1] * size
+    slots = targets.shape[1]
+    total = listed * size
     return pl.pallas_call(
         near_kernel,
         out_shape=(
             jax.ShapeDtypeStruct((3, size), F32),
             jax.ShapeDtypeStruct((3, slots), F32),
         ),
-        in_specs=[SMEM, SMEM] + [VMEM] * 5 + [ANY, ANY],
+        in_specs=[SMEM] * 4 + [VMEM] * 8,
         out_specs=(VMEM, VMEM),
         scratch_shapes=[
-            pltpu.VMEM((total + 4 * CHUNK, 48), BF16),
-            pltpu.VMEM((48, slots), BF16),
-            pltpu.VMEM((16, total + 4 * CHUNK), BF16),
+            pltpu.VMEM((16, total + REACH * CHUNK), BF16),
             pltpu.VMEM((8, slots), F32),
-            pltpu.VMEM((size, size), BF16),
-            pltpu.VMEM((slots, slots), BF16),
-            pltpu.SemaphoreType.DMA((2,)),
-            pltpu.SMEM((slots // 256,), jnp.int32),
-            pltpu.SMEM((slots // 256,), jnp.int32),
         ],
         compiler_params=pltpu.CompilerParams(vmem_limit_bytes=SMALL_LIMIT),
         name="near_body",
-    )(tile_blocks.reshape(-1), near_count, mine, other, mine_power, other_power, nodes, centre_table, node_table)
+    )(tiles, near_count, low, high, mine, other, mine_power, other_power, sources, targets, centre_table, node_table)
 
 
 def gathered(values, count, partner):
@@ -602,15 +741,21 @@
     partner = [(i, i ^ 1) for i in range(count)]
     across = [(i, i + 1) for i in range(1, count - 1, 2)]
     across = across + [(j, i) for i, j in across]
-    send_a, send_b = edge_rows(flow_state, flow_speed)
+    chips, rows = count // 2, flow_state.shape[1]
+    send_a, send_b, state, speed = edge_rows(flow_state, flow_speed)
     from_a = lax.ppermute(send_a, SLAB, partner)
     from_b = lax.ppermute(send_b, SLAB, across)
     in_order, centre_table, nodes, node_table = ordered(base_shift, normals, centres, wall_cell, near_nodes)
-    new_flow, packed = flux_and_right_side(count // 2, flow_state, flow_speed, from_a, from_b, in_order)
+    new_flow, low, high, base, chosen = inner_flux(state, speed, in_order)
+    packed, low, high = right_side(chips, rows, send_a, send_b, from_a, from_b, low, high, base, chosen)
     mine, other = gathered(packed, count, partner)
-    mine_power, other_power = gathered(powers(mine, other, count), count, partner)
+    power, new_flow = powers(mine, other, low, high, new_flow, count)
+    mine_power, other_power = gathered(power, count, partner)
+    tiles, listed = tile_blocks.reshape(-1), tile_blocks.shape[1]
+    sources, targets, first, last = near_points(tiles, listed, mine, other, nodes)
     coefficients, node_shift = near_body(
-        tile_blocks, near_count, mine, other, mine_power, other_power, nodes, centre_table, node_table
+        tiles, listed, near_count, first, last, mine, other, mine_power, other_power, sources, targets,
+        centre_table, node_table,
     )
     return new_flow, coefficients, node_shift
 

time: 58.9 us -> 54.1 us (0.919)
  waiting for transfers between devices: 5.81 us -> 1.93 us
  Pallas kernels: 20.1 us -> 19.4 us
    ppermute x1, waiting for transfers between devices: 3.97 us -> 0.94 us  [shards(): from_b = lax.ppermute(send_b, SLAB, across)]
    ppermute x2, waiting for transfers between devices: 1.84 us -> 0.99 us  [gathered(): return (mine, lax.ppermute(mine, SLAB, partner))]
    pallas_call x3 -> x5, Pallas kernels: 11.5 us -> 11.4 us  [the longest x1 5.93 us: powers(): pl.pallas_call(functools.partial(powers_kernel, count), out_shape=(jax.Sh...]
    unnamed x21 -> x19, local copies, waits for them, and re-layouts: 2.46 us -> 2.46 us
  transfers between devices with their start and end apart: 4 -> 4, of which waited for: 3 -> 2; matrix products, arithmetic and copies ran while one was open for 0% -> 0% of each run, Pallas kernels for 4% -> 12%
where the time goes in v3:
time: 54.1 us; the launch traced here: 53.8 us
  blocking collectives  21 us (39%)
  Pallas kernels  19.4 us (36%)
  starting transfers between devices  8.04 us (15%)
  local copies, waits for them, and re-layouts  2.55 us (5%)
  waiting for transfers between devices  1.93 us (4%)
  between operations  0.79 us (1%)
    all_to_all x2, blocking collectives, gathered(): mine = lax.all_to_all(values, 'chip', 0, 0)  21 us
    pallas_call x1, Pallas kernels, near_body(): pl.pallas_call(near_kernel, out_shape=(jax.ShapeDtypeStruct((3, size), F3...  5.94 us
    pallas_call x1, Pallas kernels, powers(): pl.pallas_call(functools.partial(powers_kernel, count), out_shape=(jax.Sh...  5.93 us
    ppermute x1, starting transfers between devices, shards(): from_b = lax.ppermute(send_b, SLAB, across)  4.52 us
    ppermute x2, starting transfers between devices, gathered(): return (mine, lax.ppermute(mine, SLAB, partner))  3.43 us
    pallas_call x1, Pallas kernels, inner_flux(): pl.pallas_call(inner_kernel, out_shape=(jax.ShapeDtypeStruct(flow_state.s...  3.02 us
    unnamed x19, local copies, waits for them, and re-layouts  2.46 us
    pallas_call x1, Pallas kernels, ordered(): pl.pallas_call(order_kernel, out_shape=(jax.ShapeDtypeStruct((16, count),...  2.06 us
  transfers between devices with their start and end apart: 4, of which 2 were waited for; matrix products, arithmetic and copies ran while one was open for 0% of the time, Pallas kernels for 12%

profile of v3, /device:TPU:1, one launch (start us, length us, event | category | flops | bytes accessed | tf_op | source)
XLA Modules:
  0.0 53.8 jit_solution(14635930624117445865)
XLA Ops:
  0.6 0.0 copy-start
  0.6 1.3 %copy-done = f32[5,8,8192]{2,1,0:T(8,128)S(1)} copy-done((f32[5,8,8192]{2,1,0:T(8,128)S(1)}, f32[5,8,8192]{2,1,0:T(8,128)}, u32[]{:S(2)}) %copy-start) | copy-done | bytes 1310744
  1.9 0.0 copy-start.1
  2.0 1.0 %copy-done.1 = f32[2,8,8192]{2,1,0:T(8,128)S(1)} copy-done((f32[2,8,8192]{2,1,0:T(8,128)S(1)}, f32[2,8,8192]{2,1,0:T(8,128)}, u32[]{:S(2)}) %copy-start.1) | copy-done | bytes 524312
  3.0 0.0 copy-start.6
  3.0 0.3 edge_rows.1
  3.3 0.1 collective-permute-start
  3.4 4.5 %collective-permute-start.1 = (f32[6,8192]{1,0:T(8,128)S(1)}, f32[6,8192]{1,0:T(8,128)S(1)}, u32[]{:S(2)}, u32[]{:S(2)}) collective-permute-start(f32[6,8192]{1,0:T(8,128)S(1)} %get-tuple-element.28.send_b), channel_id=1, source_target_pairs={{1,2},{3,4},{5,6},{7,8},{9,10},{11,12},{13,14},{2,1},{4,3},{6,5},{... | collective-permute-start | bytes 589832 | tf_op jit(solution)/shard_map/ppermute | solution.py:747
  7.9 0.0 copy-done.2
  8.0 0.0 copy-done.3
  8.0 0.0 copy-done.4
  8.0 0.0 copy-done.5
  8.0 0.0 copy-done.6
  8.0 2.1 %order.1 = (f32[16,512]{1,0:T(8,128)S(1)}, bf16[512,512]{1,0:T(8,128)(2,1)S(1)}, f32[8,1024]{1,0:T(8,128)S(1)}, bf16[1024,1024]{1,0:T(8,128)(2,1)S(1)}) custom-call(f32[3,512]{1,0:T(4,128)S(1)} %copy-done.3, f32[3,512]{1,0:T(4,128)S(1)} %copy-done.4, f32[3,512]{1,0:T(4,128)S(1)} %copy-done.5, s32[1,512]{1,0:T(1,128)S(1)} %bitcast.1, f32[3,1024]{1,0:T(4,128)S(1)} %copy-done.2), custom_call_target="tpu_custom_call" | custom-call | flops 8000000 | bytes 4000000 | tf_op jit(solution)/shard_map/order/pallas_call | solution.py:145
  10.1 3.0 %inner_flux.1 = (f32[5,8,8192]{2,1,0:T(8,128)}, f32[5,8192]{1,0:T(8,128)S(1)}, f32[5,8192]{1,0:T(8,128)S(1)}, f32[16,512]{1,0:T(8,128)S(1)}, bf16[512,512]{1,0:T(8,128)(2,1)S(1)}) custom-call(f32[5,8,8192]{2,1,0:T(8,128)S(1)} %get-tuple-element.29.q_ref, f32[2,8,8192]{2,1,0:T(8,128)S(1)} %get-tuple-element.30.w_ref, f32[16,512]{1,0:T(8,128)S(1)} %get-tuple-element.31.sorted_ref), custom_call_target="tpu_custom_call" | custom-call | flops 20000000 | bytes 4000000 | tf_op jit(solution)/shard_map/inner_flux/pallas_call | solution.py:307
  13.1 0.0 collective-permute-done.from_a
  13.1 0.9 %collective-permute-done.1.from_b = f32[6,8192]{1,0:T(8,128)S(1)} collective-permute-done((f32[6,8192]{1,0:T(8,128)S(1)}, f32[6,8192]{1,0:T(8,128)S(1)}, u32[]{:S(2)}, u32[]{:S(2)}) %collective-permute-start.1) | collective-permute-done | bytes 196640 | tf_op jit(solution)/shard_map/ppermute | solution.py:747
  14.1 0.6 %outer_flux.1 = (f32[8,8,512]{2,1,0:T(8,128)S(1)}, f32[5,8192]{1,0:T(8,128)S(1)}, f32[5,8192]{1,0:T(8,128)S(1)}) custom-call(f32[6,8192]{1,0:T(8,128)S(1)} %get-tuple-element.27.send_a, f32[6,8192]{1,0:T(8,128)S(1)} %get-tuple-element.28.send_b, f32[6,8192]{1,0:T(8,128)S(1)} %collective-permute-done.from_a, f32[6,8192]{1,0:T(8,128)S(1)} %collective-permute-done.1.from_b, ...), custom_call_target="tpu_custom_call" | custom-call | tf_op jit(solution)/shard_map/outer_flux/pallas_call | solution.py:359
  14.7 0.0 copy-start.8
  14.7 12.1 %all_to_all.10.mine_ref = f32[8,8,512]{2,1,0:T(8,128)S(1)} all-to-all(f32[8,8,512]{2,1,0:T(8,128)S(1)} %get-tuple-element.36), channel_id=1, replica_groups=mesh['groups'=2,'chip'=8,'core'=2] {'chip'}, dimensions={0} | all-to-all | bytes 262144 | tf_op jit(solution)/shard_map/all_to_all | solution.py:725
  26.8 1.6 %collective-permute-start.2 = (f32[8,8,512]{2,1,0:T(8,128)S(1)}, f32[8,8,512]{2,1,0:T(8,128)S(1)}, u32[]{:S(2)}, u32[]{:S(2)}) collective-permute-start(f32[8,8,512]{2,1,0:T(8,128)S(1)} %all_to_all.10.mine_ref), channel_id=1, source_target_pairs={{0,1},{1,0},{2,3},{3,2},{4,5},{5,4},{6,7},{7,6},{8,9},{9,8},{10,11... | collective-permute-start | bytes 393224 | tf_op jit(solution)/shard_map/ppermute | solution.py:726
  28.4 1.0 %collective-permute-done.2.other_ref = f32[8,8,512]{2,1,0:T(8,128)S(1)} collective-permute-done((f32[8,8,512]{2,1,0:T(8,128)S(1)}, f32[8,8,512]{2,1,0:T(8,128)S(1)}, u32[]{:S(2)}, u32[]{:S(2)}) %collective-permute-start.2) | collective-permute-done | bytes 131104 | tf_op jit(solution)/shard_map/ppermute | solution.py:726
  29.3 5.9 %powers.1 = (f32[8,8,640]{2,1,0:T(8,128)S(1)}, f32[5,8,8192]{2,1,0:T(8,128)}) custom-call(f32[8,8,512]{2,1,0:T(8,128)S(1)} %all_to_all.10.mine_ref, f32[8,8,512]{2,1,0:T(8,128)S(1)} %collective-permute-done.2.other_ref, f32[5,8192]{1,0:T(8,128)S(1)} %get-tuple-element.37.new_low, ...), custom_call_target="tpu_custom_call", output_to_operand_aliasing={{1}: (4, {})} | custom-call | tf_op jit(solution)/shard_map/powers/pallas_call | solution.py:541
  35.3 9.0 %all_to_all.11.mine_power = f32[8,8,640]{2,1,0:T(8,128)S(1)} all-to-all(f32[8,8,640]{2,1,0:T(8,128)S(1)} %get-tuple-element.44), channel_id=1, replica_groups=mesh['groups'=2,'chip'=8,'core'=2] {'chip'}, dimensions={0} | all-to-all | bytes 327680 | tf_op jit(solution)/shard_map/all_to_all | solution.py:725
  44.3 1.9 %collective-permute-start.3 = (f32[8,8,640]{2,1,0:T(8,128)S(1)}, f32[8,8,640]{2,1,0:T(8,128)S(1)}, u32[]{:S(2)}, u32[]{:S(2)}) collective-permute-start(f32[8,8,640]{2,1,0:T(8,128)S(1)} %all_to_all.11.mine_power), channel_id=1, source_target_pairs={{0,1},{1,0},{2,3},{3,2},{4,5},{5,4},{6,7},{7,6},{8,9},{9,8},{10,11... | collective-permute-start | bytes 491528 | tf_op jit(solution)/shard_map/ppermute | solution.py:726
  46.1 0.0 copy-done.8
  46.1 0.1 copy.14
  46.2 0.1 reshape.13.tile_ref
  46.3 1.5 %near_points.1 = (bf16[2944,48]{1,0:T(8,128)(2,1)S(1)}, bf16[48,1024]{1,0:T(8,128)(2,1)S(1)}, s32[8]{0:T(128)S(1)}, s32[8]{0:T(128)S(1)}) custom-call(s32[64]{0:T(128)S(1)} %reshape.13.tile_ref, f32[8,8,512]{2,1,0:T(8,128)S(1)} %all_to_all.10.mine_ref, f32[8,8,512]{2,1,0:T(8,128)S(1)} %collective-permute-done.2.other_ref, ...), custom_call_target="tpu_custom_call" | custom-call | flops 1000000 | bytes 1000000 | tf_op jit(solution)/shard_map/near_points/pallas_call | solution.py:633
  47.8 0.0 collective-permute-done.3.other_power
  47.8 0.0 copy-done.7
  47.8 5.9 %near_body.1 = (f32[3,512]{1,0:T(4,128)}, f32[3,1024]{1,0:T(4,128)}) custom-call(s32[64]{0:T(128)S(1)} %reshape.13.tile_ref, s32[16]{0:T(128)S(1)} %copy-done.7, s32[8]{0:T(128)S(1)} %get-tuple-element.42.low_ref, s32[8]{0:T(128)S(1)} %get-tuple-element.43.high_ref, f32[8,8,512]{2,1,0:T(8,128)S(1)} %all_to_all.10.mine_ref, ...), custom_call_target="tpu_custom_call" | custom-call | tf_op jit(solution)/shard_map/near_body/pallas_call | solution.py:707
  (5 shorter events, 0.0 us)
Async XLA Ops:
  0.6 1.3 %copy-start = (f32[5,8,8192]{2,1,0:T(8,128)S(1)}, f32[5,8,8192]{2,1,0:T(8,128)}, u32[]{:S(2)}) copy-start(f32[5,8,8192]{2,1,0:T(8,128)} %q_hbm.1) | copy-start | bytes 3932164
  1.9 1.0 %copy-start.1 = (f32[2,8,8192]{2,1,0:T(8,128)S(1)}, f32[2,8,8192]{2,1,0:T(8,128)}, u32[]{:S(2)}) copy-start(f32[2,8,8192]{2,1,0:T(8,128)} %w_hbm.1) | copy-start | bytes 1572868
  3.0 5.0 %copy-start.2 = (f32[3,1024]{1,0:T(4,128)S(1)}, f32[3,1024]{1,0:T(4,128)}, u32[]{:S(2)}) copy-start(f32[3,1024]{1,0:T(4,128)} %nodes_ref.1) | copy-start | bytes 36868
  3.0 5.0 %copy-start.3 = (f32[3,512]{1,0:T(4,128)S(1)}, f32[3,512]{1,0:T(4,128)}, u32[]{:S(2)}) copy-start(f32[3,512]{1,0:T(4,128)} %base_ref.1) | copy-start | bytes 18436
  3.0 5.0 %copy-start.4 = (f32[3,512]{1,0:T(4,128)S(1)}, f32[3,512]{1,0:T(4,128)}, u32[]{:S(2)}) copy-start(f32[3,512]{1,0:T(4,128)} %normal_ref.1) | copy-start | bytes 18436
  3.0 5.0 %copy-start.5 = (f32[3,512]{1,0:T(4,128)S(1)}, f32[3,512]{1,0:T(4,128)}, u32[]{:S(2)}) copy-start(f32[3,512]{1,0:T(4,128)} %centre_ref.1) | copy-start | bytes 18436
  3.0 5.0 %copy-start.6 = (s32[512]{0:T(512)S(1)}, s32[512]{0:T(512)}, u32[]{:S(2)}) copy-start(s32[512]{0:T(512)} %param.11) | copy-start | bytes 6148
  3.3 9.8 %collective-permute-start = (f32[6,8192]{1,0:T(8,128)S(1)}, f32[6,8192]{1,0:T(8,128)S(1)}, u32[]{:S(2)}, u32[]{:S(2)}) collective-permute-start(f32[6,8192]{1,0:T(8,128)S(1)} %get-tuple-element.27.send_a), channel_id=1, source_target_pairs={{0,1},{1,0},{2,3},{3,2},{4,5},{5,4},{6,7},{7,6},{8,9},{9,8},{10,11... | collective-permute-start | bytes 589832 | tf_op jit(solution)/shard_map/ppermute | solution.py:746
  3.4 10.6 %collective-permute-start.1 = (f32[6,8192]{1,0:T(8,128)S(1)}, f32[6,8192]{1,0:T(8,128)S(1)}, u32[]{:S(2)}, u32[]{:S(2)}) collective-permute-start(f32[6,8192]{1,0:T(8,128)S(1)} %get-tuple-element.28.send_b), channel_id=1, source_target_pairs={{1,2},{3,4},{5,6},{7,8},{9,10},{11,12},{13,14},{2,1},{4,3},{6,5},{... | collective-permute-start | bytes 589832 | tf_op jit(solution)/shard_map/ppermute | solution.py:747
  14.7 31.4 %copy-start.8 = (s32[16,4]{0,1:T(4,128)S(1)}, s32[16,4]{0,1:T(4,128)}, u32[]{:S(2)}) copy-start(s32[16,4]{0,1:T(4,128)} %param.15) | copy-start | bytes 772
  26.8 2.6 %collective-permute-start.2 = (f32[8,8,512]{2,1,0:T(8,128)S(1)}, f32[8,8,512]{2,1,0:T(8,128)S(1)}, u32[]{:S(2)}, u32[]{:S(2)}) collective-permute-start(f32[8,8,512]{2,1,0:T(8,128)S(1)} %all_to_all.10.mine_ref), channel_id=1, source_target_pairs={{0,1},{1,0},{2,3},{3,2},{4,5},{5,4},{6,7},{7,6},{8,9},{9,8},{10,11... | collective-permute-start | bytes 393224 | tf_op jit(solution)/shard_map/ppermute | solution.py:726
  29.3 18.5 %copy-start.7 = (s32[16]{0:T(128)S(1)}, s32[16]{0:T(128)}, u32[]{:S(2)}) copy-start(s32[16]{0:T(128)} %count_ref.1) | copy-start | bytes 196
  44.3 3.6 %collective-permute-start.3 = (f32[8,8,640]{2,1,0:T(8,128)S(1)}, f32[8,8,640]{2,1,0:T(8,128)S(1)}, u32[]{:S(2)}, u32[]{:S(2)}) collective-permute-start(f32[8,8,640]{2,1,0:T(8,128)S(1)} %all_to_all.11.mine_power), channel_id=1, source_target_pairs={{0,1},{1,0},{2,3},{3,2},{4,5},{5,4},{6,7},{7,6},{8,9},{9,8},{10,11... | collective-permute-start | bytes 491528 | tf_op jit(solution)/shard_map/ppermute | solution.py:726

commit v4 on v3

--- a/solution.py
+++ b/solution.py
@@ -18,6 +18,7 @@
 MARGIN = 1e-3
 BIG_LIMIT = 48 * 1024 * 1024
 SMALL_LIMIT = 16 * 1024 * 1024
+FULL_LIMIT = 62 * 1024 * 1024 + 768 * 1024
 F32 = jnp.float32
 BF16 = jnp.bfloat16
 SLAB = ("chip", "core")
@@ -85,13 +86,18 @@
     return jnp.concatenate(result, axis=1)
 
 
-def moved(values, table, back):
+def moved(values, table):
     rows = values.shape[0]
     stacked = jnp.concatenate(parts(values), axis=0).astype(BF16)
     both = lax.dot_general(
-        stacked, table, (((1,), (0 if back else 1,)), ((), ())), preferred_element_type=F32
+        stacked, table, (((1,), (1,)), ((), ())), preferred_element_type=F32
     )
     return (both[:rows] + both[rows : 2 * rows]) + both[2 * rows :]
+
+
+def moved_back(values, table):
+    both = jnp.dot(doubled(values), table, preferred_element_type=F32)
+    return both[:3] + both[8:11]
 
 
 def chunk_bounds(source_z, target_z, width, low_ref, high_ref):
@@ -134,10 +140,10 @@
         ],
         axis=0,
     )
-    out_ref[...] = moved(values, centre_table[...], False)
+    out_ref[...] = moved(values, centre_table[...])
     table_of(node_table, rank_of(nodes_ref[2:3]))
     nodes = jnp.concatenate([nodes_ref[...], jnp.zeros((5, nodes_ref.shape[1]), F32)], axis=0)
-    nodes_out[...] = moved(nodes, node_table[...], False)
+    nodes_out[...] = moved(nodes, node_table[...])
 
 
 def ordered(base_shift, normals, centres, wall_cell, near_nodes):
@@ -158,23 +164,25 @@
     )(base_shift, normals, centres, wall_cell.reshape(1, -1), near_nodes)
 
 
-def edge_kernel(q_hbm, w_hbm, a_ref, b_ref, q_ref, w_ref, sems):
+def edge_kernel(q_ref, w_ref, a_ref, b_ref, sems):
     count, rows, _ = q_ref.shape
-    copies = [pltpu.make_async_copy(w_hbm.at[index], w_ref.at[index], sems.at[index]) for index in range(2)]
-    copies += [
-        pltpu.make_async_copy(q_hbm.at[index], q_ref.at[index], sems.at[2 + index]) for index in range(count)
-    ]
-    for copy in copies:
-        copy.start()
+
+    def move(row_a, row_b):
+        copies = []
+        for target, row in ((a_ref, row_a), (b_ref, row_b)):
+            for index in range(count + 1):
+                source = q_ref.at[index] if index < count else w_ref.at[0]
+                copies.append(
+                    pltpu.make_async_copy(
+                        source.at[pl.ds(row, 1)], target.at[pl.ds(index, 1)], sems.at[len(copies)]
+                    )
+                )
+        for copy in copies:
+            copy.start()
+        for copy in copies:
+            copy.wait()
+
     core = lax.axis_index("core")
-    for copy in copies:
-        copy.wait()
-
-    def move(row_a, row_b):
-        for target, row in ((a_ref, row_a), (b_ref, row_b)):
-            for index in range(count):
-                target[index : index + 1] = q_ref[index, row : row + 1]
-            target[count : count + 1] = w_ref[0, row : row + 1]
 
     @pl.when(core == 0)
     def _():
@@ -190,16 +198,11 @@
     rows = jax.ShapeDtypeStruct((count + 1, plane), F32)
     return pl.pallas_call(
         edge_kernel,
-        out_shape=(
-            rows,
-            rows,
-            jax.ShapeDtypeStruct(flow_state.shape, F32),
-            jax.ShapeDtypeStruct(flow_speed.shape, F32),
-        ),
+        out_shape=(rows, rows),
         in_specs=[HBM, HBM],
-        out_specs=(VMEM,) * 4,
-        scratch_shapes=[pltpu.SemaphoreType.DMA((count + 2,))],
-        compiler_params=pltpu.CompilerParams(vmem_limit_bytes=SMALL_LIMIT),
+        out_specs=(VMEM, VMEM),
+        scratch_shapes=[pltpu.SemaphoreType.DMA((2 * count + 2,))],
+        compiler_params=pltpu.CompilerParams(vmem_limit_bytes=FULL_LIMIT),
         name="edge_rows",
     )(flow_state, flow_speed)
 
@@ -480,15 +483,17 @@
     for slot in range(slots):
         hold(zeroth[slot], slot)
 
-    def tile_step(tile, _):
-        before = jnp.maximum(tile - 1, 0)
-        image[:, lanes_of(before)] = one(before, 0)
-        build(tile, 0)
+    def two_tiles(step, _):
+        before = jnp.maximum(2 * step - 2, 0)
+        for piece in range(2):
+            image[:, lanes_of(before + piece)] = one(before + piece, 0)
+        for piece in range(2):
+            build(2 * step + piece, 0)
         return 0
 
-    build(0, 0)
-    lax.fori_loop(1, tiles, tile_step, 0)
-    image[:, (tiles - 1) * width : tiles * width] = one(tiles - 1, 0)
+    lax.fori_loop(0, tiles // 2, two_tiles, 0)
+    for tile in range(tiles - 2, tiles):
+        image[:, tile * width : (tile + 1) * width] = one(tile, 0)
 
     @pl.when(most > 1)
     def _():
@@ -604,15 +609,42 @@
 REACH = 7
 
 
-def points_kernel(tile_ref, mine_ref, other_ref, nodes_ref, source_ref, target_ref, low_ref, high_ref):
+def bounds_of(source_z, target_z):
+    chunks = source_z.shape[1] // CHUNK
+    tiles = target_z.shape[1] // CHUNK
+
+    def edges(values, pieces):
+        rows = jnp.concatenate([values[:, i * CHUNK : (i + 1) * CHUNK] for i in range(pieces)], axis=0)
+        return jnp.min(rows, axis=1, keepdims=True), jnp.max(rows, axis=1, keepdims=True)
+
+    def across(values):
+        return jnp.broadcast_to(values, (tiles, 128)).T[0:1]
+
+    source_low, source_high = edges(source_z, chunks)
+    target_low, target_high = edges(target_z, tiles)
+    near = jnp.logical_and(
+        source_high >= across(target_low) - (1.0 + MARGIN), source_low <= across(target_high) + (1.0 + MARGIN)
+    )
+    index = lax.broadcasted_iota(jnp.int32, (chunks, tiles), 0).astype(F32)
+    low = jnp.min(jnp.where(near, index, float(chunks)), axis=0, keepdims=True)
+    high = jnp.max(jnp.where(near, index + 1.0, 0.0), axis=0, keepdims=True)
+    return jnp.concatenate([low, high], axis=0)
+
+
+def first_listed(tile_ref, me):
+    return tile_ref[pl.ds(me, 1), :][0, 0]
+
+
+def points_kernel(tile_ref, mine_ref, other_ref, nodes_ref, source_ref, target_ref, bound_ref):
     size = mine_ref.shape[2]
     core = lax.axis_index("core")
     me = lax.axis_index("chip") * 2 + core
-    listed = tile_ref.shape[0] // (2 * mine_ref.shape[0])
-    origin = lax.div((tile_ref[me * listed] + 2) * 2, 5).astype(F32)
+    listed = tile_ref.shape[1]
+    start = first_listed(tile_ref, me)
+    origin = lax.div((start + 2) * 2, 5).astype(F32)
     third = []
     for index in range(listed):
-        data = block_of(mine_ref, other_ref, tile_ref[me * listed + index], core)
+        data = block_of(mine_ref, other_ref, start + index, core)
         points = local_points(data[3:6], origin)
         third.append(points[2:3])
         source, _ = sides(points)
@@ -623,42 +655,52 @@
     points = local_points(nodes_ref[0:3], origin)
     _, target = sides(points)
     target_ref[...] = target.astype(BF16)
-    chunk_bounds(jnp.concatenate(third, axis=1), points[2:3], CHUNK, low_ref, high_ref)
-
-
-def near_points(tiles, listed, mine, other, nodes):
+    bound_ref[...] = bounds_of(jnp.concatenate(third, axis=1), points[2:3])
+
+
+def near_points(tile_blocks, mine, other, nodes):
     size = mine.shape[2]
     slots = nodes.shape[1]
-    bounds = jax.ShapeDtypeStruct((slots // CHUNK,), jnp.int32)
+    listed = tile_blocks.shape[1]
     return pl.pallas_call(
         points_kernel,
         out_shape=(
             jax.ShapeDtypeStruct((listed * size + REACH * CHUNK, 48), BF16),
             jax.ShapeDtypeStruct((48, slots), BF16),
-            bounds,
-            bounds,
+            jax.ShapeDtypeStruct((2, slots // CHUNK), F32),
         ),
-        in_specs=[SMEM] + [VMEM] * 3,
-        out_specs=(VMEM, VMEM, SMEM, SMEM),
+        in_specs=[VMEM] * 4,
+        out_specs=(VMEM,) * 3,
         compiler_params=pltpu.CompilerParams(vmem_limit_bytes=SMALL_LIMIT),
         cost_estimate=pl.CostEstimate(flops=1_000_000, bytes_accessed=1_000_000, transcendentals=0),
         name="near_points",
-    )(tiles, mine, other, nodes)
+    )(tile_blocks, mine, other, nodes)
 
 
 def near_kernel(
-    tile_ref, count_ref, low_ref, high_ref, mine_ref, other_ref, mine_power, other_power, source_side, target_side,
-    centre_table, node_table, coef_ref, shift_ref, vector, result,
+    tile_ref, count_ref, bound_ref, mine_ref, other_ref, mine_power, other_power, source_side, target_side,
+    centre_table, node_table, coef_ref, shift_ref, vector, result, low_ref, step_ref,
 ):
     size = mine_ref.shape[2]
     slots = target_side.shape[1]
     chips = mine_ref.shape[0]
     core = lax.axis_index("core")
     me = lax.axis_index("chip") * 2 + core
-    listed = tile_ref.shape[0] // count_ref.shape[0]
+    listed = tile_ref.shape[1]
+    start_block = first_listed(tile_ref, me)
     width = CHUNK
+    tiles = slots // width
     span = REACH * CHUNK
     total = listed * size
+
+    bounds = bound_ref[...].astype(jnp.int32)
+    most = 0
+    for tile in range(tiles):
+        low = bounds[0, tile]
+        steps = lax.div(bounds[1, tile] - low + (REACH - 1), REACH)
+        low_ref[tile] = low
+        step_ref[tile] = steps
+        most = jnp.maximum(most, steps)
 
     summed = mine_power[0, :, size:] + other_power[0, :, size:]
     for index in range(1, chips):
@@ -673,52 +715,69 @@
         return jnp.where(keep, values, 0.0)
 
     for index in range(listed):
-        values = coefficients_of(tile_ref[me * listed + index])
-        vector[:, index * size : (index + 1) * size] = doubled(values)
+        vector[:, index * size : (index + 1) * size] = doubled(coefficients_of(start_block + index))
     vector[:, total:] = jnp.zeros((16, span), BF16)
-
-    def node_tile(tile, _):
-        lanes = pl.ds(pl.multiple_of(tile * width, width), width)
-        targets = target_side[:, lanes]
-
-        def one(step, old):
-            start = pl.multiple_of((low_ref[tile] + step * REACH) * CHUNK, CHUNK)
-            table = quarter_kernel(source_side[pl.ds(start, span)], targets)
-            window = vector[:, pl.ds(start, span)]
-            return old + jnp.dot(
-                jnp.concatenate([window, window], axis=1), doubled(table), preferred_element_type=F32
-            )
-
-        steps = lax.div(high_ref[tile] - low_ref[tile] + (REACH - 1), REACH)
-        both = lax.fori_loop(0, steps, one, jnp.zeros((16, width), F32))
-        result[:, lanes] = 4.0 * (both[:8] + both[8:])
+    coef_ref[...] = moved_back(coefficients_of(me), centre_table[...])
+
+    def lanes_of(tile):
+        return pl.ds(pl.multiple_of(tile * width, width), width)
+
+    def one(tile, step):
+        start = pl.multiple_of((low_ref[tile] + step * REACH) * CHUNK, CHUNK)
+        table = quarter_kernel(source_side[pl.ds(start, span)], target_side[:, lanes_of(tile)])
+        window = vector[:, pl.ds(start, span)]
+        return jnp.dot(jnp.concatenate([window, window], axis=1), doubled(table), preferred_element_type=F32)
+
+    def two_tiles(step, _):
+        for piece in range(2):
+            result[:, lanes_of(2 * step + piece)] = one(2 * step + piece, 0)
         return 0
 
-    lax.fori_loop(0, slots // width, node_tile, 0)
-    coef_ref[...] = moved(coefficients_of(me), centre_table[...], True)[:3]
-    slot = lax.broadcasted_iota(jnp.int32, (3, slots), 1)
-    shift_ref[...] = jnp.where(slot < count_ref[me], moved(result[...], node_table[...], True)[:3], 0.0)
-
-
-def near_body(tiles, listed, near_count, low, high, mine, other, mine_power, other_power, sources, targets, centre_table, node_table):
+    lax.fori_loop(0, tiles // 2, two_tiles, 0)
+
+    @pl.when(most > 1)
+    def _():
+        def of_tile(tile, _):
+            def add(step, _):
+                result[:, lanes_of(tile)] += one(tile, step)
+                return 0
+
+            return lax.fori_loop(1, step_ref[tile], add, 0)
+
+        lax.fori_loop(0, tiles, of_tile, 0)
+
+    lane = lax.broadcasted_iota(jnp.int32, count_ref.shape, 1)
+    live = jnp.sum(jnp.where(lane == me, count_ref[...], 0).astype(F32), axis=1, keepdims=True)
+    slot = lax.broadcasted_iota(jnp.int32, (3, slots), 1).astype(F32)
+    both = result[...]
+    shift = moved_back(4.0 * (both[:8] + both[8:]), node_table[...])
+    shift_ref[...] = jnp.where(slot < live, shift, 0.0)
+
+
+def near_body(tile_blocks, near_count, bounds, mine, other, mine_power, other_power, sources, targets, centre_table, node_table):
     size = mine.shape[2]
     slots = targets.shape[1]
-    total = listed * size
+    total = tile_blocks.shape[1] * size
     return pl.pallas_call(
         near_kernel,
         out_shape=(
             jax.ShapeDtypeStruct((3, size), F32),
             jax.ShapeDtypeStruct((3, slots), F32),
         ),
-        in_specs=[SMEM] * 4 + [VMEM] * 8,
+        in_specs=[VMEM] * 11,
         out_specs=(VMEM, VMEM),
         scratch_shapes=[
             pltpu.VMEM((16, total + REACH * CHUNK), BF16),
-            pltpu.VMEM((8, slots), F32),
+            pltpu.VMEM((16, slots), F32),
+            pltpu.SMEM((slots // CHUNK,), jnp.int32),
+            pltpu.SMEM((slots // CHUNK,), jnp.int32),
         ],
         compiler_params=pltpu.CompilerParams(vmem_limit_bytes=SMALL_LIMIT),
         name="near_body",
-    )(tiles, near_count, low, high, mine, other, mine_power, other_power, sources, targets, centre_table, node_table)
+    )(
+        tile_blocks, near_count.reshape(1, -1), bounds, mine, other, mine_power, other_power, sources, targets,
+        centre_table, node_table,
+    )
 
 
 def gathered(values, count, partner):
@@ -742,19 +801,18 @@
     across = [(i, i + 1) for i in range(1, count - 1, 2)]
     across = across + [(j, i) for i, j in across]
     chips, rows = count // 2, flow_state.shape[1]
-    send_a, send_b, state, speed = edge_rows(flow_state, flow_speed)
+    send_a, send_b = edge_rows(flow_state, flow_speed)
+    from_b = lax.ppermute(send_b, SLAB, across)
     from_a = lax.ppermute(send_a, SLAB, partner)
-    from_b = lax.ppermute(send_b, SLAB, across)
     in_order, centre_table, nodes, node_table = ordered(base_shift, normals, centres, wall_cell, near_nodes)
-    new_flow, low, high, base, chosen = inner_flux(state, speed, in_order)
+    new_flow, low, high, base, chosen = inner_flux(flow_state, flow_speed, in_order)
     packed, low, high = right_side(chips, rows, send_a, send_b, from_a, from_b, low, high, base, chosen)
     mine, other = gathered(packed, count, partner)
     power, new_flow = powers(mine, other, low, high, new_flow, count)
     mine_power, other_power = gathered(power, count, partner)
-    tiles, listed = tile_blocks.reshape(-1), tile_blocks.shape[1]
-    sources, targets, first, last = near_points(tiles, listed, mine, other, nodes)
+    sources, targets, bounds = near_points(tile_blocks, mine, other, nodes)
     coefficients, node_shift = near_body(
-        tiles, listed, near_count, first, last, mine, other, mine_power, other_power, sources, targets,
+        tile_blocks, near_count, bounds, mine, other, mine_power, other_power, sources, targets,
         centre_table, node_table,
     )
     return new_flow, coefficients, node_shift

time: 54.1 us -> 52.1 us (0.963)
  local copies, waits for them, and re-layouts: 2.55 us -> 1.44 us
  Pallas kernels: 19.4 us -> 18.7 us
    pallas_call x1, Pallas kernels: 5.94 us -> 4.15 us  [near_body(): pl.pallas_call(near_kernel, out_shape=(jax.ShapeDtypeStruct((3, size), F3...]
    pallas_call x1, Pallas kernels: 0.32 us -> 1.92 us  [edge_rows(): pl.pallas_call(edge_kernel, out_shape=(rows, rows), in_specs=[HBM, HBM],...]
    pallas_call x1, Pallas kernels: 1.51 us -> 0.36 us  [near_points(): pl.pallas_call(points_kernel, out_shape=(jax.ShapeDtypeStruct((listed * s...]
    unnamed x19 -> x23, local copies, waits for them, and re-layouts: 2.46 us -> 1.44 us
    ppermute x1, waiting for transfers between devices: 0.94 us -> 0.01 us  [shards(): from_b = lax.ppermute(send_b, SLAB, across)]
    pallas_call x1, Pallas kernels: 5.93 us -> 6.59 us  [powers(): pl.pallas_call(functools.partial(powers_kernel, count), out_shape=(jax.Sh...]
    ppermute x2, waiting for transfers between devices: 0.99 us -> 1.56 us  [gathered(): return (mine, lax.ppermute(mine, SLAB, partner))]
  transfers between devices with their start and end apart: 4 -> 4, of which waited for: 2 -> 2; matrix products, arithmetic and copies ran while one was open for 0% -> 0% of each run, Pallas kernels for 12% -> 11%
where the time goes in v4:
time: 52.1 us; the launch traced here: 51.4 us
  blocking collectives  20.8 us (40%)
  Pallas kernels  18.7 us (36%)
  starting transfers between devices  8.03 us (15%)
  waiting for transfers between devices  1.57 us (3%)
  local copies, waits for them, and re-layouts  1.44 us (3%)
  between operations  0.84 us (2%)
    all_to_all x2, blocking collectives, gathered(): mine = lax.all_to_all(values, 'chip', 0, 0)  20.8 us
    pallas_call x1, Pallas kernels, powers(): pl.pallas_call(functools.partial(powers_kernel, count), out_shape=(jax.Sh...  6.59 us
    ppermute x1, starting transfers between devices, shards(): from_b = lax.ppermute(send_b, SLAB, across)  4.52 us
    pallas_call x1, Pallas kernels, near_body(): pl.pallas_call(near_kernel, out_shape=(jax.ShapeDtypeStruct((3, size), F3...  4.15 us
    ppermute x2, starting transfers between devices, gathered(): return (mine, lax.ppermute(mine, SLAB, partner))  3.43 us
    pallas_call x1, Pallas kernels, inner_flux(): pl.pallas_call(inner_kernel, out_shape=(jax.ShapeDtypeStruct(flow_state.s...  3.01 us
    pallas_call x1, Pallas kernels, ordered(): pl.pallas_call(order_kernel, out_shape=(jax.ShapeDtypeStruct((16, count),...  2.06 us
    pallas_call x1, Pallas kernels, edge_rows(): pl.pallas_call(edge_kernel, out_shape=(rows, rows), in_specs=[HBM, HBM],...  1.92 us
  transfers between devices with their start and end apart: 4, of which 2 were waited for; matrix products, arithmetic and copies ran while one was open for 0% of the time, Pallas kernels for 11%

profile of v4, /device:TPU:1, one launch (start us, length us, event | category | flops | bytes accessed | tf_op | source)
XLA Modules:
  0.0 51.4 jit_solution(424107583940295235)
XLA Ops:
  0.6 0.0 copy-start.1
  0.6 0.0 copy-start.5
  0.7 0.0 copy-start.6
  0.7 0.0 copy-start.7
  0.7 0.0 copy-start.8
  0.7 1.9 %edge_rows.1 = (f32[6,8192]{1,0:T(8,128)}, f32[6,8192]{1,0:T(8,128)}) custom-call(f32[5,8,8192]{2,1,0:T(8,128)} %q_ref.3, f32[2,8,8192]{2,1,0:T(8,128)} %w_ref.3), custom_call_target="tpu_custom_call" | custom-call | tf_op jit(solution)/shard_map/edge_rows/pallas_call | solution.py:199
  2.6 0.1 collective-permute-start
  2.7 4.5 %collective-permute-start.1 = (f32[6,8192]{1,0:T(8,128)}, f32[6,8192]{1,0:T(8,128)S(1)}, u32[]{:S(2)}, u32[]{:S(2)}) collective-permute-start(f32[6,8192]{1,0:T(8,128)} %get-tuple-element.25.send_b), channel_id=1, source_target_pairs={{1,2},{3,4},{5,6},{7,8},{9,10},{11,12},{13,14},{2,1},{4,3},{6,5},{... | collective-permute-start | bytes 589832 | tf_op jit(solution)/shard_map/ppermute | solution.py:805
  7.2 0.0 copy-done.5
  7.2 0.0 copy-done.6
  7.3 0.0 copy-done.7
  7.3 0.0 copy-done.8
  7.3 0.0 copy-done.4
  7.3 2.1 %order.1 = (f32[16,512]{1,0:T(8,128)S(1)}, bf16[512,512]{1,0:T(8,128)(2,1)S(1)}, f32[8,1024]{1,0:T(8,128)S(1)}, bf16[1024,1024]{1,0:T(8,128)(2,1)S(1)}) custom-call(f32[3,512]{1,0:T(4,128)S(1)} %copy-done.5, f32[3,512]{1,0:T(4,128)S(1)} %copy-done.6, f32[3,512]{1,0:T(4,128)S(1)} %copy-done.7, s32[1,512]{1,0:T(1,128)S(1)} %bitcast.2, f32[3,1024]{1,0:T(4,128)S(1)} %copy-done.4), custom_call_target="tpu_custom_call" | custom-call | flops 8000000 | bytes 4000000 | tf_op jit(solution)/shard_map/order/pallas_call | solution.py:151
  9.4 0.0 copy-done.1
  9.4 0.0 copy-start
  9.4 1.3 %copy-done = f32[5,8,8192]{2,1,0:T(8,128)S(1)} copy-done((f32[5,8,8192]{2,1,0:T(8,128)S(1)}, f32[5,8,8192]{2,1,0:T(8,128)}, u32[]{:S(2)}) %copy-start) | copy-done | bytes 1310744
  10.7 3.0 %inner_flux.1 = (f32[5,8,8192]{2,1,0:T(8,128)}, f32[5,8192]{1,0:T(8,128)S(1)}, f32[5,8192]{1,0:T(8,128)S(1)}, f32[16,512]{1,0:T(8,128)S(1)}, bf16[512,512]{1,0:T(8,128)(2,1)S(1)}) custom-call(f32[5,8,8192]{2,1,0:T(8,128)S(1)} %copy-done, f32[2,8,8192]{2,1,0:T(8,128)S(1)} %copy-done.1, f32[16,512]{1,0:T(8,128)S(1)} %get-tuple-element.26.sorted_ref), custom_call_target="tpu_custom_call" | custom-call | flops 20000000 | bytes 4000000 | tf_op jit(solution)/shard_map/inner_flux/pallas_call | solution.py:310
  13.7 0.0 collective-permute-done.from_a
  13.7 0.0 collective-permute-done.1.from_b
  13.8 0.6 %outer_flux.1 = (f32[8,8,512]{2,1,0:T(8,128)S(1)}, f32[5,8192]{1,0:T(8,128)S(1)}, f32[5,8192]{1,0:T(8,128)S(1)}) custom-call(f32[6,8192]{1,0:T(8,128)S(1)} %copy-done.2, f32[6,8192]{1,0:T(8,128)S(1)} %copy-done.3, f32[6,8192]{1,0:T(8,128)S(1)} %collective-permute-done.from_a, f32[6,8192]{1,0:T(8,128)S(1)} %collective-permute-done.1.from_b, ...), custom_call_target="tpu_custom_call" | custom-call | tf_op jit(solution)/shard_map/outer_flux/pallas_call | solution.py:362
  14.4 0.0 copy-start.10
  14.4 11.9 %all_to_all.10.mine_ref = f32[8,8,512]{2,1,0:T(8,128)S(1)} all-to-all(f32[8,8,512]{2,1,0:T(8,128)S(1)} %get-tuple-element.31), channel_id=1, replica_groups=mesh['groups'=2,'chip'=8,'core'=2] {'chip'}, dimensions={0} | all-to-all | bytes 262144 | tf_op jit(solution)/shard_map/all_to_all | solution.py:784
  26.3 1.6 %collective-permute-start.2 = (f32[8,8,512]{2,1,0:T(8,128)S(1)}, f32[8,8,512]{2,1,0:T(8,128)S(1)}, u32[]{:S(2)}, u32[]{:S(2)}) collective-permute-start(f32[8,8,512]{2,1,0:T(8,128)S(1)} %all_to_all.10.mine_ref), channel_id=1, source_target_pairs={{0,1},{1,0},{2,3},{3,2},{4,5},{5,4},{6,7},{7,6},{8,9},{9,8},{10,11... | collective-permute-start | bytes 393224 | tf_op jit(solution)/shard_map/ppermute | solution.py:785
  27.9 1.0 %collective-permute-done.2.other_ref = f32[8,8,512]{2,1,0:T(8,128)S(1)} collective-permute-done((f32[8,8,512]{2,1,0:T(8,128)S(1)}, f32[8,8,512]{2,1,0:T(8,128)S(1)}, u32[]{:S(2)}, u32[]{:S(2)}) %collective-permute-start.2) | collective-permute-done | bytes 131104 | tf_op jit(solution)/shard_map/ppermute | solution.py:785
  28.8 6.6 %powers.1 = (f32[8,8,640]{2,1,0:T(8,128)S(1)}, f32[5,8,8192]{2,1,0:T(8,128)}) custom-call(f32[8,8,512]{2,1,0:T(8,128)S(1)} %all_to_all.10.mine_ref, f32[8,8,512]{2,1,0:T(8,128)S(1)} %collective-permute-done.2.other_ref, f32[5,8192]{1,0:T(8,128)S(1)} %get-tuple-element.32.new_low, ...), custom_call_target="tpu_custom_call", output_to_operand_aliasing={{1}: (4, {})} | custom-call | tf_op jit(solution)/shard_map/powers/pallas_call | solution.py:546
  35.4 9.0 %all_to_all.11.mine_power = f32[8,8,640]{2,1,0:T(8,128)S(1)} all-to-all(f32[8,8,640]{2,1,0:T(8,128)S(1)} %get-tuple-element.38), channel_id=1, replica_groups=mesh['groups'=2,'chip'=8,'core'=2] {'chip'}, dimensions={0} | all-to-all | bytes 327680 | tf_op jit(solution)/shard_map/all_to_all | solution.py:784
  44.4 1.9 %collective-permute-start.3 = (f32[8,8,640]{2,1,0:T(8,128)S(1)}, f32[8,8,640]{2,1,0:T(8,128)S(1)}, u32[]{:S(2)}, u32[]{:S(2)}) collective-permute-start(f32[8,8,640]{2,1,0:T(8,128)S(1)} %all_to_all.11.mine_power), channel_id=1, source_target_pairs={{0,1},{1,0},{2,3},{3,2},{4,5},{5,4},{6,7},{7,6},{8,9},{9,8},{10,11... | collective-permute-start | bytes 491528 | tf_op jit(solution)/shard_map/ppermute | solution.py:785
  46.3 0.1 copy.14.tile_ref
  46.3 0.4 near_points.1
  46.7 0.6 %collective-permute-done.3.other_power = f32[8,8,640]{2,1,0:T(8,128)S(1)} collective-permute-done((f32[8,8,640]{2,1,0:T(8,128)S(1)}, f32[8,8,640]{2,1,0:T(8,128)S(1)}, u32[]{:S(2)}, u32[]{:S(2)}) %collective-permute-start.3) | collective-permute-done | bytes 163872 | tf_op jit(solution)/shard_map/ppermute | solution.py:785
  47.3 4.2 %near_body.1 = (f32[3,512]{1,0:T(4,128)}, f32[3,1024]{1,0:T(4,128)}) custom-call(s32[16,4]{1,0:T(8,128)S(1)} %copy.14.tile_ref, s32[1,16]{1,0:T(1,128)S(1)} %bitcast.3, f32[2,8]{1,0:T(2,128)S(1)} %get-tuple-element.37.bound_ref, f32[8,8,512]{2,1,0:T(8,128)S(1)} %all_to_all.10.mine_ref, f32[8,8,512]{2,1,0:T(8,128)S(1)} %collective-permute-done.2.other_ref, ...), custom_call_target="tpu_custom_call" | custom-call | tf_op jit(solution)/shard_map/near_body/pallas_call | solution.py:761
  (8 shorter events, 0.0 us)
Async XLA Ops:
  0.6 8.7 %copy-start.1 = (f32[2,8,8192]{2,1,0:T(8,128)S(1)}, f32[2,8,8192]{2,1,0:T(8,128)}, u32[]{:S(2)}) copy-start(f32[2,8,8192]{2,1,0:T(8,128)} %w_ref.3) | copy-start | bytes 1572868
  0.6 6.6 %copy-start.5 = (f32[3,512]{1,0:T(4,128)S(1)}, f32[3,512]{1,0:T(4,128)}, u32[]{:S(2)}) copy-start(f32[3,512]{1,0:T(4,128)} %base_ref.1) | copy-start | bytes 18436
  0.7 6.6 %copy-start.6 = (f32[3,512]{1,0:T(4,128)S(1)}, f32[3,512]{1,0:T(4,128)}, u32[]{:S(2)}) copy-start(f32[3,512]{1,0:T(4,128)} %normal_ref.1) | copy-start | bytes 18436
  0.7 6.6 %copy-start.7 = (f32[3,512]{1,0:T(4,128)S(1)}, f32[3,512]{1,0:T(4,128)}, u32[]{:S(2)}) copy-start(f32[3,512]{1,0:T(4,128)} %centre_ref.1) | copy-start | bytes 18436
  0.7 6.6 %copy-start.8 = (s32[512]{0:T(512)S(1)}, s32[512]{0:T(512)}, u32[]{:S(2)}) copy-start(s32[512]{0:T(512)} %param.11) | copy-start | bytes 6148
  0.7 6.6 %copy-start.4 = (f32[3,1024]{1,0:T(4,128)S(1)}, f32[3,1024]{1,0:T(4,128)}, u32[]{:S(2)}) copy-start(f32[3,1024]{1,0:T(4,128)} %nodes_ref.1) | copy-start | bytes 36868
  2.6 11.1 %collective-permute-start = (f32[6,8192]{1,0:T(8,128)}, f32[6,8192]{1,0:T(8,128)S(1)}, u32[]{:S(2)}, u32[]{:S(2)}) collective-permute-start(f32[6,8192]{1,0:T(8,128)} %get-tuple-element.24.send_a), channel_id=1, source_target_pairs={{0,1},{1,0},{2,3},{3,2},{4,5},{5,4},{6,7},{7,6},{8,9},{9,8},{10,11... | collective-permute-start | bytes 589832 | tf_op jit(solution)/shard_map/ppermute | solution.py:806
  2.7 11.0 %collective-permute-start.1 = (f32[6,8192]{1,0:T(8,128)}, f32[6,8192]{1,0:T(8,128)S(1)}, u32[]{:S(2)}, u32[]{:S(2)}) collective-permute-start(f32[6,8192]{1,0:T(8,128)} %get-tuple-element.25.send_b), channel_id=1, source_target_pairs={{1,2},{3,4},{5,6},{7,8},{9,10},{11,12},{13,14},{2,1},{4,3},{6,5},{... | collective-permute-start | bytes 589832 | tf_op jit(solution)/shard_map/ppermute | solution.py:805
  9.4 1.3 %copy-start = (f32[5,8,8192]{2,1,0:T(8,128)S(1)}, f32[5,8,8192]{2,1,0:T(8,128)}, u32[]{:S(2)}) copy-start(f32[5,8,8192]{2,1,0:T(8,128)} %q_ref.3) | copy-start | bytes 3932164
  10.7 3.0 %copy-start.2 = (f32[6,8192]{1,0:T(8,128)S(1)}, f32[6,8192]{1,0:T(8,128)}, u32[]{:S(2)}) copy-start(f32[6,8192]{1,0:T(8,128)} %get-tuple-element.24.send_a) | copy-start | bytes 589828
  10.7 3.1 %copy-start.3 = (f32[6,8192]{1,0:T(8,128)S(1)}, f32[6,8192]{1,0:T(8,128)}, u32[]{:S(2)}) copy-start(f32[6,8192]{1,0:T(8,128)} %get-tuple-element.25.send_b) | copy-start | bytes 589828
  14.4 31.9 %copy-start.10 = (s32[16,4]{0,1:T(4,128)S(1)}, s32[16,4]{0,1:T(4,128)}, u32[]{:S(2)}) copy-start(s32[16,4]{0,1:T(4,128)} %param.15) | copy-start | bytes 772
  26.3 2.6 %collective-permute-start.2 = (f32[8,8,512]{2,1,0:T(8,128)S(1)}, f32[8,8,512]{2,1,0:T(8,128)S(1)}, u32[]{:S(2)}, u32[]{:S(2)}) collective-permute-start(f32[8,8,512]{2,1,0:T(8,128)S(1)} %all_to_all.10.mine_ref), channel_id=1, source_target_pairs={{0,1},{1,0},{2,3},{3,2},{4,5},{5,4},{6,7},{7,6},{8,9},{9,8},{10,11... | collective-permute-start | bytes 393224 | tf_op jit(solution)/shard_map/ppermute | solution.py:785
  28.8 18.4 %copy-start.9 = (s32[16]{0:T(128)S(1)}, s32[16]{0:T(128)}, u32[]{:S(2)}) copy-start(s32[16]{0:T(128)} %param.16) | copy-start | bytes 196
  44.4 2.9 %collective-permute-start.3 = (f32[8,8,640]{2,1,0:T(8,128)S(1)}, f32[8,8,640]{2,1,0:T(8,128)S(1)}, u32[]{:S(2)}, u32[]{:S(2)}) collective-permute-start(f32[8,8,640]{2,1,0:T(8,128)S(1)} %all_to_all.11.mine_power), channel_id=1, source_target_pairs={{0,1},{1,0},{2,3},{3,2},{4,5},{5,4},{6,7},{7,6},{8,9},{9,8},{10,11... | collective-permute-start | bytes 491528 | tf_op jit(solution)/shard_map/ppermute | solution.py:785

commit v5 on v4

--- a/solution.py
+++ b/solution.py
@@ -7,6 +7,7 @@
 from jax.experimental.pallas import tpu as pltpu
 from jax.sharding import Mesh
 from jax.sharding import PartitionSpec as P
+
 
 FLUX_STEP = 0.2
 SUPPORT = 0.15
@@ -16,6 +17,7 @@
 DEPTH = 0.4
 CHUNK = 128
 MARGIN = 1e-3
+ORDER_FLOPS = 2_000_000_000
 BIG_LIMIT = 48 * 1024 * 1024
 SMALL_LIMIT = 16 * 1024 * 1024
 FULL_LIMIT = 62 * 1024 * 1024 + 768 * 1024
@@ -159,24 +161,22 @@
         in_specs=[VMEM] * 5,
         out_specs=(VMEM,) * 4,
         compiler_params=pltpu.CompilerParams(vmem_limit_bytes=SMALL_LIMIT),
-        cost_estimate=pl.CostEstimate(flops=8_000_000, bytes_accessed=4_000_000, transcendentals=0),
+        cost_estimate=pl.CostEstimate(flops=ORDER_FLOPS, bytes_accessed=4_000_000, transcendentals=0),
         name="order",
     )(base_shift, normals, centres, wall_cell.reshape(1, -1), near_nodes)
 
 
-def edge_kernel(q_ref, w_ref, a_ref, b_ref, sems):
+def edge_kernel(even_last, q_ref, w_ref, *rest):
+    target, sems = rest[-2:]
     count, rows, _ = q_ref.shape
 
-    def move(row_a, row_b):
+    def move(row):
         copies = []
-        for target, row in ((a_ref, row_a), (b_ref, row_b)):
-            for index in range(count + 1):
-                source = q_ref.at[index] if index < count else w_ref.at[0]
-                copies.append(
-                    pltpu.make_async_copy(
-                        source.at[pl.ds(row, 1)], target.at[pl.ds(index, 1)], sems.at[len(copies)]
-                    )
-                )
+        for index in range(count + 1):
+            source = q_ref.at[index] if index < count else w_ref.at[0]
+            copies.append(
+                pltpu.make_async_copy(source.at[pl.ds(row, 1)], target.at[pl.ds(index, 1)], sems.at[index])
+            )
         for copy in copies:
             copy.start()
         for copy in copies:
@@ -186,25 +186,24 @@
 
     @pl.when(core == 0)
     def _():
-        move(rows - 1, 0)
+        move(rows - 1 if even_last else 0)
 
     @pl.when(core != 0)
     def _():
-        move(0, rows - 1)
-
-
-def edge_rows(flow_state, flow_speed):
+        move(0 if even_last else rows - 1)
+
+
+def edge_rows(even_last, flow_state, flow_speed, *after):
     count, _, plane = flow_state.shape
-    rows = jax.ShapeDtypeStruct((count + 1, plane), F32)
     return pl.pallas_call(
-        edge_kernel,
-        out_shape=(rows, rows),
-        in_specs=[HBM, HBM],
-        out_specs=(VMEM, VMEM),
-        scratch_shapes=[pltpu.SemaphoreType.DMA((2 * count + 2,))],
+        functools.partial(edge_kernel, even_last),
+        out_shape=jax.ShapeDtypeStruct((count + 1, plane), F32),
+        in_specs=[HBM, HBM] + [HBM] * len(after),
+        out_specs=VMEM,
+        scratch_shapes=[pltpu.SemaphoreType.DMA((count + 1,))],
         compiler_params=pltpu.CompilerParams(vmem_limit_bytes=FULL_LIMIT),
         name="edge_rows",
-    )(flow_state, flow_speed)
+    )(flow_state, flow_speed, *after)
 
 
 RATE = 0.5 * FLUX_STEP
@@ -483,17 +482,14 @@
     for slot in range(slots):
         hold(zeroth[slot], slot)
 
-    def two_tiles(step, _):
-        before = jnp.maximum(2 * step - 2, 0)
-        for piece in range(2):
-            image[:, lanes_of(before + piece)] = one(before + piece, 0)
-        for piece in range(2):
-            build(2 * step + piece, 0)
+    def tile_step(tile, _):
+        before = jnp.maximum(tile - 1, 0)
+        image[:, lanes_of(before)] = one(before, 0)
+        build(tile, 0)
         return 0
 
-    lax.fori_loop(0, tiles // 2, two_tiles, 0)
-    for tile in range(tiles - 2, tiles):
-        image[:, tile * width : (tile + 1) * width] = one(tile, 0)
+    lax.fori_loop(0, tiles, tile_step, 0)
+    image[:, (tiles - 1) * width : tiles * width] = one(tiles - 1, 0)
 
     @pl.when(most > 1)
     def _():
@@ -780,7 +776,7 @@
     )
 
 
-def gathered(values, count, partner):
+def gathered(values, partner):
     mine = lax.all_to_all(values, "chip", 0, 0)
     return mine, lax.ppermute(mine, SLAB, partner)
 
@@ -801,15 +797,16 @@
     across = [(i, i + 1) for i in range(1, count - 1, 2)]
     across = across + [(j, i) for i, j in across]
     chips, rows = count // 2, flow_state.shape[1]
-    send_a, send_b = edge_rows(flow_state, flow_speed)
+    send_b = edge_rows(False, flow_state, flow_speed)
     from_b = lax.ppermute(send_b, SLAB, across)
+    send_a = edge_rows(True, flow_state, flow_speed, send_b)
     from_a = lax.ppermute(send_a, SLAB, partner)
     in_order, centre_table, nodes, node_table = ordered(base_shift, normals, centres, wall_cell, near_nodes)
     new_flow, low, high, base, chosen = inner_flux(flow_state, flow_speed, in_order)
     packed, low, high = right_side(chips, rows, send_a, send_b, from_a, from_b, low, high, base, chosen)
-    mine, other = gathered(packed, count, partner)
+    mine, other = gathered(packed, partner)
     power, new_flow = powers(mine, other, low, high, new_flow, count)
-    mine_power, other_power = gathered(power, count, partner)
+    mine_power, other_power = gathered(power, partner)
     sources, targets, bounds = near_points(tile_blocks, mine, other, nodes)
     coefficients, node_shift = near_body(
         tile_blocks, near_count, bounds, mine, other, mine_power, other_power, sources, targets,

time: 52.1 us -> 52.6 us (level)
  local copies, waits for them, and re-layouts: 1.44 us -> 0.15 us
  waiting for transfers between devices: 1.57 us -> 2.46 us
  Pallas kernels: 18.7 us -> 19.5 us
    pallas_call x1 -> x2, Pallas kernels: 1.92 us -> 3.29 us  [edge_rows(): pl.pallas_call(functools.partial(edge_kernel, even_last), out_shape=jax.S...]
    unnamed x23, local copies, waits for them, and re-layouts: 1.44 us -> 0.15 us
    ppermute x1, waiting for transfers between devices: 0.01 us -> 0.89 us  [shards(): from_b = lax.ppermute(send_b, SLAB, across)]
    pallas_call x1, Pallas kernels: 6.59 us -> 5.97 us  [powers(): pl.pallas_call(functools.partial(powers_kernel, count), out_shape=(jax.Sh...]
  transfers between devices with their start and end apart: 4 -> 4, of which waited for: 2 -> 3; matrix products, arithmetic and copies ran while one was open for 0% -> 0% of each run, Pallas kernels for 11% -> 10%
where the time goes in v5:
time: 52.6 us; the launch traced here: 52 us
  blocking collectives  21 us (40%)
  Pallas kernels  19.5 us (37%)
  starting transfers between devices  8.03 us (15%)
  waiting for transfers between devices  2.46 us (5%)
  between operations  0.85 us (2%)
    all_to_all x2, blocking collectives, gathered(): mine = lax.all_to_all(values, 'chip', 0, 0)  21 us
    pallas_call x1, Pallas kernels, powers(): pl.pallas_call(functools.partial(powers_kernel, count), out_shape=(jax.Sh...  5.97 us
    ppermute x1, starting transfers between devices, shards(): from_b = lax.ppermute(send_b, SLAB, across)  4.52 us
    pallas_call x1, Pallas kernels, near_body(): pl.pallas_call(near_kernel, out_shape=(jax.ShapeDtypeStruct((3, size), F3...  4.15 us
    ppermute x2, starting transfers between devices, gathered(): return (mine, lax.ppermute(mine, SLAB, partner))  3.44 us
    pallas_call x2, Pallas kernels, edge_rows(): pl.pallas_call(functools.partial(edge_kernel, even_last), out_shape=jax.S...  3.29 us
    pallas_call x1, Pallas kernels, inner_flux(): pl.pallas_call(inner_kernel, out_shape=(jax.ShapeDtypeStruct(flow_state.s...  3.02 us
    pallas_call x1, Pallas kernels, ordered(): pl.pallas_call(order_kernel, out_shape=(jax.ShapeDtypeStruct((16, count),...  2.06 us
  transfers between devices with their start and end apart: 4, of which 3 were waited for; matrix products, arithmetic and copies ran while one was open for 0% of the time, Pallas kernels for 10%

profile of v5, /device:TPU:1, one launch (start us, length us, event | category | flops | bytes accessed | tf_op | source)
XLA Modules:
  0.0 52.0 jit_solution(54306712928248300)
XLA Ops:
  0.6 1.6 %edge_rows.2.rest_0_.send_b = f32[6,8192]{1,0:T(8,128)} custom-call(f32[5,8,8192]{2,1,0:T(8,128)} %q_ref.5, f32[2,8,8192]{2,1,0:T(8,128)} %w_ref.5), custom_call_target="tpu_custom_call" | custom-call | tf_op jit(solution)/shard_map/edge_rows/pallas_call | solution.py:198
  2.2 0.0 copy-start.2
  2.3 0.0 copy-start.5
  2.3 0.0 copy-start.6
  2.3 0.0 copy-start.7
  2.3 0.0 copy-start.8
  2.3 0.0 copy-start.9
  2.3 1.7 %edge_rows.3.send_a = f32[6,8192]{1,0:T(8,128)} custom-call(f32[5,8,8192]{2,1,0:T(8,128)} %q_ref.5, f32[2,8,8192]{2,1,0:T(8,128)} %w_ref.5, f32[6,8192]{1,0:T(8,128)} %edge_rows.2.rest_0_.send_b), custom_call_target="tpu_custom_call" | custom-call | tf_op jit(solution)/shard_map/edge_rows/pallas_call | solution.py:198
  4.0 0.1 collective-permute-start
  4.1 0.0 copy-done.2
  4.1 4.5 %collective-permute-start.1 = (f32[6,8192]{1,0:T(8,128)S(1)}, f32[6,8192]{1,0:T(8,128)S(1)}, u32[]{:S(2)}, u32[]{:S(2)}) collective-permute-start(f32[6,8192]{1,0:T(8,128)S(1)} %copy-done.2), channel_id=1, source_target_pairs={{1,2},{3,4},{5,6},{7,8},{9,10},{11,12},{13,14},{2,1},{4,3},{6,5},{... | collective-permute-start | bytes 589832 | tf_op jit(solution)/shard_map/ppermute | solution.py:801
  8.6 0.0 copy-done.5
  8.6 0.0 copy-done.6
  8.7 0.0 copy-start
  8.7 0.0 copy-start.1
  8.7 2.1 %order.1 = (f32[16,512]{1,0:T(8,128)S(1)}, bf16[512,512]{1,0:T(8,128)(2,1)S(1)}, f32[8,1024]{1,0:T(8,128)S(1)}, bf16[1024,1024]{1,0:T(8,128)(2,1)S(1)}) custom-call(f32[3,512]{1,0:T(4,128)S(1)} %copy-done.6, f32[3,512]{1,0:T(4,128)S(1)} %copy-done.7, f32[3,512]{1,0:T(4,128)S(1)} %copy-done.8, s32[1,512]{1,0:T(1,128)S(1)} %bitcast.3, f32[3,1024]{1,0:T(4,128)S(1)} %copy-done.5), custom_call_target="tpu_custom_call" | custom-call | flops 2000000000 | bytes 4000000 | tf_op jit(solution)/shard_map/order/pallas_call | solution.py:153
  10.8 0.0 copy-start.3
  10.8 3.0 %inner_flux.1 = (f32[5,8,8192]{2,1,0:T(8,128)}, f32[5,8192]{1,0:T(8,128)S(1)}, f32[5,8192]{1,0:T(8,128)S(1)}, f32[16,512]{1,0:T(8,128)S(1)}, bf16[512,512]{1,0:T(8,128)(2,1)S(1)}) custom-call(f32[5,8,8192]{2,1,0:T(8,128)S(1)} %copy-done, f32[2,8,8192]{2,1,0:T(8,128)S(1)} %copy-done.1, f32[16,512]{1,0:T(8,128)S(1)} %get-tuple-element.22.sorted_ref), custom_call_target="tpu_custom_call" | custom-call | flops 20000000 | bytes 4000000 | tf_op jit(solution)/shard_map/inner_flux/pallas_call | solution.py:309
  13.8 0.0 collective-permute-done.from_a
  13.8 0.9 %collective-permute-done.1.from_b = f32[6,8192]{1,0:T(8,128)S(1)} collective-permute-done((f32[6,8192]{1,0:T(8,128)S(1)}, f32[6,8192]{1,0:T(8,128)S(1)}, u32[]{:S(2)}, u32[]{:S(2)}) %collective-permute-start.1) | collective-permute-done | bytes 196640 | tf_op jit(solution)/shard_map/ppermute | solution.py:801
  14.7 0.6 %outer_flux.1 = (f32[8,8,512]{2,1,0:T(8,128)S(1)}, f32[5,8192]{1,0:T(8,128)S(1)}, f32[5,8192]{1,0:T(8,128)S(1)}) custom-call(f32[6,8192]{1,0:T(8,128)S(1)} %copy-done.3, f32[6,8192]{1,0:T(8,128)S(1)} %copy-done.2, f32[6,8192]{1,0:T(8,128)S(1)} %collective-permute-done.from_a, f32[6,8192]{1,0:T(8,128)S(1)} %collective-permute-done.1.from_b, ...), custom_call_target="tpu_custom_call" | custom-call | tf_op jit(solution)/shard_map/outer_flux/pallas_call | solution.py:361
  15.3 0.0 copy-start.10
  15.4 12.1 %all_to_all.10.mine_ref = f32[8,8,512]{2,1,0:T(8,128)S(1)} all-to-all(f32[8,8,512]{2,1,0:T(8,128)S(1)} %get-tuple-element.27), channel_id=1, replica_groups=mesh['groups'=2,'chip'=8,'core'=2] {'chip'}, dimensions={0} | all-to-all | bytes 262144 | tf_op jit(solution)/shard_map/all_to_all | solution.py:780
  27.4 1.6 %collective-permute-start.2 = (f32[8,8,512]{2,1,0:T(8,128)S(1)}, f32[8,8,512]{2,1,0:T(8,128)S(1)}, u32[]{:S(2)}, u32[]{:S(2)}) collective-permute-start(f32[8,8,512]{2,1,0:T(8,128)S(1)} %all_to_all.10.mine_ref), channel_id=1, source_target_pairs={{0,1},{1,0},{2,3},{3,2},{4,5},{5,4},{6,7},{7,6},{8,9},{9,8},{10,11... | collective-permute-start | bytes 393224 | tf_op jit(solution)/shard_map/ppermute | solution.py:781
  29.0 1.0 %collective-permute-done.2.other_ref = f32[8,8,512]{2,1,0:T(8,128)S(1)} collective-permute-done((f32[8,8,512]{2,1,0:T(8,128)S(1)}, f32[8,8,512]{2,1,0:T(8,128)S(1)}, u32[]{:S(2)}, u32[]{:S(2)}) %collective-permute-start.2) | collective-permute-done | bytes 131104 | tf_op jit(solution)/shard_map/ppermute | solution.py:781
  30.0 6.0 %powers.1 = (f32[8,8,640]{2,1,0:T(8,128)S(1)}, f32[5,8,8192]{2,1,0:T(8,128)}) custom-call(f32[8,8,512]{2,1,0:T(8,128)S(1)} %all_to_all.10.mine_ref, f32[8,8,512]{2,1,0:T(8,128)S(1)} %collective-permute-done.2.other_ref, f32[5,8192]{1,0:T(8,128)S(1)} %get-tuple-element.28.new_low, ...), custom_call_target="tpu_custom_call", output_to_operand_aliasing={{1}: (4, {})} | custom-call | tf_op jit(solution)/shard_map/powers/pallas_call | solution.py:542
  36.0 9.0 %all_to_all.11.mine_power = f32[8,8,640]{2,1,0:T(8,128)S(1)} all-to-all(f32[8,8,640]{2,1,0:T(8,128)S(1)} %get-tuple-element.34), channel_id=1, replica_groups=mesh['groups'=2,'chip'=8,'core'=2] {'chip'}, dimensions={0} | all-to-all | bytes 327680 | tf_op jit(solution)/shard_map/all_to_all | solution.py:780
  44.9 1.9 %collective-permute-start.3 = (f32[8,8,640]{2,1,0:T(8,128)S(1)}, f32[8,8,640]{2,1,0:T(8,128)S(1)}, u32[]{:S(2)}, u32[]{:S(2)}) collective-permute-start(f32[8,8,640]{2,1,0:T(8,128)S(1)} %all_to_all.11.mine_power), channel_id=1, source_target_pairs={{0,1},{1,0},{2,3},{3,2},{4,5},{5,4},{6,7},{7,6},{8,9},{9,8},{10,11... | collective-permute-start | bytes 491528 | tf_op jit(solution)/shard_map/ppermute | solution.py:781
  46.8 0.1 copy.14.tile_ref
  46.9 0.4 near_points.1
  47.3 0.6 %collective-permute-done.3.other_power = f32[8,8,640]{2,1,0:T(8,128)S(1)} collective-permute-done((f32[8,8,640]{2,1,0:T(8,128)S(1)}, f32[8,8,640]{2,1,0:T(8,128)S(1)}, u32[]{:S(2)}, u32[]{:S(2)}) %collective-permute-start.3) | collective-permute-done | bytes 163872 | tf_op jit(solution)/shard_map/ppermute | solution.py:781
  47.8 4.2 %near_body.1 = (f32[3,512]{1,0:T(4,128)}, f32[3,1024]{1,0:T(4,128)}) custom-call(s32[16,4]{1,0:T(8,128)S(1)} %copy.14.tile_ref, s32[1,16]{1,0:T(1,128)S(1)} %bitcast.2, f32[2,8]{1,0:T(2,128)S(1)} %get-tuple-element.33.bound_ref, f32[8,8,512]{2,1,0:T(8,128)S(1)} %all_to_all.10.mine_ref, f32[8,8,512]{2,1,0:T(8,128)S(1)} %collective-permute-done.2.other_ref, ...), custom_call_target="tpu_custom_call" | custom-call | tf_op jit(solution)/shard_map/near_body/pallas_call | solution.py:757
  (9 shorter events, 0.0 us)
Async XLA Ops:
  2.2 1.8 %copy-start.2 = (f32[6,8192]{1,0:T(8,128)S(1)}, f32[6,8192]{1,0:T(8,128)}, u32[]{:S(2)}) copy-start(f32[6,8192]{1,0:T(8,128)} %edge_rows.2.rest_0_.send_b) | copy-start | bytes 589828
  2.3 6.4 %copy-start.5 = (f32[3,1024]{1,0:T(4,128)S(1)}, f32[3,1024]{1,0:T(4,128)}, u32[]{:S(2)}) copy-start(f32[3,1024]{1,0:T(4,128)} %nodes_ref.1) | copy-start | bytes 36868
  2.3 6.4 %copy-start.6 = (f32[3,512]{1,0:T(4,128)S(1)}, f32[3,512]{1,0:T(4,128)}, u32[]{:S(2)}) copy-start(f32[3,512]{1,0:T(4,128)} %base_ref.1) | copy-start | bytes 18436
  2.3 6.4 %copy-start.7 = (f32[3,512]{1,0:T(4,128)S(1)}, f32[3,512]{1,0:T(4,128)}, u32[]{:S(2)}) copy-start(f32[3,512]{1,0:T(4,128)} %normal_ref.1) | copy-start | bytes 18436
  2.3 6.4 %copy-start.8 = (f32[3,512]{1,0:T(4,128)S(1)}, f32[3,512]{1,0:T(4,128)}, u32[]{:S(2)}) copy-start(f32[3,512]{1,0:T(4,128)} %centre_ref.1) | copy-start | bytes 18436
  2.3 6.3 %copy-start.9 = (s32[512]{0:T(512)S(1)}, s32[512]{0:T(512)}, u32[]{:S(2)}) copy-start(s32[512]{0:T(512)} %param.11) | copy-start | bytes 6148
  4.0 9.8 %collective-permute-start = (f32[6,8192]{1,0:T(8,128)}, f32[6,8192]{1,0:T(8,128)S(1)}, u32[]{:S(2)}, u32[]{:S(2)}) collective-permute-start(f32[6,8192]{1,0:T(8,128)} %edge_rows.3.send_a), channel_id=1, source_target_pairs={{0,1},{1,0},{2,3},{3,2},{4,5},{5,4},{6,7},{7,6},{8,9},{9,8},{10,11... | collective-permute-start | bytes 589832 | tf_op jit(solution)/shard_map/ppermute | solution.py:803
  4.1 10.6 %collective-permute-start.1 = (f32[6,8192]{1,0:T(8,128)S(1)}, f32[6,8192]{1,0:T(8,128)S(1)}, u32[]{:S(2)}, u32[]{:S(2)}) collective-permute-start(f32[6,8192]{1,0:T(8,128)S(1)} %copy-done.2), channel_id=1, source_target_pairs={{1,2},{3,4},{5,6},{7,8},{9,10},{11,12},{13,14},{2,1},{4,3},{6,5},{... | collective-permute-start | bytes 589832 | tf_op jit(solution)/shard_map/ppermute | solution.py:801
  8.7 2.1 %copy-start = (f32[5,8,8192]{2,1,0:T(8,128)S(1)}, f32[5,8,8192]{2,1,0:T(8,128)}, u32[]{:S(2)}) copy-start(f32[5,8,8192]{2,1,0:T(8,128)} %q_ref.5) | copy-start | bytes 3932164
  8.7 2.1 %copy-start.1 = (f32[2,8,8192]{2,1,0:T(8,128)S(1)}, f32[2,8,8192]{2,1,0:T(8,128)}, u32[]{:S(2)}) copy-start(f32[2,8,8192]{2,1,0:T(8,128)} %w_ref.5) | copy-start | bytes 1572868
  10.8 4.0 %copy-start.3 = (f32[6,8192]{1,0:T(8,128)S(1)}, f32[6,8192]{1,0:T(8,128)}, u32[]{:S(2)}) copy-start(f32[6,8192]{1,0:T(8,128)} %edge_rows.3.send_a) | copy-start | bytes 589828
  15.3 31.5 %copy-start.10 = (s32[16,4]{0,1:T(4,128)S(1)}, s32[16,4]{0,1:T(4,128)}, u32[]{:S(2)}) copy-start(s32[16,4]{0,1:T(4,128)} %param.15) | copy-start | bytes 772
  27.4 2.6 %collective-permute-start.2 = (f32[8,8,512]{2,1,0:T(8,128)S(1)}, f32[8,8,512]{2,1,0:T(8,128)S(1)}, u32[]{:S(2)}, u32[]{:S(2)}) collective-permute-start(f32[8,8,512]{2,1,0:T(8,128)S(1)} %all_to_all.10.mine_ref), channel_id=1, source_target_pairs={{0,1},{1,0},{2,3},{3,2},{4,5},{5,4},{6,7},{7,6},{8,9},{9,8},{10,11... | collective-permute-start | bytes 393224 | tf_op jit(solution)/shard_map/ppermute | solution.py:781
  30.0 17.8 %copy-start.4 = (s32[16]{0:T(128)S(1)}, s32[16]{0:T(128)}, u32[]{:S(2)}) copy-start(s32[16]{0:T(128)} %param.16) | copy-start | bytes 196
  44.9 2.9 %collective-permute-start.3 = (f32[8,8,640]{2,1,0:T(8,128)S(1)}, f32[8,8,640]{2,1,0:T(8,128)S(1)}, u32[]{:S(2)}, u32[]{:S(2)}) collective-permute-start(f32[8,8,640]{2,1,0:T(8,128)S(1)} %all_to_all.11.mine_power), channel_id=1, source_target_pairs={{0,1},{1,0},{2,3},{3,2},{4,5},{5,4},{6,7},{7,6},{8,9},{9,8},{10,11... | collective-permute-start | bytes 491528 | tf_op jit(solution)/shard_map/ppermute | solution.py:781

commit v6 on v5

--- a/solution.py
+++ b/solution.py
@@ -20,7 +20,7 @@
 ORDER_FLOPS = 2_000_000_000
 BIG_LIMIT = 48 * 1024 * 1024
 SMALL_LIMIT = 16 * 1024 * 1024
-FULL_LIMIT = 62 * 1024 * 1024 + 768 * 1024
+
 F32 = jnp.float32
 BF16 = jnp.bfloat16
 SLAB = ("chip", "core")
@@ -166,8 +166,7 @@
     )(base_shift, normals, centres, wall_cell.reshape(1, -1), near_nodes)
 
 
-def edge_kernel(even_last, q_ref, w_ref, *rest):
-    target, sems = rest[-2:]
+def edge_kernel(even_last, q_ref, w_ref, target, sems):
     count, rows, _ = q_ref.shape
 
     def move(row):
@@ -193,17 +192,20 @@
         move(0 if even_last else rows - 1)
 
 
-def edge_rows(even_last, flow_state, flow_speed, *after):
+def edge_rows(even_last, flow_state, flow_speed):
     count, _, plane = flow_state.shape
     return pl.pallas_call(
         functools.partial(edge_kernel, even_last),
         out_shape=jax.ShapeDtypeStruct((count + 1, plane), F32),
-        in_specs=[HBM, HBM] + [HBM] * len(after),
+        in_specs=[HBM, HBM],
         out_specs=VMEM,
         scratch_shapes=[pltpu.SemaphoreType.DMA((count + 1,))],
-        compiler_params=pltpu.CompilerParams(vmem_limit_bytes=FULL_LIMIT),
+        compiler_params=pltpu.CompilerParams(vmem_limit_bytes=SMALL_LIMIT),
         name="edge_rows",
-    )(flow_state, flow_speed, *after)
+    )(
+        pltpu.with_memory_space_constraint(flow_state, pltpu.HBM),
+        pltpu.with_memory_space_constraint(flow_speed, pltpu.HBM),
+    )
 
 
 RATE = 0.5 * FLUX_STEP
@@ -799,7 +801,7 @@
     chips, rows = count // 2, flow_state.shape[1]
     send_b = edge_rows(False, flow_state, flow_speed)
     from_b = lax.ppermute(send_b, SLAB, across)
-    send_a = edge_rows(True, flow_state, flow_speed, send_b)
+    send_a = edge_rows(True, flow_state, flow_speed)
     from_a = lax.ppermute(send_a, SLAB, partner)
     in_order, centre_table, nodes, node_table = ordered(base_shift, normals, centres, wall_cell, near_nodes)
     new_flow, low, high, base, chosen = inner_flux(flow_state, flow_speed, in_order)

time: 52.6 us -> 51.2 us (0.973)
  Pallas kernels: 19.5 us -> 18 us
    pallas_call x2, Pallas kernels: 3.29 us -> 1.82 us  [edge_rows(): pl.pallas_call(functools.partial(edge_kernel, even_last), out_shape=jax.S...]
  transfers between devices with their start and end apart: 4 -> 4, of which waited for: 3 -> 3; matrix products, arithmetic and copies ran while one was open for 0% -> 0% of each run, Pallas kernels for 10% -> 13%
where the time goes in v6:
time: 51.2 us; the launch traced here: 50.5 us
  blocking collectives  21 us (41%)
  Pallas kernels  18 us (35%)
  starting transfers between devices  8.01 us (16%)
  waiting for transfers between devices  2.47 us (5%)
  between operations  0.83 us (2%)
    all_to_all x2, blocking collectives, gathered(): mine = lax.all_to_all(values, 'chip', 0, 0)  21 us
    pallas_call x1, Pallas kernels, powers(): pl.pallas_call(functools.partial(powers_kernel, count), out_shape=(jax.Sh...  5.97 us
    ppermute x1, starting transfers between devices, shards(): from_b = lax.ppermute(send_b, SLAB, across)  4.51 us
    pallas_call x1, Pallas kernels, near_body(): pl.pallas_call(near_kernel, out_shape=(jax.ShapeDtypeStruct((3, size), F3...  4.16 us
    ppermute x2, starting transfers between devices, gathered(): return (mine, lax.ppermute(mine, SLAB, partner))  3.43 us
    pallas_call x1, Pallas kernels, inner_flux(): pl.pallas_call(inner_kernel, out_shape=(jax.ShapeDtypeStruct(flow_state.s...  3.02 us
    pallas_call x1, Pallas kernels, ordered(): pl.pallas_call(order_kernel, out_shape=(jax.ShapeDtypeStruct((16, count),...  2.06 us
    pallas_call x2, Pallas kernels, edge_rows(): pl.pallas_call(functools.partial(edge_kernel, even_last), out_shape=jax.S...  1.82 us
  transfers between devices with their start and end apart: 4, of which 3 were waited for; matrix products, arithmetic and copies ran while one was open for 0% of the time, Pallas kernels for 13%

profile of v6, /device:TPU:1, one launch (start us, length us, event | category | flops | bytes accessed | tf_op | source)
XLA Modules:
  0.0 50.5 jit_solution(14087222651659721681)
XLA Ops:
  0.6 0.9 %edge_rows.2.send_a = f32[6,8192]{1,0:T(8,128)S(1)} custom-call(f32[5,8,8192]{2,1,0:T(8,128)} %q_ref.5, f32[2,8,8192]{2,1,0:T(8,128)} %w_ref.5), custom_call_target="tpu_custom_call" | custom-call | tf_op jit(solution)/shard_map/edge_rows/pallas_call | solution.py:197
  1.5 0.0 copy-start.3
  1.6 0.0 copy-start.4
  1.6 0.0 copy-start.5
  1.6 0.0 copy-start.6
  1.6 0.0 copy-start.7
  1.6 0.1 collective-permute-start
  1.7 0.9 %edge_rows.3.send_b = f32[6,8192]{1,0:T(8,128)S(1)} custom-call(f32[5,8,8192]{2,1,0:T(8,128)} %q_ref.5, f32[2,8,8192]{2,1,0:T(8,128)} %w_ref.5), custom_call_target="tpu_custom_call" | custom-call | tf_op jit(solution)/shard_map/edge_rows/pallas_call | solution.py:197
  2.6 4.5 %collective-permute-start.1 = (f32[6,8192]{1,0:T(8,128)S(1)}, f32[6,8192]{1,0:T(8,128)S(1)}, u32[]{:S(2)}, u32[]{:S(2)}) collective-permute-start(f32[6,8192]{1,0:T(8,128)S(1)} %edge_rows.3.send_b), channel_id=1, source_target_pairs={{1,2},{3,4},{5,6},{7,8},{9,10},{11,12},{13,14},{2,1},{4,3},{6,5},{... | collective-permute-start | bytes 589832 | tf_op jit(solution)/shard_map/ppermute | solution.py:803
  7.1 0.0 copy-done.3
  7.1 0.0 copy-done.4
  7.1 0.0 copy-done.5
  7.2 0.0 copy-start
  7.2 0.0 copy-start.1
  7.2 2.1 %order.1 = (f32[16,512]{1,0:T(8,128)S(1)}, bf16[512,512]{1,0:T(8,128)(2,1)S(1)}, f32[8,1024]{1,0:T(8,128)S(1)}, bf16[1024,1024]{1,0:T(8,128)(2,1)S(1)}) custom-call(f32[3,512]{1,0:T(4,128)S(1)} %copy-done.4, f32[3,512]{1,0:T(4,128)S(1)} %copy-done.5, f32[3,512]{1,0:T(4,128)S(1)} %copy-done.6, s32[1,512]{1,0:T(1,128)S(1)} %bitcast.3, f32[3,1024]{1,0:T(4,128)S(1)} %copy-done.3), custom_call_target="tpu_custom_call" | custom-call | flops 2000000000 | bytes 4000000 | tf_op jit(solution)/shard_map/order/pallas_call | solution.py:153
  9.3 0.0 copy-done
  9.3 3.0 %inner_flux.1 = (f32[5,8,8192]{2,1,0:T(8,128)}, f32[5,8192]{1,0:T(8,128)S(1)}, f32[5,8192]{1,0:T(8,128)S(1)}, f32[16,512]{1,0:T(8,128)S(1)}, bf16[512,512]{1,0:T(8,128)(2,1)S(1)}) custom-call(f32[5,8,8192]{2,1,0:T(8,128)S(1)} %copy-done, f32[2,8,8192]{2,1,0:T(8,128)S(1)} %copy-done.1, f32[16,512]{1,0:T(8,128)S(1)} %get-tuple-element.22.sorted_ref), custom_call_target="tpu_custom_call" | custom-call | flops 20000000 | bytes 4000000 | tf_op jit(solution)/shard_map/inner_flux/pallas_call | solution.py:311
  12.3 0.0 collective-permute-done.from_a
  12.3 0.9 %collective-permute-done.1.from_b = f32[6,8192]{1,0:T(8,128)S(1)} collective-permute-done((f32[6,8192]{1,0:T(8,128)S(1)}, f32[6,8192]{1,0:T(8,128)S(1)}, u32[]{:S(2)}, u32[]{:S(2)}) %collective-permute-start.1) | collective-permute-done | bytes 196640 | tf_op jit(solution)/shard_map/ppermute | solution.py:803
  13.2 0.6 %outer_flux.1 = (f32[8,8,512]{2,1,0:T(8,128)S(1)}, f32[5,8192]{1,0:T(8,128)S(1)}, f32[5,8192]{1,0:T(8,128)S(1)}) custom-call(f32[6,8192]{1,0:T(8,128)S(1)} %edge_rows.2.send_a, f32[6,8192]{1,0:T(8,128)S(1)} %edge_rows.3.send_b, f32[6,8192]{1,0:T(8,128)S(1)} %collective-permute-done.from_a, f32[6,8192]{1,0:T(8,128)S(1)} %collective-permute-done.1.from_b, ...), custom_call_target="tpu_custom_call" | custom-call | tf_op jit(solution)/shard_map/outer_flux/pallas_call | solution.py:363
  13.8 0.0 copy-start.8
  13.9 12.1 %all_to_all.10.mine_ref = f32[8,8,512]{2,1,0:T(8,128)S(1)} all-to-all(f32[8,8,512]{2,1,0:T(8,128)S(1)} %get-tuple-element.27), channel_id=1, replica_groups=mesh['groups'=2,'chip'=8,'core'=2] {'chip'}, dimensions={0} | all-to-all | bytes 262144 | tf_op jit(solution)/shard_map/all_to_all | solution.py:782
  25.9 1.6 %collective-permute-start.2 = (f32[8,8,512]{2,1,0:T(8,128)S(1)}, f32[8,8,512]{2,1,0:T(8,128)S(1)}, u32[]{:S(2)}, u32[]{:S(2)}) collective-permute-start(f32[8,8,512]{2,1,0:T(8,128)S(1)} %all_to_all.10.mine_ref), channel_id=1, source_target_pairs={{0,1},{1,0},{2,3},{3,2},{4,5},{5,4},{6,7},{7,6},{8,9},{9,8},{10,11... | collective-permute-start | bytes 393224 | tf_op jit(solution)/shard_map/ppermute | solution.py:783
  27.5 1.0 %collective-permute-done.2.other_ref = f32[8,8,512]{2,1,0:T(8,128)S(1)} collective-permute-done((f32[8,8,512]{2,1,0:T(8,128)S(1)}, f32[8,8,512]{2,1,0:T(8,128)S(1)}, u32[]{:S(2)}, u32[]{:S(2)}) %collective-permute-start.2) | collective-permute-done | bytes 131104 | tf_op jit(solution)/shard_map/ppermute | solution.py:783
  28.5 6.0 %powers.1 = (f32[8,8,640]{2,1,0:T(8,128)S(1)}, f32[5,8,8192]{2,1,0:T(8,128)}) custom-call(f32[8,8,512]{2,1,0:T(8,128)S(1)} %all_to_all.10.mine_ref, f32[8,8,512]{2,1,0:T(8,128)S(1)} %collective-permute-done.2.other_ref, f32[5,8192]{1,0:T(8,128)S(1)} %get-tuple-element.28.new_low, ...), custom_call_target="tpu_custom_call", output_to_operand_aliasing={{1}: (4, {})} | custom-call | tf_op jit(solution)/shard_map/powers/pallas_call | solution.py:544
  34.5 9.0 %all_to_all.11.mine_power = f32[8,8,640]{2,1,0:T(8,128)S(1)} all-to-all(f32[8,8,640]{2,1,0:T(8,128)S(1)} %get-tuple-element.34), channel_id=1, replica_groups=mesh['groups'=2,'chip'=8,'core'=2] {'chip'}, dimensions={0} | all-to-all | bytes 327680 | tf_op jit(solution)/shard_map/all_to_all | solution.py:782
  43.5 1.9 %collective-permute-start.3 = (f32[8,8,640]{2,1,0:T(8,128)S(1)}, f32[8,8,640]{2,1,0:T(8,128)S(1)}, u32[]{:S(2)}, u32[]{:S(2)}) collective-permute-start(f32[8,8,640]{2,1,0:T(8,128)S(1)} %all_to_all.11.mine_power), channel_id=1, source_target_pairs={{0,1},{1,0},{2,3},{3,2},{4,5},{5,4},{6,7},{7,6},{8,9},{9,8},{10,11... | collective-permute-start | bytes 491528 | tf_op jit(solution)/shard_map/ppermute | solution.py:783
  45.3 0.1 copy.14.tile_ref
  45.4 0.4 near_points.1
  45.8 0.6 %collective-permute-done.3.other_power = f32[8,8,640]{2,1,0:T(8,128)S(1)} collective-permute-done((f32[8,8,640]{2,1,0:T(8,128)S(1)}, f32[8,8,640]{2,1,0:T(8,128)S(1)}, u32[]{:S(2)}, u32[]{:S(2)}) %collective-permute-start.3) | collective-permute-done | bytes 163872 | tf_op jit(solution)/shard_map/ppermute | solution.py:783
  46.3 0.0 copy-done.2
  46.3 4.2 %near_body.1 = (f32[3,512]{1,0:T(4,128)}, f32[3,1024]{1,0:T(4,128)}) custom-call(s32[16,4]{1,0:T(8,128)S(1)} %copy.14.tile_ref, s32[1,16]{1,0:T(1,128)S(1)} %bitcast.2, f32[2,8]{1,0:T(2,128)S(1)} %get-tuple-element.33.bound_ref, f32[8,8,512]{2,1,0:T(8,128)S(1)} %all_to_all.10.mine_ref, f32[8,8,512]{2,1,0:T(8,128)S(1)} %collective-permute-done.2.other_ref, ...), custom_call_target="tpu_custom_call" | custom-call | tf_op jit(solution)/shard_map/near_body/pallas_call | solution.py:759
  (5 shorter events, 0.0 us)
Async XLA Ops:
  1.5 5.6 %copy-start.3 = (f32[3,1024]{1,0:T(4,128)S(1)}, f32[3,1024]{1,0:T(4,128)}, u32[]{:S(2)}) copy-start(f32[3,1024]{1,0:T(4,128)} %nodes_ref.1) | copy-start | bytes 36868
  1.6 5.6 %copy-start.4 = (f32[3,512]{1,0:T(4,128)S(1)}, f32[3,512]{1,0:T(4,128)}, u32[]{:S(2)}) copy-start(f32[3,512]{1,0:T(4,128)} %base_ref.1) | copy-start | bytes 18436
  1.6 5.6 %copy-start.5 = (f32[3,512]{1,0:T(4,128)S(1)}, f32[3,512]{1,0:T(4,128)}, u32[]{:S(2)}) copy-start(f32[3,512]{1,0:T(4,128)} %normal_ref.1) | copy-start | bytes 18436
  1.6 5.6 %copy-start.6 = (f32[3,512]{1,0:T(4,128)S(1)}, f32[3,512]{1,0:T(4,128)}, u32[]{:S(2)}) copy-start(f32[3,512]{1,0:T(4,128)} %centre_ref.1) | copy-start | bytes 18436
  1.6 5.6 %copy-start.7 = (s32[512]{0:T(512)S(1)}, s32[512]{0:T(512)}, u32[]{:S(2)}) copy-start(s32[512]{0:T(512)} %param.11) | copy-start | bytes 6148
  1.6 10.7 %collective-permute-start = (f32[6,8192]{1,0:T(8,128)S(1)}, f32[6,8192]{1,0:T(8,128)S(1)}, u32[]{:S(2)}, u32[]{:S(2)}) collective-permute-start(f32[6,8192]{1,0:T(8,128)S(1)} %edge_rows.2.send_a), channel_id=1, source_target_pairs={{0,1},{1,0},{2,3},{3,2},{4,5},{5,4},{6,7},{7,6},{8,9},{9,8},{10,11... | collective-permute-start | bytes 589832 | tf_op jit(solution)/shard_map/ppermute | solution.py:805
  2.6 10.6 %collective-permute-start.1 = (f32[6,8192]{1,0:T(8,128)S(1)}, f32[6,8192]{1,0:T(8,128)S(1)}, u32[]{:S(2)}, u32[]{:S(2)}) collective-permute-start(f32[6,8192]{1,0:T(8,128)S(1)} %edge_rows.3.send_b), channel_id=1, source_target_pairs={{1,2},{3,4},{5,6},{7,8},{9,10},{11,12},{13,14},{2,1},{4,3},{6,5},{... | collective-permute-start | bytes 589832 | tf_op jit(solution)/shard_map/ppermute | solution.py:803
  7.2 2.1 %copy-start = (f32[5,8,8192]{2,1,0:T(8,128)S(1)}, f32[5,8,8192]{2,1,0:T(8,128)}, u32[]{:S(2)}) copy-start(f32[5,8,8192]{2,1,0:T(8,128)} %q_ref.5) | copy-start | bytes 3932164
  7.2 2.1 %copy-start.1 = (f32[2,8,8192]{2,1,0:T(8,128)S(1)}, f32[2,8,8192]{2,1,0:T(8,128)}, u32[]{:S(2)}) copy-start(f32[2,8,8192]{2,1,0:T(8,128)} %w_ref.5) | copy-start | bytes 1572868
  13.8 31.5 %copy-start.8 = (s32[16,4]{0,1:T(4,128)S(1)}, s32[16,4]{0,1:T(4,128)}, u32[]{:S(2)}) copy-start(s32[16,4]{0,1:T(4,128)} %param.15) | copy-start | bytes 772
  25.9 2.6 %collective-permute-start.2 = (f32[8,8,512]{2,1,0:T(8,128)S(1)}, f32[8,8,512]{2,1,0:T(8,128)S(1)}, u32[]{:S(2)}, u32[]{:S(2)}) collective-permute-start(f32[8,8,512]{2,1,0:T(8,128)S(1)} %all_to_all.10.mine_ref), channel_id=1, source_target_pairs={{0,1},{1,0},{2,3},{3,2},{4,5},{5,4},{6,7},{7,6},{8,9},{9,8},{10,11... | collective-permute-start | bytes 393224 | tf_op jit(solution)/shard_map/ppermute | solution.py:783
  28.5 17.8 %copy-start.2 = (s32[16]{0:T(128)S(1)}, s32[16]{0:T(128)}, u32[]{:S(2)}) copy-start(s32[16]{0:T(128)} %param.16) | copy-start | bytes 196
  43.5 2.9 %collective-permute-start.3 = (f32[8,8,640]{2,1,0:T(8,128)S(1)}, f32[8,8,640]{2,1,0:T(8,128)S(1)}, u32[]{:S(2)}, u32[]{:S(2)}) collective-permute-start(f32[8,8,640]{2,1,0:T(8,128)S(1)} %all_to_all.11.mine_power), channel_id=1, source_target_pairs={{0,1},{1,0},{2,3},{3,2},{4,5},{5,4},{6,7},{7,6},{8,9},{9,8},{10,11... | collective-permute-start | bytes 491528 | tf_op jit(solution)/shard_map/ppermute | solution.py:783

commit v7 on v6

--- a/solution.py
+++ b/solution.py
@@ -14,6 +14,8 @@
 DIAG_SHIFT = 0.5
 CENTRE_SHIFT = DIAG_SHIFT + 1.0
 TINY = 1e-12
+ITERS = 3
+LOSS = 0.01
 DEPTH = 0.4
 CHUNK = 128
 MARGIN = 1e-3
@@ -311,7 +313,7 @@
     return pl.pallas_call(
         inner_kernel,
         out_shape=(
-            jax.ShapeDtypeStruct(flow_state.shape, F32),
+            pltpu.HBM(flow_state.shape, F32),
             edge,
             edge,
             jax.ShapeDtypeStruct((16, centres), F32),
@@ -545,7 +547,7 @@
         functools.partial(powers_kernel, count),
         out_shape=(
             jax.ShapeDtypeStruct((chips, 8, size + 128), F32),
-            jax.ShapeDtypeStruct(new_flow.shape, F32),
+            pltpu.HBM(new_flow.shape, F32),
         ),
         in_specs=[VMEM] * 4 + [HBM],
         out_specs=(VMEM, HBM),
@@ -562,7 +564,7 @@
         input_output_aliases={4: 1},
         compiler_params=pltpu.CompilerParams(vmem_limit_bytes=BIG_LIMIT),
         name="powers",
-    )(mine, other, new_low, new_high, new_flow)
+    )(mine, other, new_low, new_high, pltpu.with_memory_space_constraint(new_flow, pltpu.HBM))
 
 
 def ratio(top, bottom):
@@ -571,37 +573,43 @@
 
 
 def weights_of(moments):
+    lost = jnp.zeros_like(moments[0])
+
     def inner(left, right):
-        total = None
+        total = size = None
         for i, a in enumerate(left):
             for j, c in enumerate(right):
                 term = a * c * moments[i + j]
                 total = term if total is None else total + term
-        return total
+                size = jnp.abs(term) if size is None else size + jnp.abs(term)
+        return total, jnp.where(total > LOSS * size, 0.0, jnp.where(size > 0.0, 1.0, 0.0))
 
     one = jnp.ones_like(moments[0])
     residual, search = [one], [one]
-    coefficients = [0.0 * one] * 3
+    coefficients = [0.0 * one] * ITERS
     energy = moments[0]
-    for step in range(3):
+    for step in range(ITERS):
         image = [CENTRE_SHIFT * value for value in search] + [0.0 * one]
         for index, value in enumerate(search):
             image[index + 1] = image[index + 1] + value
-        length = ratio(energy, inner(search, image))
+        along, bad = inner(search, image)
+        lost = lost + bad
+        length = ratio(energy, along)
         for index, value in enumerate(search):
             coefficients[index] = coefficients[index] + length * value
-        if step == 2:
+        if step == ITERS - 1:
             break
         longer = residual + [0.0 * one]
         residual = [value - length * other for value, other in zip(longer, image)]
-        fresh = jnp.maximum(inner(residual, residual), 0.0)
+        fresh, bad = inner(residual, residual)
+        lost = lost + bad
         scale = ratio(fresh, energy)
         search = [
             value + scale * (search[index] if index < len(search) else 0.0)
             for index, value in enumerate(residual)
         ]
         energy = fresh
-    return coefficients
+    return coefficients, lost
 
 
 REACH = 7
@@ -677,7 +685,7 @@
 
 def near_kernel(
     tile_ref, count_ref, bound_ref, mine_ref, other_ref, mine_power, other_power, source_side, target_side,
-    centre_table, node_table, coef_ref, shift_ref, vector, result, low_ref, step_ref,
+    centre_table, node_table, coef_ref, shift_ref, lost_ref, vector, result, low_ref, step_ref,
 ):
     size = mine_ref.shape[2]
     slots = target_side.shape[1]
@@ -703,7 +711,8 @@
     summed = mine_power[0, :, size:] + other_power[0, :, size:]
     for index in range(1, chips):
         summed = summed + (mine_power[index, :, size:] + other_power[index, :, size:])
-    weights = weights_of([summed[:, index : index + 1] for index in range(6)])
+    weights, lost = weights_of([summed[:, index : index + 1] for index in range(6)])
+    lost_ref[...] = jnp.broadcast_to(jnp.max(lost[:3], axis=0, keepdims=True), (1, 128))
 
     def coefficients_of(block):
         data = block_of(mine_ref, other_ref, block, core)
@@ -761,9 +770,10 @@
         out_shape=(
             jax.ShapeDtypeStruct((3, size), F32),
             jax.ShapeDtypeStruct((3, slots), F32),
+            jax.ShapeDtypeStruct((1, 128), F32),
         ),
         in_specs=[VMEM] * 11,
-        out_specs=(VMEM, VMEM),
+        out_specs=(VMEM,) * 3,
         scratch_shapes=[
             pltpu.VMEM((16, total + REACH * CHUNK), BF16),
             pltpu.VMEM((16, slots), F32),
@@ -781,6 +791,51 @@
 def gathered(values, partner):
     mine = lax.all_to_all(values, "chip", 0, 0)
     return mine, lax.ppermute(mine, SLAB, partner)
+
+
+def step_by_step(count, right, centres, tile_blocks, near_count, near_nodes):
+    size = centres.shape[1]
+    up = [(i, i + 1) for i in range(count - 1)]
+    down = [(i + 1, i) for i in range(count - 1)]
+
+    def widened(values):
+        return jnp.concatenate([lax.ppermute(values, SLAB, up), values, lax.ppermute(values, SLAB, down)], axis=1)
+
+    def table_of(sources, targets):
+        scaled = jnp.sqrt(sum((sources[k][:, None] - targets[k][None, :]) ** 2 for k in range(3))) / SUPPORT
+        inside = jnp.maximum(1.0 - scaled, 0.0)
+        square_in = inside * inside
+        return square_in * square_in * (4.0 * scaled + 1.0)
+
+    def total(left, other):
+        return lax.psum(jnp.sum(left * other, axis=1), SLAB)
+
+    def product(values, table):
+        return jnp.dot(values, table, precision=lax.Precision.HIGHEST, preferred_element_type=F32)
+
+    around = widened(centres)
+
+    def step(_, held):
+        coefficients, residual, search, energy = held
+        image = product(widened(search), table_of(around, centres)) + DIAG_SHIFT * search
+        length = energy / total(search, image)
+        coefficients = coefficients + length[:, None] * search
+        residual = residual - length[:, None] * image
+        fresh = total(residual, residual)
+        return coefficients, residual, residual + (fresh / energy)[:, None] * search, fresh
+
+    coefficients = lax.fori_loop(0, ITERS, step, (jnp.zeros_like(right), right, right, total(right, right)))[0]
+    everywhere = lax.all_gather(jnp.concatenate([centres, coefficients], axis=0), SLAB, axis=1, tiled=True)
+    me = lax.axis_index(SLAB)
+    slots = near_nodes.shape[1]
+
+    def listed(index, sums):
+        data = lax.dynamic_slice_in_dim(everywhere, tile_blocks[me, index] * size, size, 1)
+        return sums + product(data[3:], table_of(data[:3], near_nodes))
+
+    shift = lax.fori_loop(0, tile_blocks.shape[1], listed, jnp.zeros((3, slots), F32))
+    live = lax.iota(jnp.int32, slots) < near_count[me]
+    return coefficients, jnp.where(live[None, :], shift, 0.0)
 
 
 def shards(
@@ -810,9 +865,23 @@
     power, new_flow = powers(mine, other, low, high, new_flow, count)
     mine_power, other_power = gathered(power, partner)
     sources, targets, bounds = near_points(tile_blocks, mine, other, nodes)
-    coefficients, node_shift = near_body(
+    coefficients, node_shift, lost = near_body(
         tile_blocks, near_count, bounds, mine, other, mine_power, other_power, sources, targets,
         centre_table, node_table,
+    )
+
+    def again(held):
+        one = jnp.where(held[0][0, 0] > 0.0, 1.0, 0.0)
+        whole = one.astype(jnp.int32)
+        own = packed[0] * one
+        found, shifted = step_by_step(
+            count, own[0:3], own[3:6], tile_blocks * whole, near_count * whole, near_nodes * one
+        )
+        back = jnp.dot(found, centre_table.astype(F32) * one, precision=lax.Precision.HIGHEST)
+        return jnp.zeros_like(held[0]), back, shifted
+
+    _, coefficients, node_shift = lax.while_loop(
+        lambda held: held[0][0, 0] > 0.0, again, (lost, coefficients, node_shift)
     )
     return new_flow, coefficients, node_shift
 

time: 51.2 us -> 52.2 us (1.020)
  loops' own time: 0 us -> 0.87 us
    another operation x0 -> x1, loops' own time: none -> 0.87 us  [shards(): lax.while_loop(lambda held: held[0][0, 0] > 0.0, again, (lost, coefficien...]
  transfers between devices with their start and end apart: 4 -> 4, of which waited for: 3 -> 3; matrix products, arithmetic and copies ran while one was open for 0% -> 0% of each run, Pallas kernels for 13% -> 12%
where the time goes in v7:
time: 52.2 us; the launch traced here: 51.5 us
  blocking collectives  21.1 us (40%)
  Pallas kernels  18 us (34%)
  starting transfers between devices  8.02 us (15%)
  waiting for transfers between devices  2.46 us (5%)
  between operations  0.98 us (2%)
  loops' own time  0.87 us (2%)
    all_to_all x2, blocking collectives, gathered(): mine = lax.all_to_all(values, 'chip', 0, 0)  21.1 us
    pallas_call x1, Pallas kernels, powers(): pl.pallas_call(functools.partial(powers_kernel, count), out_shape=(jax.Sh...  5.97 us
    ppermute x1, starting transfers between devices, shards(): from_b = lax.ppermute(send_b, SLAB, across)  4.52 us
    pallas_call x1, Pallas kernels, near_body(): pl.pallas_call(near_kernel, out_shape=(jax.ShapeDtypeStruct((3, size), F3...  4.15 us
    ppermute x2, starting transfers between devices, gathered(): return (mine, lax.ppermute(mine, SLAB, partner))  3.42 us
    pallas_call x1, Pallas kernels, inner_flux(): pl.pallas_call(inner_kernel, out_shape=(pltpu.HBM(flow_state.shape, F32),...  3.02 us
    pallas_call x1, Pallas kernels, ordered(): pl.pallas_call(order_kernel, out_shape=(jax.ShapeDtypeStruct((16, count),...  2.06 us
    pallas_call x2, Pallas kernels, edge_rows(): pl.pallas_call(functools.partial(edge_kernel, even_last), out_shape=jax.S...  1.83 us
  transfers between devices with their start and end apart: 4, of which 3 were waited for; matrix products, arithmetic and copies ran while one was open for 0% of the time, Pallas kernels for 12%

profile of v7, /device:TPU:1, one launch (start us, length us, event | category | flops | bytes accessed | tf_op | source)
XLA Modules:
  0.0 51.5 jit_solution(16569825481106857312)
XLA Ops:
  0.6 0.0 copy-start.2
  0.6 0.0 copy-start.3
  0.7 0.0 copy-start.4
  0.7 0.0 copy-start.5
  0.7 0.0 copy-start.6
  0.7 0.9 %edge_rows.2.send_a = f32[6,8192]{1,0:T(8,128)S(1)} custom-call(f32[5,8,8192]{2,1,0:T(8,128)} %q_ref.5, f32[2,8,8192]{2,1,0:T(8,128)} %w_ref.5), custom_call_target="tpu_custom_call" | custom-call | tf_op jit(solution)/shard_map/edge_rows/pallas_call | solution.py:199
  1.6 0.1 collective-permute-start.4
  1.7 0.9 %edge_rows.3.send_b = f32[6,8192]{1,0:T(8,128)S(1)} custom-call(f32[5,8,8192]{2,1,0:T(8,128)} %q_ref.5, f32[2,8,8192]{2,1,0:T(8,128)} %w_ref.5), custom_call_target="tpu_custom_call" | custom-call | tf_op jit(solution)/shard_map/edge_rows/pallas_call | solution.py:199
  2.6 4.5 %collective-permute-start.5 = (f32[6,8192]{1,0:T(8,128)S(1)}, f32[6,8192]{1,0:T(8,128)S(1)}, u32[]{:S(2)}, u32[]{:S(2)}) collective-permute-start(f32[6,8192]{1,0:T(8,128)S(1)} %edge_rows.3.send_b), channel_id=1, source_target_pairs={{1,2},{3,4},{5,6},{7,8},{9,10},{11,12},{13,14},{2,1},{4,3},{6,5},{... | collective-permute-start | bytes 589832 | tf_op jit(solution)/shard_map/ppermute | solution.py:858
  7.1 0.0 copy-done.2
  7.1 0.0 copy-done.3
  7.2 0.0 copy-start
  7.2 0.0 copy-start.1
  7.2 2.1 %order.1 = (f32[16,512]{1,0:T(8,128)S(1)}, bf16[512,512]{1,0:T(8,128)(2,1)S(1)}, f32[8,1024]{1,0:T(8,128)S(1)}, bf16[1024,1024]{1,0:T(8,128)(2,1)S(1)}) custom-call(f32[3,512]{1,0:T(4,128)S(1)} %copy-done.2, f32[3,512]{1,0:T(4,128)S(1)} %copy-done.3, f32[3,512]{1,0:T(4,128)S(1)} %copy-done.4, s32[1,512]{1,0:T(1,128)S(1)} %bitcast.58, f32[3,1024]{1,0:T(4,128)S(1)} %copy-done.6), custom_call_target="tpu_custom_call" | custom-call | flops 2000000000 | bytes 4000000 | tf_op jit(solution)/shard_map/order/pallas_call | solution.py:155
  9.3 0.0 copy-done
  9.3 0.0 copy-done.1
  9.3 3.0 %inner_flux.1 = (f32[5,8,8192]{2,1,0:T(8,128)}, f32[5,8192]{1,0:T(8,128)S(1)}, f32[5,8192]{1,0:T(8,128)S(1)}, f32[16,512]{1,0:T(8,128)S(1)}, bf16[512,512]{1,0:T(8,128)(2,1)S(1)}) custom-call(f32[5,8,8192]{2,1,0:T(8,128)S(1)} %copy-done, f32[2,8,8192]{2,1,0:T(8,128)S(1)} %copy-done.1, f32[16,512]{1,0:T(8,128)S(1)} %get-tuple-element.437.sorted_ref), custom_call_target="tpu_custom_call" | custom-call | flops 20000000 | bytes 4000000 | tf_op jit(solution)/shard_map/inner_flux/pallas_call | solution.py:313
  12.3 0.0 collective-permute-done.4.from_a
  12.3 0.9 %collective-permute-done.5.from_b = f32[6,8192]{1,0:T(8,128)S(1)} collective-permute-done((f32[6,8192]{1,0:T(8,128)S(1)}, f32[6,8192]{1,0:T(8,128)S(1)}, u32[]{:S(2)}, u32[]{:S(2)}) %collective-permute-start.5) | collective-permute-done | bytes 196640 | tf_op jit(solution)/shard_map/ppermute | solution.py:858
  13.2 0.6 %outer_flux.1 = (f32[8,8,512]{2,1,0:T(8,128)S(1)}, f32[5,8192]{1,0:T(8,128)S(1)}, f32[5,8192]{1,0:T(8,128)S(1)}) custom-call(f32[6,8192]{1,0:T(8,128)S(1)} %edge_rows.2.send_a, f32[6,8192]{1,0:T(8,128)S(1)} %edge_rows.3.send_b, f32[6,8192]{1,0:T(8,128)S(1)} %collective-permute-done.4.from_a, f32[6,8192]{1,0:T(8,128)S(1)} %collective-permute-done.5.from_b, ...), custom_call_target="tpu_custom_call" | custom-call | tf_op jit(solution)/shard_map/outer_flux/pallas_call | solution.py:365
  13.9 12.1 %all_to_all.10.mine_ref = f32[8,8,512]{2,1,0:T(8,128)S(1)} all-to-all(f32[8,8,512]{2,1,0:T(8,128)S(1)} %get-tuple-element.831), channel_id=1, replica_groups=mesh['groups'=2,'chip'=8,'core'=2] {'chip'}, dimensions={0} | all-to-all | bytes 262144 | tf_op jit(solution)/shard_map/all_to_all | solution.py:792
  25.9 1.6 %collective-permute-start.6 = (f32[8,8,512]{2,1,0:T(8,128)S(1)}, f32[8,8,512]{2,1,0:T(8,128)S(1)}, u32[]{:S(2)}, u32[]{:S(2)}) collective-permute-start(f32[8,8,512]{2,1,0:T(8,128)S(1)} %all_to_all.10.mine_ref), channel_id=1, source_target_pairs={{0,1},{1,0},{2,3},{3,2},{4,5},{5,4},{6,7},{7,6},{8,9},{9,8},{10,11... | collective-permute-start | bytes 393224 | tf_op jit(solution)/shard_map/ppermute | solution.py:793
  27.5 1.0 %collective-permute-done.6.other_ref = f32[8,8,512]{2,1,0:T(8,128)S(1)} collective-permute-done((f32[8,8,512]{2,1,0:T(8,128)S(1)}, f32[8,8,512]{2,1,0:T(8,128)S(1)}, u32[]{:S(2)}, u32[]{:S(2)}) %collective-permute-start.6) | collective-permute-done | bytes 131104 | tf_op jit(solution)/shard_map/ppermute | solution.py:793
  28.5 6.0 %powers.1 = (f32[8,8,640]{2,1,0:T(8,128)S(1)}, f32[5,8,8192]{2,1,0:T(8,128)}) custom-call(f32[8,8,512]{2,1,0:T(8,128)S(1)} %all_to_all.10.mine_ref, f32[8,8,512]{2,1,0:T(8,128)S(1)} %collective-permute-done.6.other_ref, f32[5,8192]{1,0:T(8,128)S(1)} %get-tuple-element.443.new_low, ...), custom_call_target="tpu_custom_call", output_to_operand_aliasing={{1}: (4, {})} | custom-call | tf_op jit(solution)/shard_map/powers/pallas_call | solution.py:546
  34.5 9.0 %all_to_all.11.mine_power = f32[8,8,640]{2,1,0:T(8,128)S(1)} all-to-all(f32[8,8,640]{2,1,0:T(8,128)S(1)} %get-tuple-element.449), channel_id=1, replica_groups=mesh['groups'=2,'chip'=8,'core'=2] {'chip'}, dimensions={0} | all-to-all | bytes 327680 | tf_op jit(solution)/shard_map/all_to_all | solution.py:792
  43.5 1.8 %collective-permute-start.7 = (f32[8,8,640]{2,1,0:T(8,128)S(1)}, f32[8,8,640]{2,1,0:T(8,128)S(1)}, u32[]{:S(2)}, u32[]{:S(2)}) collective-permute-start(f32[8,8,640]{2,1,0:T(8,128)S(1)} %all_to_all.11.mine_power), channel_id=1, source_target_pairs={{0,1},{1,0},{2,3},{3,2},{4,5},{5,4},{6,7},{7,6},{8,9},{9,8},{10,11... | collective-permute-start | bytes 491528 | tf_op jit(solution)/shard_map/ppermute | solution.py:793
  45.3 0.1 copy.14.tile_ref
  45.4 0.4 near_points.1
  45.8 0.6 %collective-permute-done.7.other_power = f32[8,8,640]{2,1,0:T(8,128)S(1)} collective-permute-done((f32[8,8,640]{2,1,0:T(8,128)S(1)}, f32[8,8,640]{2,1,0:T(8,128)S(1)}, u32[]{:S(2)}, u32[]{:S(2)}) %collective-permute-start.7) | collective-permute-done | bytes 163872 | tf_op jit(solution)/shard_map/ppermute | solution.py:793
  46.3 0.0 copy-done.8
  46.3 4.1 %near_body.1 = (f32[3,512]{1,0:T(4,128)}, f32[3,1024]{1,0:T(4,128)}, f32[1,128]{1,0:T(1,128)}) custom-call(s32[16,4]{1,0:T(8,128)S(1)} %copy.14.tile_ref, s32[1,16]{1,0:T(1,128)S(1)} %bitcast.68, f32[2,8]{1,0:T(2,128)S(1)} %get-tuple-element.448.bound_ref, f32[8,8,512]{2,1,0:T(8,128)S(1)} %all_to_all.10.mine_ref, ...), custom_call_target="tpu_custom_call" | custom-call | tf_op jit(solution)/shard_map/near_body/pallas_call | solution.py:768
  50.5 0.9 %while.71 = (f32[1,128]{1,0:T(1,128)}, f32[3,512]{1,0:T(4,128)}, f32[3,1024]{1,0:T(4,128)}, f32[8,8,512]{2,1,0:T(8,128)S(1)}, bf16[512,512]{1,0:T(8,128)(2,1)S(1...) while((f32[1,128]{1,0:T(1,128)}, f32[3,512]{1,0:T(4,128)}, ...), condition=%wide.region_11.12_spmd, body=%wide.region_0.11_spmd.sunk | while | flops 78180960 | bytes 1274309 | solution.py:883
  (6 shorter events, 0.0 us)
Async XLA Ops:
  0.6 6.5 %copy-start.2 = (f32[3,512]{1,0:T(4,128)S(1)}, f32[3,512]{1,0:T(4,128)}, u32[]{:S(2)}) copy-start(f32[3,512]{1,0:T(4,128)} %base_ref.1) | copy-start | bytes 18436
  0.6 6.5 %copy-start.3 = (f32[3,512]{1,0:T(4,128)S(1)}, f32[3,512]{1,0:T(4,128)}, u32[]{:S(2)}) copy-start(f32[3,512]{1,0:T(4,128)} %normal_ref.1) | copy-start | bytes 18436
  0.7 6.5 %copy-start.4 = (f32[3,512]{1,0:T(4,128)S(1)}, f32[3,512]{1,0:T(4,128)}, u32[]{:S(2)}) copy-start(f32[3,512]{1,0:T(4,128)} %centre_ref.1) | copy-start | bytes 18436
  0.7 6.5 %copy-start.5 = (s32[512]{0:T(512)S(1)}, s32[512]{0:T(512)}, u32[]{:S(2)}) copy-start(s32[512]{0:T(512)} %param.17) | copy-start | bytes 6148
  0.7 6.5 %copy-start.6 = (f32[3,1024]{1,0:T(4,128)S(1)}, f32[3,1024]{1,0:T(4,128)}, u32[]{:S(2)}) copy-start(f32[3,1024]{1,0:T(4,128)} %nodes_ref.1) | copy-start | bytes 36868
  1.6 10.7 %collective-permute-start.4 = (f32[6,8192]{1,0:T(8,128)S(1)}, f32[6,8192]{1,0:T(8,128)S(1)}, u32[]{:S(2)}, u32[]{:S(2)}) collective-permute-start(f32[6,8192]{1,0:T(8,128)S(1)} %edge_rows.2.send_a), channel_id=1, source_target_pairs={{0,1},{1,0},{2,3},{3,2},{4,5},{5,4},{6,7},{7,6},{8,9},{9,8},{10,11... | collective-permute-start | bytes 589832 | tf_op jit(solution)/shard_map/ppermute | solution.py:860
  2.6 10.6 %collective-permute-start.5 = (f32[6,8192]{1,0:T(8,128)S(1)}, f32[6,8192]{1,0:T(8,128)S(1)}, u32[]{:S(2)}, u32[]{:S(2)}) collective-permute-start(f32[6,8192]{1,0:T(8,128)S(1)} %edge_rows.3.send_b), channel_id=1, source_target_pairs={{1,2},{3,4},{5,6},{7,8},{9,10},{11,12},{13,14},{2,1},{4,3},{6,5},{... | collective-permute-start | bytes 589832 | tf_op jit(solution)/shard_map/ppermute | solution.py:858
  7.2 2.1 %copy-start = (f32[5,8,8192]{2,1,0:T(8,128)S(1)}, f32[5,8,8192]{2,1,0:T(8,128)}, u32[]{:S(2)}) copy-start(f32[5,8,8192]{2,1,0:T(8,128)} %q_ref.5) | copy-start | bytes 3932164
  7.2 2.1 %copy-start.1 = (f32[2,8,8192]{2,1,0:T(8,128)S(1)}, f32[2,8,8192]{2,1,0:T(8,128)}, u32[]{:S(2)}) copy-start(f32[2,8,8192]{2,1,0:T(8,128)} %w_ref.5) | copy-start | bytes 1572868
  13.2 32.1 %copy-start.7 = (s32[16,4]{0,1:T(4,128)S(1)}, s32[16,4]{0,1:T(4,128)}, u32[]{:S(2)}) copy-start(s32[16,4]{0,1:T(4,128)} %param.21) | copy-start | bytes 772
  13.2 33.1 %copy-start.8 = (s32[16]{0:T(128)S(1)}, s32[16]{0:T(128)}, u32[]{:S(2)}) copy-start(s32[16]{0:T(128)} %param.22) | copy-start | bytes 196
  25.9 2.6 %collective-permute-start.6 = (f32[8,8,512]{2,1,0:T(8,128)S(1)}, f32[8,8,512]{2,1,0:T(8,128)S(1)}, u32[]{:S(2)}, u32[]{:S(2)}) collective-permute-start(f32[8,8,512]{2,1,0:T(8,128)S(1)} %all_to_all.10.mine_ref), channel_id=1, source_target_pairs={{0,1},{1,0},{2,3},{3,2},{4,5},{5,4},{6,7},{7,6},{8,9},{9,8},{10,11... | collective-permute-start | bytes 393224 | tf_op jit(solution)/shard_map/ppermute | solution.py:793
  43.5 2.9 %collective-permute-start.7 = (f32[8,8,640]{2,1,0:T(8,128)S(1)}, f32[8,8,640]{2,1,0:T(8,128)S(1)}, u32[]{:S(2)}, u32[]{:S(2)}) collective-permute-start(f32[8,8,640]{2,1,0:T(8,128)S(1)} %all_to_all.11.mine_power), channel_id=1, source_target_pairs={{0,1},{1,0},{2,3},{3,2},{4,5},{5,4},{6,7},{7,6},{8,9},{9,8},{10,11... | collective-permute-start | bytes 491528 | tf_op jit(solution)/shard_map/ppermute | solution.py:793

commit v8 on v7

--- a/solution.py
+++ b/solution.py
@@ -124,16 +124,21 @@
         high_ref[tile] = jnp.max(jnp.where(near, index + 1.0, 0.0)).astype(jnp.int32)
 
 
-def order_kernel(base_ref, normal_ref, centre_ref, cell_ref, nodes_ref, out_ref, centre_table, nodes_out, node_table):
-    def table_of(ref, rank):
+def order_kernel(base_ref, normal_ref, centre_ref, cell_ref, nodes_ref, out_ref, centre_hbm, nodes_out, node_hbm, centre_table, node_table, sems):
+    copies = []
+
+    def table_of(ref, target, rank):
         count = rank.shape[1]
         rows = 128
         for start in range(0, count, rows):
             row = lax.broadcasted_iota(jnp.int32, (rows, count), 0).astype(F32) + float(start)
             ref[start : start + rows] = jnp.where(row == rank, 1.0, 0.0).astype(BF16)
+            piece = pl.ds(start, rows)
+            copies.append(pltpu.make_async_copy(ref.at[piece], target.at[piece], sems.at[len(copies)]))
+            copies[-1].start()
 
     count = centre_ref.shape[1]
-    table_of(centre_table, rank_of(centre_ref[2:3]))
+    table_of(centre_table, centre_hbm, rank_of(centre_ref[2:3]))
     values = jnp.concatenate(
         [
             base_ref[...],
@@ -145,9 +150,11 @@
         axis=0,
     )
     out_ref[...] = moved(values, centre_table[...])
-    table_of(node_table, rank_of(nodes_ref[2:3]))
+    table_of(node_table, node_hbm, rank_of(nodes_ref[2:3]))
     nodes = jnp.concatenate([nodes_ref[...], jnp.zeros((5, nodes_ref.shape[1]), F32)], axis=0)
     nodes_out[...] = moved(nodes, node_table[...])
+    for copy in copies:
+        copy.wait()
 
 
 def ordered(base_shift, normals, centres, wall_cell, near_nodes):
@@ -156,12 +163,17 @@
         order_kernel,
         out_shape=(
             jax.ShapeDtypeStruct((16, count), F32),
-            jax.ShapeDtypeStruct((count, count), BF16),
+            pltpu.HBM((count, count), BF16),
             jax.ShapeDtypeStruct((8, slots), F32),
-            jax.ShapeDtypeStruct((slots, slots), BF16),
+            pltpu.HBM((slots, slots), BF16),
         ),
         in_specs=[VMEM] * 5,
-        out_specs=(VMEM,) * 4,
+        out_specs=(VMEM, HBM, VMEM, HBM),
+        scratch_shapes=[
+            pltpu.VMEM((count, count), BF16),
+            pltpu.VMEM((slots, slots), BF16),
+            pltpu.SemaphoreType.DMA(((count + slots) // 128,)),
+        ],
         compiler_params=pltpu.CompilerParams(vmem_limit_bytes=SMALL_LIMIT),
         cost_estimate=pl.CostEstimate(flops=ORDER_FLOPS, bytes_accessed=4_000_000, transcendentals=0),
         name="order",
@@ -641,7 +653,27 @@
     return tile_ref[pl.ds(me, 1), :][0, 0]
 
 
-def points_kernel(tile_ref, mine_ref, other_ref, nodes_ref, source_ref, target_ref, bound_ref):
+def scalars_of(bound_ref, low_ref, step_ref):
+    bounds = bound_ref[...].astype(jnp.int32)
+    most = 0
+    for tile in range(bounds.shape[1]):
+        low = bounds[0, tile]
+        steps = lax.div(bounds[1, tile] - low + (REACH - 1), REACH)
+        low_ref[tile] = low
+        step_ref[tile] = steps
+        most = jnp.maximum(most, steps)
+    return most
+
+
+def near_table(source_ref, target_ref, low_ref, tile, step):
+    start = pl.multiple_of((low_ref[tile] + step * REACH) * CHUNK, CHUNK)
+    lanes = pl.ds(pl.multiple_of(tile * CHUNK, CHUNK), CHUNK)
+    return doubled(quarter_kernel(source_ref[pl.ds(start, REACH * CHUNK)], target_ref[:, lanes]))
+
+
+def points_kernel(
+    tile_ref, mine_ref, other_ref, nodes_ref, source_ref, target_ref, bound_ref, table_ref, low_ref, step_ref
+):
     size = mine_ref.shape[2]
     core = lax.axis_index("core")
     me = lax.axis_index("chip") * 2 + core
@@ -662,6 +694,15 @@
     _, target = sides(points)
     target_ref[...] = target.astype(BF16)
     bound_ref[...] = bounds_of(jnp.concatenate(third, axis=1), points[2:3])
+    scalars_of(bound_ref, low_ref, step_ref)
+
+    def two_tiles(step, _):
+        for piece in range(2):
+            tile = 2 * step + piece
+            table_ref[tile] = near_table(source_ref, target_ref, low_ref, tile, 0)
+        return 0
+
+    lax.fori_loop(0, table_ref.shape[0] // 2, two_tiles, 0)
 
 
 def near_points(tile_blocks, mine, other, nodes):
@@ -674,19 +715,31 @@
             jax.ShapeDtypeStruct((listed * size + REACH * CHUNK, 48), BF16),
             jax.ShapeDtypeStruct((48, slots), BF16),
             jax.ShapeDtypeStruct((2, slots // CHUNK), F32),
+            jax.ShapeDtypeStruct((slots // CHUNK // 2, 2 * REACH * CHUNK, CHUNK), BF16),
         ),
         in_specs=[VMEM] * 4,
-        out_specs=(VMEM,) * 3,
+        out_specs=(VMEM,) * 4,
+        scratch_shapes=[
+            pltpu.SMEM((slots // CHUNK,), jnp.int32),
+            pltpu.SMEM((slots // CHUNK,), jnp.int32),
+        ],
         compiler_params=pltpu.CompilerParams(vmem_limit_bytes=SMALL_LIMIT),
-        cost_estimate=pl.CostEstimate(flops=1_000_000, bytes_accessed=1_000_000, transcendentals=0),
+        cost_estimate=pl.CostEstimate(flops=1_000_000_000, bytes_accessed=4_000_000, transcendentals=0),
         name="near_points",
     )(tile_blocks, mine, other, nodes)
 
 
 def near_kernel(
     tile_ref, count_ref, bound_ref, mine_ref, other_ref, mine_power, other_power, source_side, target_side,
-    centre_table, node_table, coef_ref, shift_ref, lost_ref, vector, result, low_ref, step_ref,
+    table_ref, centre_hbm, node_hbm, coef_ref, shift_ref, lost_ref,
+    centre_table, node_table, vector, result, low_ref, step_ref, sems,
 ):
+    copies = [
+        pltpu.make_async_copy(centre_hbm, centre_table, sems.at[0]),
+        pltpu.make_async_copy(node_hbm, node_table, sems.at[1]),
+    ]
+    for copy in copies:
+        copy.start()
     size = mine_ref.shape[2]
     slots = target_side.shape[1]
     chips = mine_ref.shape[0]
@@ -699,15 +752,7 @@
     span = REACH * CHUNK
     total = listed * size
 
-    bounds = bound_ref[...].astype(jnp.int32)
-    most = 0
-    for tile in range(tiles):
-        low = bounds[0, tile]
-        steps = lax.div(bounds[1, tile] - low + (REACH - 1), REACH)
-        low_ref[tile] = low
-        step_ref[tile] = steps
-        most = jnp.maximum(most, steps)
-
+    most = scalars_of(bound_ref, low_ref, step_ref)
     summed = mine_power[0, :, size:] + other_power[0, :, size:]
     for index in range(1, chips):
         summed = summed + (mine_power[index, :, size:] + other_power[index, :, size:])
@@ -724,29 +769,34 @@
     for index in range(listed):
         vector[:, index * size : (index + 1) * size] = doubled(coefficients_of(start_block + index))
     vector[:, total:] = jnp.zeros((16, span), BF16)
-    coef_ref[...] = moved_back(coefficients_of(me), centre_table[...])
 
     def lanes_of(tile):
         return pl.ds(pl.multiple_of(tile * width, width), width)
 
-    def one(tile, step):
+    def one(tile, step, table):
         start = pl.multiple_of((low_ref[tile] + step * REACH) * CHUNK, CHUNK)
-        table = quarter_kernel(source_side[pl.ds(start, span)], target_side[:, lanes_of(tile)])
         window = vector[:, pl.ds(start, span)]
-        return jnp.dot(jnp.concatenate([window, window], axis=1), doubled(table), preferred_element_type=F32)
+        return jnp.dot(jnp.concatenate([window, window], axis=1), table, preferred_element_type=F32)
+
+    early = table_ref.shape[0]
+    for tile in range(early):
+        result[:, tile * width : (tile + 1) * width] = one(tile, 0, table_ref[tile])
 
     def two_tiles(step, _):
         for piece in range(2):
-            result[:, lanes_of(2 * step + piece)] = one(2 * step + piece, 0)
+            tile = early + 2 * step + piece
+            table = near_table(source_side, target_side, low_ref, tile, 0)
+            result[:, lanes_of(tile)] = one(tile, 0, table)
         return 0
 
-    lax.fori_loop(0, tiles // 2, two_tiles, 0)
+    lax.fori_loop(0, (tiles - early) // 2, two_tiles, 0)
 
     @pl.when(most > 1)
     def _():
         def of_tile(tile, _):
             def add(step, _):
-                result[:, lanes_of(tile)] += one(tile, step)
+                table = near_table(source_side, target_side, low_ref, tile, step)
+                result[:, lanes_of(tile)] += one(tile, step, table)
                 return 0
 
             return lax.fori_loop(1, step_ref[tile], add, 0)
@@ -757,11 +807,14 @@
     live = jnp.sum(jnp.where(lane == me, count_ref[...], 0).astype(F32), axis=1, keepdims=True)
     slot = lax.broadcasted_iota(jnp.int32, (3, slots), 1).astype(F32)
     both = result[...]
+    for copy in copies:
+        copy.wait()
+    coef_ref[...] = moved_back(coefficients_of(me), centre_table[...])
     shift = moved_back(4.0 * (both[:8] + both[8:]), node_table[...])
     shift_ref[...] = jnp.where(slot < live, shift, 0.0)
 
 
-def near_body(tile_blocks, near_count, bounds, mine, other, mine_power, other_power, sources, targets, centre_table, node_table):
+def near_body(tile_blocks, near_count, bounds, mine, other, mine_power, other_power, sources, targets, tables, centre_table, node_table):
     size = mine.shape[2]
     slots = targets.shape[1]
     total = tile_blocks.shape[1] * size
@@ -772,19 +825,24 @@
             jax.ShapeDtypeStruct((3, slots), F32),
             jax.ShapeDtypeStruct((1, 128), F32),
         ),
-        in_specs=[VMEM] * 11,
+        in_specs=[VMEM] * 10 + [HBM] * 2,
         out_specs=(VMEM,) * 3,
         scratch_shapes=[
+            pltpu.VMEM((size, size), BF16),
+            pltpu.VMEM((slots, slots), BF16),
             pltpu.VMEM((16, total + REACH * CHUNK), BF16),
             pltpu.VMEM((16, slots), F32),
             pltpu.SMEM((slots // CHUNK,), jnp.int32),
             pltpu.SMEM((slots // CHUNK,), jnp.int32),
+            pltpu.SemaphoreType.DMA((2,)),
         ],
         compiler_params=pltpu.CompilerParams(vmem_limit_bytes=SMALL_LIMIT),
         name="near_body",
     )(
         tile_blocks, near_count.reshape(1, -1), bounds, mine, other, mine_power, other_power, sources, targets,
-        centre_table, node_table,
+        tables,
+        pltpu.with_memory_space_constraint(centre_table, pltpu.HBM),
+        pltpu.with_memory_space_constraint(node_table, pltpu.HBM),
     )
 
 
@@ -864,10 +922,10 @@
     mine, other = gathered(packed, partner)
     power, new_flow = powers(mine, other, low, high, new_flow, count)
     mine_power, other_power = gathered(power, partner)
-    sources, targets, bounds = near_points(tile_blocks, mine, other, nodes)
+    sources, targets, bounds, tables = near_points(tile_blocks, mine, other, nodes)
     coefficients, node_shift, lost = near_body(
         tile_blocks, near_count, bounds, mine, other, mine_power, other_power, sources, targets,
-        centre_table, node_table,
+        tables, centre_table, node_table,
     )
 
     def again(held):

time: 52.2 us -> 51.7 us (level)
  Pallas kernels: 18 us -> 19.5 us
  waiting for transfers between devices: 2.46 us -> 0.99 us
    pallas_call x1, Pallas kernels: 0.36 us -> 1.54 us  [near_points(): pl.pallas_call(points_kernel, out_shape=(jax.ShapeDtypeStruct((listed * s...]
    pallas_call x1, Pallas kernels: 2.06 us -> 3.18 us  [ordered(): pl.pallas_call(order_kernel, out_shape=(jax.ShapeDtypeStruct((16, count),...]
    ppermute x1, waiting for transfers between devices: 0.89 us -> 0.01 us  [shards(): from_b = lax.ppermute(send_b, SLAB, across)]
    pallas_call x1, Pallas kernels: 4.15 us -> 3.34 us  [near_body(): pl.pallas_call(near_kernel, out_shape=(jax.ShapeDtypeStruct((3, size), F3...]
    ppermute x2, waiting for transfers between devices: 1.56 us -> 0.99 us  [gathered(): return (mine, lax.ppermute(mine, SLAB, partner))]
  transfers between devices with their start and end apart: 4 -> 4, of which waited for: 3 -> 1; matrix products, arithmetic and copies ran while one was open for 0% -> 0% of each run, Pallas kernels for 12% -> 17%
where the time goes in v8:
time: 51.7 us; the launch traced here: 51.3 us
  blocking collectives  20.8 us (40%)
  Pallas kernels  19.5 us (38%)
  starting transfers between devices  8.04 us (16%)
  between operations  1.04 us (2%)
  waiting for transfers between devices  0.99 us (2%)
  loops' own time  0.76 us (1%)
    all_to_all x2, blocking collectives, gathered(): mine = lax.all_to_all(values, 'chip', 0, 0)  20.8 us
    pallas_call x1, Pallas kernels, powers(): pl.pallas_call(functools.partial(powers_kernel, count), out_shape=(jax.Sh...  5.97 us
    ppermute x1, starting transfers between devices, shards(): from_b = lax.ppermute(send_b, SLAB, across)  4.52 us
    ppermute x2, starting transfers between devices, gathered(): return (mine, lax.ppermute(mine, SLAB, partner))  3.43 us
    pallas_call x1, Pallas kernels, near_body(): pl.pallas_call(near_kernel, out_shape=(jax.ShapeDtypeStruct((3, size), F3...  3.34 us
    pallas_call x1, Pallas kernels, ordered(): pl.pallas_call(order_kernel, out_shape=(jax.ShapeDtypeStruct((16, count),...  3.18 us
    pallas_call x1, Pallas kernels, inner_flux(): pl.pallas_call(inner_kernel, out_shape=(pltpu.HBM(flow_state.shape, F32),...  3.02 us
    pallas_call x2, Pallas kernels, edge_rows(): pl.pallas_call(functools.partial(edge_kernel, even_last), out_shape=jax.S...  1.83 us
  transfers between devices with their start and end apart: 4, of which 1 were waited for; matrix products, arithmetic and copies ran while one was open for 0% of the time, Pallas kernels for 17%

profile of v8, /device:TPU:1, one launch (start us, length us, event | category | flops | bytes accessed | tf_op | source)
XLA Modules:
  0.0 51.3 jit_solution(13549854574987057632)
XLA Ops:
  0.6 0.0 copy-start.2
  0.6 0.0 copy-start.3
  0.7 0.0 copy-start.4
  0.7 0.0 copy-start.5
  0.7 0.0 copy-start.7
  0.7 0.9 %edge_rows.2.send_a = f32[6,8192]{1,0:T(8,128)S(1)} custom-call(f32[5,8,8192]{2,1,0:T(8,128)} %q_ref.5, f32[2,8,8192]{2,1,0:T(8,128)} %w_ref.5), custom_call_target="tpu_custom_call" | custom-call | tf_op jit(solution)/shard_map/edge_rows/pallas_call | solution.py:211
  1.6 0.1 collective-permute-start.4
  1.7 0.9 %edge_rows.3.send_b = f32[6,8192]{1,0:T(8,128)S(1)} custom-call(f32[5,8,8192]{2,1,0:T(8,128)} %q_ref.5, f32[2,8,8192]{2,1,0:T(8,128)} %w_ref.5), custom_call_target="tpu_custom_call" | custom-call | tf_op jit(solution)/shard_map/edge_rows/pallas_call | solution.py:211
  2.6 4.5 %collective-permute-start.5 = (f32[6,8192]{1,0:T(8,128)S(1)}, f32[6,8192]{1,0:T(8,128)S(1)}, u32[]{:S(2)}, u32[]{:S(2)}) collective-permute-start(f32[6,8192]{1,0:T(8,128)S(1)} %edge_rows.3.send_b), channel_id=1, source_target_pairs={{1,2},{3,4},{5,6},{7,8},{9,10},{11,12},{13,14},{2,1},{4,3},{6,5},{... | collective-permute-start | bytes 589832 | tf_op jit(solution)/shard_map/ppermute | solution.py:916
  7.1 0.0 copy-done.2
  7.1 0.0 copy-done.3
  7.2 0.0 copy-start
  7.2 0.0 copy-start.1
  7.2 3.2 %order.1 = (f32[16,512]{1,0:T(8,128)S(1)}, bf16[512,512]{1,0:T(8,128)(2,1)}, f32[8,1024]{1,0:T(8,128)S(1)}, bf16[1024,1024]{1,0:T(8,128)(2,1)}) custom-call(f32[3,512]{1,0:T(4,128)S(1)} %copy-done.2, f32[3,512]{1,0:T(4,128)S(1)} %copy-done.3, f32[3,512]{1,0:T(4,128)S(1)} %copy-done.4, s32[1,512]{1,0:T(1,128)S(1)} %bitcast.58, f32[3,1024]{1,0:T(4,128)S(1)} %copy-done.7), custom_call_target="tpu_custom_call" | custom-call | flops 2000000000 | bytes 4000000 | tf_op jit(solution)/shard_map/order/pallas_call | solution.py:162
  10.4 3.0 %inner_flux.1 = (f32[5,8,8192]{2,1,0:T(8,128)}, f32[5,8192]{1,0:T(8,128)S(1)}, f32[5,8192]{1,0:T(8,128)S(1)}, f32[16,512]{1,0:T(8,128)S(1)}, bf16[512,512]{1,0:T(8,128)(2,1)S(1)}) custom-call(f32[5,8,8192]{2,1,0:T(8,128)S(1)} %copy-done, f32[2,8,8192]{2,1,0:T(8,128)S(1)} %copy-done.1, f32[16,512]{1,0:T(8,128)S(1)} %get-tuple-element.438.sorted_ref), custom_call_target="tpu_custom_call" | custom-call | flops 20000000 | bytes 4000000 | tf_op jit(solution)/shard_map/inner_flux/pallas_call | solution.py:325
  13.4 0.0 collective-permute-done.4.from_a
  13.5 0.0 collective-permute-done.5.from_b
  13.5 0.0 copy-start.8
  13.5 0.6 %outer_flux.1 = (f32[8,8,512]{2,1,0:T(8,128)S(1)}, f32[5,8192]{1,0:T(8,128)S(1)}, f32[5,8192]{1,0:T(8,128)S(1)}) custom-call(f32[6,8192]{1,0:T(8,128)S(1)} %edge_rows.2.send_a, f32[6,8192]{1,0:T(8,128)S(1)} %edge_rows.3.send_b, f32[6,8192]{1,0:T(8,128)S(1)} %collective-permute-done.4.from_a, f32[6,8192]{1,0:T(8,128)S(1)} %collective-permute-done.5.from_b, ...), custom_call_target="tpu_custom_call" | custom-call | tf_op jit(solution)/shard_map/outer_flux/pallas_call | solution.py:377
  14.1 11.8 %all_to_all.10.mine_ref = f32[8,8,512]{2,1,0:T(8,128)S(1)} all-to-all(f32[8,8,512]{2,1,0:T(8,128)S(1)} %get-tuple-element.833), channel_id=1, replica_groups=mesh['groups'=2,'chip'=8,'core'=2] {'chip'}, dimensions={0} | all-to-all | bytes 262144 | tf_op jit(solution)/shard_map/all_to_all | solution.py:850
  25.9 1.6 %collective-permute-start.6 = (f32[8,8,512]{2,1,0:T(8,128)S(1)}, f32[8,8,512]{2,1,0:T(8,128)S(1)}, u32[]{:S(2)}, u32[]{:S(2)}) collective-permute-start(f32[8,8,512]{2,1,0:T(8,128)S(1)} %all_to_all.10.mine_ref), channel_id=1, source_target_pairs={{0,1},{1,0},{2,3},{3,2},{4,5},{5,4},{6,7},{7,6},{8,9},{9,8},{10,11... | collective-permute-start | bytes 393224 | tf_op jit(solution)/shard_map/ppermute | solution.py:851
  27.5 1.0 %collective-permute-done.6.other_ref = f32[8,8,512]{2,1,0:T(8,128)S(1)} collective-permute-done((f32[8,8,512]{2,1,0:T(8,128)S(1)}, f32[8,8,512]{2,1,0:T(8,128)S(1)}, u32[]{:S(2)}, u32[]{:S(2)}) %collective-permute-start.6) | collective-permute-done | bytes 131104 | tf_op jit(solution)/shard_map/ppermute | solution.py:851
  28.5 6.0 %powers.1 = (f32[8,8,640]{2,1,0:T(8,128)S(1)}, f32[5,8,8192]{2,1,0:T(8,128)}) custom-call(f32[8,8,512]{2,1,0:T(8,128)S(1)} %all_to_all.10.mine_ref, f32[8,8,512]{2,1,0:T(8,128)S(1)} %collective-permute-done.6.other_ref, f32[5,8192]{1,0:T(8,128)S(1)} %get-tuple-element.444.new_low, ...), custom_call_target="tpu_custom_call", output_to_operand_aliasing={{1}: (4, {})} | custom-call | tf_op jit(solution)/shard_map/powers/pallas_call | solution.py:558
  34.5 0.0 copy-start.9
  34.5 9.0 %all_to_all.11.mine_power = f32[8,8,640]{2,1,0:T(8,128)S(1)} all-to-all(f32[8,8,640]{2,1,0:T(8,128)S(1)} %get-tuple-element.450), channel_id=1, replica_groups=mesh['groups'=2,'chip'=8,'core'=2] {'chip'}, dimensions={0} | all-to-all | bytes 327680 | tf_op jit(solution)/shard_map/all_to_all | solution.py:850
  43.5 1.8 %collective-permute-start.7 = (f32[8,8,640]{2,1,0:T(8,128)S(1)}, f32[8,8,640]{2,1,0:T(8,128)S(1)}, u32[]{:S(2)}, u32[]{:S(2)}) collective-permute-start(f32[8,8,640]{2,1,0:T(8,128)S(1)} %all_to_all.11.mine_power), channel_id=1, source_target_pairs={{0,1},{1,0},{2,3},{3,2},{4,5},{5,4},{6,7},{7,6},{8,9},{9,8},{10,11... | collective-permute-start | bytes 491528 | tf_op jit(solution)/shard_map/ppermute | solution.py:851
  45.3 0.0 copy-done.8
  45.3 0.1 copy.14.tile_ref
  45.4 1.5 %near_points.1 = (bf16[2944,48]{1,0:T(8,128)(2,1)S(1)}, bf16[48,1024]{1,0:T(8,128)(2,1)S(1)}, f32[2,8]{1,0:T(2,128)S(1)}, bf16[4,1792,128]{2,1,0:T(8,128)(2,1)S(1)}) custom-call(s32[16,4]{1,0:T(8,128)S(1)} %copy.14.tile_ref, f32[8,8,512]{2,1,0:T(8,128)S(1)} %all_to_all.10.mine_ref, f32[8,8,512]{2,1,0:T(8,128)S(1)} %collective-permute-done.6.other_ref, ...), custom_call_target="tpu_custom_call" | custom-call | flops 1000000000 | bytes 4000000 | tf_op jit(solution)/shard_map/near_points/pallas_call | solution.py:712
  47.0 0.0 collective-permute-done.7.other_power
  47.0 3.3 %near_body.1 = (f32[3,512]{1,0:T(4,128)}, f32[3,1024]{1,0:T(4,128)}, f32[1,128]{1,0:T(1,128)}) custom-call(s32[16,4]{1,0:T(8,128)S(1)} %copy.14.tile_ref, s32[1,16]{1,0:T(1,128)S(1)} %bitcast.68, f32[2,8]{1,0:T(2,128)S(1)} %get-tuple-element.449.bound_ref, f32[8,8,512]{2,1,0:T(8,128)S(1)} %all_to_all.10.mine_ref, ...), custom_call_target="tpu_custom_call" | custom-call | tf_op jit(solution)/shard_map/near_body/pallas_call | solution.py:821
  50.3 0.8 %while.71 = (f32[1,128]{1,0:T(1,128)}, f32[3,512]{1,0:T(4,128)}, f32[3,1024]{1,0:T(4,128)}, f32[8,8,512]{2,1,0:T(8,128)S(1)}, bf16[512,512]{1,0:T(8,128)(2,1)S(1...) while((f32[1,128]{1,0:T(1,128)}, f32[3,512]{1,0:T(4,128)}, ...), condition=%wide.region_11.12_spmd, body=%wide.region_0.11_spmd.sunk | while | flops 78180960 | bytes 1274309 | solution.py:941
  (8 shorter events, 0.0 us)
Async XLA Ops:
  0.6 6.5 %copy-start.2 = (f32[3,512]{1,0:T(4,128)S(1)}, f32[3,512]{1,0:T(4,128)}, u32[]{:S(2)}) copy-start(f32[3,512]{1,0:T(4,128)} %base_ref.1) | copy-start | bytes 18436
  0.6 6.5 %copy-start.3 = (f32[3,512]{1,0:T(4,128)S(1)}, f32[3,512]{1,0:T(4,128)}, u32[]{:S(2)}) copy-start(f32[3,512]{1,0:T(4,128)} %normal_ref.1) | copy-start | bytes 18436
  0.7 6.5 %copy-start.4 = (f32[3,512]{1,0:T(4,128)S(1)}, f32[3,512]{1,0:T(4,128)}, u32[]{:S(2)}) copy-start(f32[3,512]{1,0:T(4,128)} %centre_ref.1) | copy-start | bytes 18436
  0.7 6.5 %copy-start.5 = (s32[512]{0:T(512)S(1)}, s32[512]{0:T(512)}, u32[]{:S(2)}) copy-start(s32[512]{0:T(512)} %param.17) | copy-start | bytes 6148
  0.7 6.5 %copy-start.7 = (f32[3,1024]{1,0:T(4,128)S(1)}, f32[3,1024]{1,0:T(4,128)}, u32[]{:S(2)}) copy-start(f32[3,1024]{1,0:T(4,128)} %nodes_ref.1) | copy-start | bytes 36868
  1.6 11.8 %collective-permute-start.4 = (f32[6,8192]{1,0:T(8,128)S(1)}, f32[6,8192]{1,0:T(8,128)S(1)}, u32[]{:S(2)}, u32[]{:S(2)}) collective-permute-start(f32[6,8192]{1,0:T(8,128)S(1)} %edge_rows.2.send_a), channel_id=1, source_target_pairs={{0,1},{1,0},{2,3},{3,2},{4,5},{5,4},{6,7},{7,6},{8,9},{9,8},{10,11... | collective-permute-start | bytes 589832 | tf_op jit(solution)/shard_map/ppermute | solution.py:918
  2.6 10.9 %collective-permute-start.5 = (f32[6,8192]{1,0:T(8,128)S(1)}, f32[6,8192]{1,0:T(8,128)S(1)}, u32[]{:S(2)}, u32[]{:S(2)}) collective-permute-start(f32[6,8192]{1,0:T(8,128)S(1)} %edge_rows.3.send_b), channel_id=1, source_target_pairs={{1,2},{3,4},{5,6},{7,8},{9,10},{11,12},{13,14},{2,1},{4,3},{6,5},{... | collective-permute-start | bytes 589832 | tf_op jit(solution)/shard_map/ppermute | solution.py:916
  7.2 3.2 %copy-start = (f32[5,8,8192]{2,1,0:T(8,128)S(1)}, f32[5,8,8192]{2,1,0:T(8,128)}, u32[]{:S(2)}) copy-start(f32[5,8,8192]{2,1,0:T(8,128)} %q_ref.5) | copy-start | bytes 3932164
  7.2 3.2 %copy-start.1 = (f32[2,8,8192]{2,1,0:T(8,128)S(1)}, f32[2,8,8192]{2,1,0:T(8,128)}, u32[]{:S(2)}) copy-start(f32[2,8,8192]{2,1,0:T(8,128)} %w_ref.5) | copy-start | bytes 1572868
  13.5 31.9 %copy-start.8 = (s32[16,4]{0,1:T(4,128)S(1)}, s32[16,4]{0,1:T(4,128)}, u32[]{:S(2)}) copy-start(s32[16,4]{0,1:T(4,128)} %param.21) | copy-start | bytes 772
  25.9 2.6 %collective-permute-start.6 = (f32[8,8,512]{2,1,0:T(8,128)S(1)}, f32[8,8,512]{2,1,0:T(8,128)S(1)}, u32[]{:S(2)}, u32[]{:S(2)}) collective-permute-start(f32[8,8,512]{2,1,0:T(8,128)S(1)} %all_to_all.10.mine_ref), channel_id=1, source_target_pairs={{0,1},{1,0},{2,3},{3,2},{4,5},{5,4},{6,7},{7,6},{8,9},{9,8},{10,11... | collective-permute-start | bytes 393224 | tf_op jit(solution)/shard_map/ppermute | solution.py:851
  34.5 12.5 %copy-start.9 = (s32[16]{0:T(128)S(1)}, s32[16]{0:T(128)}, u32[]{:S(2)}) copy-start(s32[16]{0:T(128)} %param.22) | copy-start | bytes 196
  43.5 3.5 %collective-permute-start.7 = (f32[8,8,640]{2,1,0:T(8,128)S(1)}, f32[8,8,640]{2,1,0:T(8,128)S(1)}, u32[]{:S(2)}, u32[]{:S(2)}) collective-permute-start(f32[8,8,640]{2,1,0:T(8,128)S(1)} %all_to_all.11.mine_power), channel_id=1, source_target_pairs={{0,1},{1,0},{2,3},{3,2},{4,5},{5,4},{6,7},{7,6},{8,9},{9,8},{10,11... | collective-permute-start | bytes 491528 | tf_op jit(solution)/shard_map/ppermute | solution.py:851
  47.0 3.4 %copy-start.6 = (bf16[512,512]{1,0:T(8,128)(2,1)S(1)}, bf16[512,512]{1,0:T(8,128)(2,1)}, u32[]{:S(2)}) copy-start(bf16[512,512]{1,0:T(8,128)(2,1)} %get-tuple-element.834.centre_hbm) | copy-start | bytes 1572868

commit v9 on v7

--- a/solution.py
+++ b/solution.py
@@ -427,6 +427,24 @@
     most = steps_of(0)
     for tile in range(1, tiles):
         most = jnp.maximum(most, steps_of(tile))
+
+    skipped, per_tile, mine_first = size // CHUNK, width // CHUNK, size // width
+    per_block = size // width
+
+    def tiles_up_to(chunk):
+        return lax.div(chunk - skipped + (per_tile - 1), per_tile)
+
+    second_end = high_ref[mine_first]
+    for tile in range(mine_first + 1, 2 * mine_first):
+        second_end = jnp.maximum(second_end, high_ref[tile])
+    second_end = jnp.clip(tiles_up_to(second_end), 2 * per_block, 3 * per_block)
+    read_low, read_high = low_ref[mine_first], high_ref[mine_first]
+    for tile in range(mine_first + 1, 3 * per_block):
+        read = tile < second_end
+        read_low = jnp.minimum(read_low, jnp.where(read, low_ref[tile], read_low))
+        read_high = jnp.maximum(read_high, jnp.where(read, high_ref[tile], read_high))
+    first_start = jnp.clip(lax.div(jnp.maximum(read_low - skipped, 0), per_tile), 0, per_block)
+    first_end = jnp.clip(tiles_up_to(read_high), second_end, tiles)
     same = lax.broadcasted_iota(jnp.int32, (CHUNK, CHUNK), 0) == lax.broadcasted_iota(
         jnp.int32, (CHUNK, CHUNK), 1
     )
@@ -473,11 +491,20 @@
         both = image[:, (slot - 1) * size : slot * size]
         return jnp.where(live[slot], 4.0 * (both[:8] + both[8:]), 0.0)
 
-    def power(slots):
-        first, last = (slots[0] - 1) * size // width, slots[-1] * size // width
+    def power(slots, end):
+        first, last = (slots[0] - 1) * per_block, slots[-1] * per_block
         for tile in range(first, last):
-            image[:, tile * width : (tile + 1) * width] = one(tile, 0)
-        further(first, last)
+            here = slice(tile * width, (tile + 1) * width)
+            if tile < 2 * per_block:
+                image[:, here] = one(tile, 0)
+            else:
+                image[:, here] = jnp.zeros((16, width), F32)
+
+                @pl.when(tile < end)
+                def _(tile=tile, here=here):
+                    image[:, here] = one(tile, 0)
+
+        further(first, end)
         return {slot: image_of(slot) for slot in slots}
 
     def hold(values, slot):
@@ -486,14 +513,17 @@
     for slot in range(slots):
         hold(zeroth[slot], slot)
 
+    for tile in (*range(per_block), *range(2 * per_block, tiles)):
+        image[:, tile * width : (tile + 1) * width] = jnp.zeros((16, width), F32)
+
     def tile_step(tile, _):
-        before = jnp.maximum(tile - 1, 0)
+        before = jnp.maximum(tile - 1, first_start)
         image[:, lanes_of(before)] = one(before, 0)
         build(tile, 0)
         return 0
 
-    lax.fori_loop(0, tiles, tile_step, 0)
-    image[:, (tiles - 1) * width : tiles * width] = one(tiles - 1, 0)
+    lax.fori_loop(first_start, first_end, tile_step, 0)
+    image[:, lanes_of(first_end - 1)] = one(first_end - 1, 0)
 
     @pl.when(most > 1)
     def _():
@@ -504,17 +534,17 @@
 
             return lax.fori_loop(1, steps_of(tile), more, 0)
 
-        lax.fori_loop(0, tiles, of_tile, 0)
-
-    further(0, tiles)
+        lax.fori_loop(first_start, first_end, of_tile, 0)
+
+    further(first_start, first_end)
     first = {slot: image_of(slot) for slot in range(1, 5)}
     for slot in range(1, 5):
         hold(first[slot], slot)
-    second = power([2, 3])
+    second = power([2, 3], second_end)
     hold(jnp.zeros((8, size), F32), 1)
     hold(second[2], 2)
     hold(2.0 * second[3], 3)
-    last = power([2])[2]
+    last = power([2], 2 * per_block)[2]
 
     def inner(left, right):
         return jnp.sum(left * right, axis=1, keepdims=True)

time: 52.2 us -> 50.6 us (0.969)
  Pallas kernels: 18 us -> 16.4 us
    pallas_call x1, Pallas kernels: 5.97 us -> 4.33 us  [powers(): pl.pallas_call(functools.partial(powers_kernel, count), out_shape=(jax.Sh...]
  transfers between devices with their start and end apart: 4 -> 4, of which waited for: 3 -> 3; matrix products, arithmetic and copies ran while one was open for 0% -> 0% of each run, Pallas kernels for 12% -> 13%
where the time goes in v9:
time: 50.6 us; the launch traced here: 49.9 us
  blocking collectives  21.1 us (42%)
  Pallas kernels  16.4 us (32%)
  starting transfers between devices  8.02 us (16%)
  waiting for transfers between devices  2.46 us (5%)
  between operations  0.98 us (2%)
  loops' own time  0.87 us (2%)
    all_to_all x2, blocking collectives, gathered(): mine = lax.all_to_all(values, 'chip', 0, 0)  21.1 us
    ppermute x1, starting transfers between devices, shards(): from_b = lax.ppermute(send_b, SLAB, across)  4.52 us
    pallas_call x1, Pallas kernels, powers(): pl.pallas_call(functools.partial(powers_kernel, count), out_shape=(jax.Sh...  4.33 us
    pallas_call x1, Pallas kernels, near_body(): pl.pallas_call(near_kernel, out_shape=(jax.ShapeDtypeStruct((3, size), F3...  4.15 us
    ppermute x2, starting transfers between devices, gathered(): return (mine, lax.ppermute(mine, SLAB, partner))  3.42 us
    pallas_call x1, Pallas kernels, inner_flux(): pl.pallas_call(inner_kernel, out_shape=(pltpu.HBM(flow_state.shape, F32),...  3.02 us
    pallas_call x1, Pallas kernels, ordered(): pl.pallas_call(order_kernel, out_shape=(jax.ShapeDtypeStruct((16, count),...  2.06 us
    pallas_call x2, Pallas kernels, edge_rows(): pl.pallas_call(functools.partial(edge_kernel, even_last), out_shape=jax.S...  1.83 us
  transfers between devices with their start and end apart: 4, of which 3 were waited for; matrix products, arithmetic and copies ran while one was open for 0% of the time, Pallas kernels for 13%

profile of v9, /device:TPU:1, one launch (start us, length us, event | category | flops | bytes accessed | tf_op | source)
XLA Modules:
  0.0 49.9 jit_solution(13075578639773189709)
XLA Ops:
  0.6 0.0 copy-start.2
  0.6 0.0 copy-start.3
  0.7 0.0 copy-start.4
  0.7 0.0 copy-start.5
  0.7 0.0 copy-start.6
  0.7 0.9 %edge_rows.2.send_a = f32[6,8192]{1,0:T(8,128)S(1)} custom-call(f32[5,8,8192]{2,1,0:T(8,128)} %q_ref.5, f32[2,8,8192]{2,1,0:T(8,128)} %w_ref.5), custom_call_target="tpu_custom_call" | custom-call | tf_op jit(solution)/shard_map/edge_rows/pallas_call | solution.py:199
  1.6 0.1 collective-permute-start.4
  1.7 0.9 %edge_rows.3.send_b = f32[6,8192]{1,0:T(8,128)S(1)} custom-call(f32[5,8,8192]{2,1,0:T(8,128)} %q_ref.5, f32[2,8,8192]{2,1,0:T(8,128)} %w_ref.5), custom_call_target="tpu_custom_call" | custom-call | tf_op jit(solution)/shard_map/edge_rows/pallas_call | solution.py:199
  2.6 4.5 %collective-permute-start.5 = (f32[6,8192]{1,0:T(8,128)S(1)}, f32[6,8192]{1,0:T(8,128)S(1)}, u32[]{:S(2)}, u32[]{:S(2)}) collective-permute-start(f32[6,8192]{1,0:T(8,128)S(1)} %edge_rows.3.send_b), channel_id=1, source_target_pairs={{1,2},{3,4},{5,6},{7,8},{9,10},{11,12},{13,14},{2,1},{4,3},{6,5},{... | collective-permute-start | bytes 589832 | tf_op jit(solution)/shard_map/ppermute | solution.py:888
  7.1 0.0 copy-done.2
  7.1 0.0 copy-done.3
  7.2 0.0 copy-done.4
  7.2 0.0 copy-start
  7.2 0.0 copy-start.1
  7.2 2.1 %order.1 = (f32[16,512]{1,0:T(8,128)S(1)}, bf16[512,512]{1,0:T(8,128)(2,1)S(1)}, f32[8,1024]{1,0:T(8,128)S(1)}, bf16[1024,1024]{1,0:T(8,128)(2,1)S(1)}) custom-call(f32[3,512]{1,0:T(4,128)S(1)} %copy-done.2, f32[3,512]{1,0:T(4,128)S(1)} %copy-done.3, f32[3,512]{1,0:T(4,128)S(1)} %copy-done.4, s32[1,512]{1,0:T(1,128)S(1)} %bitcast.58, f32[3,1024]{1,0:T(4,128)S(1)} %copy-done.6), custom_call_target="tpu_custom_call" | custom-call | flops 2000000000 | bytes 4000000 | tf_op jit(solution)/shard_map/order/pallas_call | solution.py:155
  9.3 0.0 copy-done
  9.3 0.0 copy-done.1
  9.3 3.0 %inner_flux.1 = (f32[5,8,8192]{2,1,0:T(8,128)}, f32[5,8192]{1,0:T(8,128)S(1)}, f32[5,8192]{1,0:T(8,128)S(1)}, f32[16,512]{1,0:T(8,128)S(1)}, bf16[512,512]{1,0:T(8,128)(2,1)S(1)}) custom-call(f32[5,8,8192]{2,1,0:T(8,128)S(1)} %copy-done, f32[2,8,8192]{2,1,0:T(8,128)S(1)} %copy-done.1, f32[16,512]{1,0:T(8,128)S(1)} %get-tuple-element.437.sorted_ref), custom_call_target="tpu_custom_call" | custom-call | flops 20000000 | bytes 4000000 | tf_op jit(solution)/shard_map/inner_flux/pallas_call | solution.py:313
  12.3 0.0 collective-permute-done.4.from_a
  12.3 0.9 %collective-permute-done.5.from_b = f32[6,8192]{1,0:T(8,128)S(1)} collective-permute-done((f32[6,8192]{1,0:T(8,128)S(1)}, f32[6,8192]{1,0:T(8,128)S(1)}, u32[]{:S(2)}, u32[]{:S(2)}) %collective-permute-start.5) | collective-permute-done | bytes 196640 | tf_op jit(solution)/shard_map/ppermute | solution.py:888
  13.2 0.6 %outer_flux.1 = (f32[8,8,512]{2,1,0:T(8,128)S(1)}, f32[5,8192]{1,0:T(8,128)S(1)}, f32[5,8192]{1,0:T(8,128)S(1)}) custom-call(f32[6,8192]{1,0:T(8,128)S(1)} %edge_rows.2.send_a, f32[6,8192]{1,0:T(8,128)S(1)} %edge_rows.3.send_b, f32[6,8192]{1,0:T(8,128)S(1)} %collective-permute-done.4.from_a, f32[6,8192]{1,0:T(8,128)S(1)} %collective-permute-done.5.from_b, ...), custom_call_target="tpu_custom_call" | custom-call | tf_op jit(solution)/shard_map/outer_flux/pallas_call | solution.py:365
  13.9 12.1 %all_to_all.10.mine_ref = f32[8,8,512]{2,1,0:T(8,128)S(1)} all-to-all(f32[8,8,512]{2,1,0:T(8,128)S(1)} %get-tuple-element.831), channel_id=1, replica_groups=mesh['groups'=2,'chip'=8,'core'=2] {'chip'}, dimensions={0} | all-to-all | bytes 262144 | tf_op jit(solution)/shard_map/all_to_all | solution.py:822
  25.9 1.6 %collective-permute-start.6 = (f32[8,8,512]{2,1,0:T(8,128)S(1)}, f32[8,8,512]{2,1,0:T(8,128)S(1)}, u32[]{:S(2)}, u32[]{:S(2)}) collective-permute-start(f32[8,8,512]{2,1,0:T(8,128)S(1)} %all_to_all.10.mine_ref), channel_id=1, source_target_pairs={{0,1},{1,0},{2,3},{3,2},{4,5},{5,4},{6,7},{7,6},{8,9},{9,8},{10,11... | collective-permute-start | bytes 393224 | tf_op jit(solution)/shard_map/ppermute | solution.py:823
  27.5 1.0 %collective-permute-done.6.other_ref = f32[8,8,512]{2,1,0:T(8,128)S(1)} collective-permute-done((f32[8,8,512]{2,1,0:T(8,128)S(1)}, f32[8,8,512]{2,1,0:T(8,128)S(1)}, u32[]{:S(2)}, u32[]{:S(2)}) %collective-permute-start.6) | collective-permute-done | bytes 131104 | tf_op jit(solution)/shard_map/ppermute | solution.py:823
  28.5 4.3 %powers.1 = (f32[8,8,640]{2,1,0:T(8,128)S(1)}, f32[5,8,8192]{2,1,0:T(8,128)}) custom-call(f32[8,8,512]{2,1,0:T(8,128)S(1)} %all_to_all.10.mine_ref, f32[8,8,512]{2,1,0:T(8,128)S(1)} %collective-permute-done.6.other_ref, f32[5,8192]{1,0:T(8,128)S(1)} %get-tuple-element.443.new_low, ...), custom_call_target="tpu_custom_call", output_to_operand_aliasing={{1}: (4, {})} | custom-call | tf_op jit(solution)/shard_map/powers/pallas_call | solution.py:576
  32.9 9.0 %all_to_all.11.mine_power = f32[8,8,640]{2,1,0:T(8,128)S(1)} all-to-all(f32[8,8,640]{2,1,0:T(8,128)S(1)} %get-tuple-element.449), channel_id=1, replica_groups=mesh['groups'=2,'chip'=8,'core'=2] {'chip'}, dimensions={0} | all-to-all | bytes 327680 | tf_op jit(solution)/shard_map/all_to_all | solution.py:822
  41.8 1.8 %collective-permute-start.7 = (f32[8,8,640]{2,1,0:T(8,128)S(1)}, f32[8,8,640]{2,1,0:T(8,128)S(1)}, u32[]{:S(2)}, u32[]{:S(2)}) collective-permute-start(f32[8,8,640]{2,1,0:T(8,128)S(1)} %all_to_all.11.mine_power), channel_id=1, source_target_pairs={{0,1},{1,0},{2,3},{3,2},{4,5},{5,4},{6,7},{7,6},{8,9},{9,8},{10,11... | collective-permute-start | bytes 491528 | tf_op jit(solution)/shard_map/ppermute | solution.py:823
  43.7 0.1 copy.14.tile_ref
  43.8 0.4 near_points.1
  44.1 0.6 %collective-permute-done.7.other_power = f32[8,8,640]{2,1,0:T(8,128)S(1)} collective-permute-done((f32[8,8,640]{2,1,0:T(8,128)S(1)}, f32[8,8,640]{2,1,0:T(8,128)S(1)}, u32[]{:S(2)}, u32[]{:S(2)}) %collective-permute-start.7) | collective-permute-done | bytes 163872 | tf_op jit(solution)/shard_map/ppermute | solution.py:823
  44.7 4.2 %near_body.1 = (f32[3,512]{1,0:T(4,128)}, f32[3,1024]{1,0:T(4,128)}, f32[1,128]{1,0:T(1,128)}) custom-call(s32[16,4]{1,0:T(8,128)S(1)} %copy.14.tile_ref, s32[1,16]{1,0:T(1,128)S(1)} %bitcast.68, f32[2,8]{1,0:T(2,128)S(1)} %get-tuple-element.448.bound_ref, f32[8,8,512]{2,1,0:T(8,128)S(1)} %all_to_all.10.mine_ref, ...), custom_call_target="tpu_custom_call" | custom-call | tf_op jit(solution)/shard_map/near_body/pallas_call | solution.py:798
  48.9 0.9 %while.71 = (f32[1,128]{1,0:T(1,128)}, f32[3,512]{1,0:T(4,128)}, f32[3,1024]{1,0:T(4,128)}, f32[8,8,512]{2,1,0:T(8,128)S(1)}, bf16[512,512]{1,0:T(8,128)(2,1)S(1...) while((f32[1,128]{1,0:T(1,128)}, f32[3,512]{1,0:T(4,128)}, ...), condition=%wide.region_11.12_spmd, body=%wide.region_0.11_spmd.sunk | while | flops 78180960 | bytes 1274309 | solution.py:913
  (6 shorter events, 0.0 us)
Async XLA Ops:
  0.6 6.5 %copy-start.2 = (f32[3,512]{1,0:T(4,128)S(1)}, f32[3,512]{1,0:T(4,128)}, u32[]{:S(2)}) copy-start(f32[3,512]{1,0:T(4,128)} %base_ref.1) | copy-start | bytes 18436
  0.6 6.5 %copy-start.3 = (f32[3,512]{1,0:T(4,128)S(1)}, f32[3,512]{1,0:T(4,128)}, u32[]{:S(2)}) copy-start(f32[3,512]{1,0:T(4,128)} %normal_ref.1) | copy-start | bytes 18436
  0.7 6.5 %copy-start.4 = (f32[3,512]{1,0:T(4,128)S(1)}, f32[3,512]{1,0:T(4,128)}, u32[]{:S(2)}) copy-start(f32[3,512]{1,0:T(4,128)} %centre_ref.1) | copy-start | bytes 18436
  0.7 6.5 %copy-start.5 = (s32[512]{0:T(512)S(1)}, s32[512]{0:T(512)}, u32[]{:S(2)}) copy-start(s32[512]{0:T(512)} %param.17) | copy-start | bytes 6148
  0.7 6.5 %copy-start.6 = (f32[3,1024]{1,0:T(4,128)S(1)}, f32[3,1024]{1,0:T(4,128)}, u32[]{:S(2)}) copy-start(f32[3,1024]{1,0:T(4,128)} %nodes_ref.1) | copy-start | bytes 36868
  1.6 10.7 %collective-permute-start.4 = (f32[6,8192]{1,0:T(8,128)S(1)}, f32[6,8192]{1,0:T(8,128)S(1)}, u32[]{:S(2)}, u32[]{:S(2)}) collective-permute-start(f32[6,8192]{1,0:T(8,128)S(1)} %edge_rows.2.send_a), channel_id=1, source_target_pairs={{0,1},{1,0},{2,3},{3,2},{4,5},{5,4},{6,7},{7,6},{8,9},{9,8},{10,11... | collective-permute-start | bytes 589832 | tf_op jit(solution)/shard_map/ppermute | solution.py:890
  2.6 10.6 %collective-permute-start.5 = (f32[6,8192]{1,0:T(8,128)S(1)}, f32[6,8192]{1,0:T(8,128)S(1)}, u32[]{:S(2)}, u32[]{:S(2)}) collective-permute-start(f32[6,8192]{1,0:T(8,128)S(1)} %edge_rows.3.send_b), channel_id=1, source_target_pairs={{1,2},{3,4},{5,6},{7,8},{9,10},{11,12},{13,14},{2,1},{4,3},{6,5},{... | collective-permute-start | bytes 589832 | tf_op jit(solution)/shard_map/ppermute | solution.py:888
  7.2 2.1 %copy-start = (f32[5,8,8192]{2,1,0:T(8,128)S(1)}, f32[5,8,8192]{2,1,0:T(8,128)}, u32[]{:S(2)}) copy-start(f32[5,8,8192]{2,1,0:T(8,128)} %q_ref.5) | copy-start | bytes 3932164
  7.2 2.1 %copy-start.1 = (f32[2,8,8192]{2,1,0:T(8,128)S(1)}, f32[2,8,8192]{2,1,0:T(8,128)}, u32[]{:S(2)}) copy-start(f32[2,8,8192]{2,1,0:T(8,128)} %w_ref.5) | copy-start | bytes 1572868
  13.2 30.4 %copy-start.7 = (s32[16,4]{0,1:T(4,128)S(1)}, s32[16,4]{0,1:T(4,128)}, u32[]{:S(2)}) copy-start(s32[16,4]{0,1:T(4,128)} %param.21) | copy-start | bytes 772
  13.2 31.5 %copy-start.8 = (s32[16]{0:T(128)S(1)}, s32[16]{0:T(128)}, u32[]{:S(2)}) copy-start(s32[16]{0:T(128)} %param.22) | copy-start | bytes 196
  25.9 2.6 %collective-permute-start.6 = (f32[8,8,512]{2,1,0:T(8,128)S(1)}, f32[8,8,512]{2,1,0:T(8,128)S(1)}, u32[]{:S(2)}, u32[]{:S(2)}) collective-permute-start(f32[8,8,512]{2,1,0:T(8,128)S(1)} %all_to_all.10.mine_ref), channel_id=1, source_target_pairs={{0,1},{1,0},{2,3},{3,2},{4,5},{5,4},{6,7},{7,6},{8,9},{9,8},{10,11... | collective-permute-start | bytes 393224 | tf_op jit(solution)/shard_map/ppermute | solution.py:823
  41.8 2.9 %collective-permute-start.7 = (f32[8,8,640]{2,1,0:T(8,128)S(1)}, f32[8,8,640]{2,1,0:T(8,128)S(1)}, u32[]{:S(2)}, u32[]{:S(2)}) collective-permute-start(f32[8,8,640]{2,1,0:T(8,128)S(1)} %all_to_all.11.mine_power), channel_id=1, source_target_pairs={{0,1},{1,0},{2,3},{3,2},{4,5},{5,4},{6,7},{7,6},{8,9},{9,8},{10,11... | collective-permute-start | bytes 491528 | tf_op jit(solution)/shard_map/ppermute | solution.py:823

commit v10 on v9

--- a/solution.py
+++ b/solution.py
@@ -671,7 +671,30 @@
     return tile_ref[pl.ds(me, 1), :][0, 0]
 
 
-def points_kernel(tile_ref, mine_ref, other_ref, nodes_ref, source_ref, target_ref, bound_ref):
+def scalars_of(bound_ref, low_ref, step_ref):
+    bounds = bound_ref[...].astype(jnp.int32)
+    most = 0
+    for tile in range(bounds.shape[1]):
+        low = bounds[0, tile]
+        steps = lax.div(bounds[1, tile] - low + (REACH - 1), REACH)
+        low_ref[tile] = low
+        step_ref[tile] = steps
+        most = jnp.maximum(most, steps)
+    return most
+
+
+def near_table(source_ref, target_ref, low_ref, tile, step):
+    start = pl.multiple_of((low_ref[tile] + step * REACH) * CHUNK, CHUNK)
+    lanes = pl.ds(pl.multiple_of(tile * CHUNK, CHUNK), CHUNK)
+    return doubled(quarter_kernel(source_ref[pl.ds(start, REACH * CHUNK)], target_ref[:, lanes]))
+
+
+EARLY = 2
+
+
+def points_kernel(
+    tile_ref, mine_ref, other_ref, nodes_ref, source_ref, target_ref, bound_ref, table_ref, low_ref, step_ref
+):
     size = mine_ref.shape[2]
     core = lax.axis_index("core")
     me = lax.axis_index("chip") * 2 + core
@@ -692,6 +715,9 @@
     _, target = sides(points)
     target_ref[...] = target.astype(BF16)
     bound_ref[...] = bounds_of(jnp.concatenate(third, axis=1), points[2:3])
+    scalars_of(bound_ref, low_ref, step_ref)
+    for tile in range(EARLY):
+        table_ref[tile] = near_table(source_ref, target_ref, low_ref, tile, 0)
 
 
 def near_points(tile_blocks, mine, other, nodes):
@@ -704,9 +730,14 @@
             jax.ShapeDtypeStruct((listed * size + REACH * CHUNK, 48), BF16),
             jax.ShapeDtypeStruct((48, slots), BF16),
             jax.ShapeDtypeStruct((2, slots // CHUNK), F32),
+            jax.ShapeDtypeStruct((EARLY, 2 * REACH * CHUNK, CHUNK), BF16),
         ),
         in_specs=[VMEM] * 4,
-        out_specs=(VMEM,) * 3,
+        out_specs=(VMEM,) * 4,
+        scratch_shapes=[
+            pltpu.SMEM((slots // CHUNK,), jnp.int32),
+            pltpu.SMEM((slots // CHUNK,), jnp.int32),
+        ],
         compiler_params=pltpu.CompilerParams(vmem_limit_bytes=SMALL_LIMIT),
         cost_estimate=pl.CostEstimate(flops=1_000_000, bytes_accessed=1_000_000, transcendentals=0),
         name="near_points",
@@ -715,7 +746,7 @@
 
 def near_kernel(
     tile_ref, count_ref, bound_ref, mine_ref, other_ref, mine_power, other_power, source_side, target_side,
-    centre_table, node_table, coef_ref, shift_ref, lost_ref, vector, result, low_ref, step_ref,
+    table_ref, centre_table, node_table, coef_ref, shift_ref, lost_ref, vector, result, low_ref, step_ref,
 ):
     size = mine_ref.shape[2]
     slots = target_side.shape[1]
@@ -729,15 +760,7 @@
     span = REACH * CHUNK
     total = listed * size
 
-    bounds = bound_ref[...].astype(jnp.int32)
-    most = 0
-    for tile in range(tiles):
-        low = bounds[0, tile]
-        steps = lax.div(bounds[1, tile] - low + (REACH - 1), REACH)
-        low_ref[tile] = low
-        step_ref[tile] = steps
-        most = jnp.maximum(most, steps)
-
+    most = scalars_of(bound_ref, low_ref, step_ref)
     summed = mine_power[0, :, size:] + other_power[0, :, size:]
     for index in range(1, chips):
         summed = summed + (mine_power[index, :, size:] + other_power[index, :, size:])
@@ -759,24 +782,29 @@
     def lanes_of(tile):
         return pl.ds(pl.multiple_of(tile * width, width), width)
 
-    def one(tile, step):
+    def one(tile, step, table):
         start = pl.multiple_of((low_ref[tile] + step * REACH) * CHUNK, CHUNK)
-        table = quarter_kernel(source_side[pl.ds(start, span)], target_side[:, lanes_of(tile)])
         window = vector[:, pl.ds(start, span)]
-        return jnp.dot(jnp.concatenate([window, window], axis=1), doubled(table), preferred_element_type=F32)
+        return jnp.dot(jnp.concatenate([window, window], axis=1), table, preferred_element_type=F32)
+
+    for tile in range(EARLY):
+        result[:, tile * width : (tile + 1) * width] = one(tile, 0, table_ref[tile])
 
     def two_tiles(step, _):
         for piece in range(2):
-            result[:, lanes_of(2 * step + piece)] = one(2 * step + piece, 0)
+            tile = EARLY + 2 * step + piece
+            table = near_table(source_side, target_side, low_ref, tile, 0)
+            result[:, lanes_of(tile)] = one(tile, 0, table)
         return 0
 
-    lax.fori_loop(0, tiles // 2, two_tiles, 0)
+    lax.fori_loop(0, (tiles - EARLY) // 2, two_tiles, 0)
 
     @pl.when(most > 1)
     def _():
         def of_tile(tile, _):
             def add(step, _):
-                result[:, lanes_of(tile)] += one(tile, step)
+                table = near_table(source_side, target_side, low_ref, tile, step)
+                result[:, lanes_of(tile)] += one(tile, step, table)
                 return 0
 
             return lax.fori_loop(1, step_ref[tile], add, 0)
@@ -791,7 +819,7 @@
     shift_ref[...] = jnp.where(slot < live, shift, 0.0)
 
 
-def near_body(tile_blocks, near_count, bounds, mine, other, mine_power, other_power, sources, targets, centre_table, node_table):
+def near_body(tile_blocks, near_count, bounds, mine, other, mine_power, other_power, sources, targets, tables, centre_table, node_table):
     size = mine.shape[2]
     slots = targets.shape[1]
     total = tile_blocks.shape[1] * size
@@ -802,7 +830,7 @@
             jax.ShapeDtypeStruct((3, slots), F32),
             jax.ShapeDtypeStruct((1, 128), F32),
         ),
-        in_specs=[VMEM] * 11,
+        in_specs=[VMEM] * 12,
         out_specs=(VMEM,) * 3,
         scratch_shapes=[
             pltpu.VMEM((16, total + REACH * CHUNK), BF16),
@@ -814,7 +842,7 @@
         name="near_body",
     )(
         tile_blocks, near_count.reshape(1, -1), bounds, mine, other, mine_power, other_power, sources, targets,
-        centre_table, node_table,
+        tables, centre_table, node_table,
     )
 
 
@@ -894,10 +922,10 @@
     mine, other = gathered(packed, partner)
     power, new_flow = powers(mine, other, low, high, new_flow, count)
     mine_power, other_power = gathered(power, partner)
-    sources, targets, bounds = near_points(tile_blocks, mine, other, nodes)
+    sources, targets, bounds, tables = near_points(tile_blocks, mine, other, nodes)
     coefficients, node_shift, lost = near_body(
         tile_blocks, near_count, bounds, mine, other, mine_power, other_power, sources, targets,
-        centre_table, node_table,
+        tables, centre_table, node_table,
     )
 
     def again(held):

time: 50.6 us -> 50 us (0.988)
  waiting for transfers between devices: 2.46 us -> 1.89 us
    ppermute x2, waiting for transfers between devices: 1.56 us -> 1 us  [gathered(): return (mine, lax.ppermute(mine, SLAB, partner))]
    pallas_call x1, Pallas kernels: 0.36 us -> 0.93 us  [near_points(): pl.pallas_call(points_kernel, out_shape=(jax.ShapeDtypeStruct((listed * s...]
    pallas_call x1, Pallas kernels: 4.15 us -> 3.59 us  [near_body(): pl.pallas_call(near_kernel, out_shape=(jax.ShapeDtypeStruct((3, size), F3...]
  transfers between devices with their start and end apart: 4 -> 4, of which waited for: 3 -> 2; matrix products, arithmetic and copies ran while one was open for 0% -> 0% of each run, Pallas kernels for 13% -> 14%
where the time goes in v10:
time: 50 us; the launch traced here: 49.3 us
  blocking collectives  21.1 us (42%)
  Pallas kernels  16.4 us (33%)
  starting transfers between devices  8.02 us (16%)
  waiting for transfers between devices  1.89 us (4%)
  between operations  1 us (2%)
  loops' own time  0.87 us (2%)
    all_to_all x2, blocking collectives, gathered(): mine = lax.all_to_all(values, 'chip', 0, 0)  21.1 us
    ppermute x1, starting transfers between devices, shards(): from_b = lax.ppermute(send_b, SLAB, across)  4.52 us
    pallas_call x1, Pallas kernels, powers(): pl.pallas_call(functools.partial(powers_kernel, count), out_shape=(jax.Sh...  4.33 us
    pallas_call x1, Pallas kernels, near_body(): pl.pallas_call(near_kernel, out_shape=(jax.ShapeDtypeStruct((3, size), F3...  3.59 us
    ppermute x2, starting transfers between devices, gathered(): return (mine, lax.ppermute(mine, SLAB, partner))  3.42 us
    pallas_call x1, Pallas kernels, inner_flux(): pl.pallas_call(inner_kernel, out_shape=(pltpu.HBM(flow_state.shape, F32),...  3.02 us
    pallas_call x1, Pallas kernels, ordered(): pl.pallas_call(order_kernel, out_shape=(jax.ShapeDtypeStruct((16, count),...  2.06 us
    pallas_call x2, Pallas kernels, edge_rows(): pl.pallas_call(functools.partial(edge_kernel, even_last), out_shape=jax.S...  1.83 us
  transfers between devices with their start and end apart: 4, of which 2 were waited for; matrix products, arithmetic and copies ran while one was open for 0% of the time, Pallas kernels for 14%

profile of v10, /device:TPU:1, one launch (start us, length us, event | category | flops | bytes accessed | tf_op | source)
XLA Modules:
  0.0 49.3 jit_solution(7608199183364433255)
XLA Ops:
  0.6 0.0 copy-start.2
  0.6 0.0 copy-start.3
  0.7 0.0 copy-start.4
  0.7 0.0 copy-start.5
  0.7 0.0 copy-start.6
  0.7 0.9 %edge_rows.2.send_a = f32[6,8192]{1,0:T(8,128)S(1)} custom-call(f32[5,8,8192]{2,1,0:T(8,128)} %q_ref.5, f32[2,8,8192]{2,1,0:T(8,128)} %w_ref.5), custom_call_target="tpu_custom_call" | custom-call | tf_op jit(solution)/shard_map/edge_rows/pallas_call | solution.py:199
  1.6 0.1 collective-permute-start.4
  1.7 0.9 %edge_rows.3.send_b = f32[6,8192]{1,0:T(8,128)S(1)} custom-call(f32[5,8,8192]{2,1,0:T(8,128)} %q_ref.5, f32[2,8,8192]{2,1,0:T(8,128)} %w_ref.5), custom_call_target="tpu_custom_call" | custom-call | tf_op jit(solution)/shard_map/edge_rows/pallas_call | solution.py:199
  2.6 4.5 %collective-permute-start.5 = (f32[6,8192]{1,0:T(8,128)S(1)}, f32[6,8192]{1,0:T(8,128)S(1)}, u32[]{:S(2)}, u32[]{:S(2)}) collective-permute-start(f32[6,8192]{1,0:T(8,128)S(1)} %edge_rows.3.send_b), channel_id=1, source_target_pairs={{1,2},{3,4},{5,6},{7,8},{9,10},{11,12},{13,14},{2,1},{4,3},{6,5},{... | collective-permute-start | bytes 589832 | tf_op jit(solution)/shard_map/ppermute | solution.py:916
  7.1 0.0 copy-done.2
  7.1 0.0 copy-done.3
  7.2 0.0 copy-done.4
  7.2 0.0 copy-start
  7.2 0.0 copy-start.1
  7.2 2.1 %order.1 = (f32[16,512]{1,0:T(8,128)S(1)}, bf16[512,512]{1,0:T(8,128)(2,1)S(1)}, f32[8,1024]{1,0:T(8,128)S(1)}, bf16[1024,1024]{1,0:T(8,128)(2,1)S(1)}) custom-call(f32[3,512]{1,0:T(4,128)S(1)} %copy-done.2, f32[3,512]{1,0:T(4,128)S(1)} %copy-done.3, f32[3,512]{1,0:T(4,128)S(1)} %copy-done.4, s32[1,512]{1,0:T(1,128)S(1)} %bitcast.58, f32[3,1024]{1,0:T(4,128)S(1)} %copy-done.6), custom_call_target="tpu_custom_call" | custom-call | flops 2000000000 | bytes 4000000 | tf_op jit(solution)/shard_map/order/pallas_call | solution.py:155
  9.3 0.0 copy-done
  9.3 0.0 copy-done.1
  9.3 3.0 %inner_flux.1 = (f32[5,8,8192]{2,1,0:T(8,128)}, f32[5,8192]{1,0:T(8,128)S(1)}, f32[5,8192]{1,0:T(8,128)S(1)}, f32[16,512]{1,0:T(8,128)S(1)}, bf16[512,512]{1,0:T(8,128)(2,1)S(1)}) custom-call(f32[5,8,8192]{2,1,0:T(8,128)S(1)} %copy-done, f32[2,8,8192]{2,1,0:T(8,128)S(1)} %copy-done.1, f32[16,512]{1,0:T(8,128)S(1)} %get-tuple-element.438.sorted_ref), custom_call_target="tpu_custom_call" | custom-call | flops 20000000 | bytes 4000000 | tf_op jit(solution)/shard_map/inner_flux/pallas_call | solution.py:313
  12.3 0.0 collective-permute-done.4.from_a
  12.3 0.9 %collective-permute-done.5.from_b = f32[6,8192]{1,0:T(8,128)S(1)} collective-permute-done((f32[6,8192]{1,0:T(8,128)S(1)}, f32[6,8192]{1,0:T(8,128)S(1)}, u32[]{:S(2)}, u32[]{:S(2)}) %collective-permute-start.5) | collective-permute-done | bytes 196640 | tf_op jit(solution)/shard_map/ppermute | solution.py:916
  13.2 0.6 %outer_flux.1 = (f32[8,8,512]{2,1,0:T(8,128)S(1)}, f32[5,8192]{1,0:T(8,128)S(1)}, f32[5,8192]{1,0:T(8,128)S(1)}) custom-call(f32[6,8192]{1,0:T(8,128)S(1)} %edge_rows.2.send_a, f32[6,8192]{1,0:T(8,128)S(1)} %edge_rows.3.send_b, f32[6,8192]{1,0:T(8,128)S(1)} %collective-permute-done.4.from_a, f32[6,8192]{1,0:T(8,128)S(1)} %collective-permute-done.5.from_b, ...), custom_call_target="tpu_custom_call" | custom-call | tf_op jit(solution)/shard_map/outer_flux/pallas_call | solution.py:365
  13.9 12.1 %all_to_all.10.mine_ref = f32[8,8,512]{2,1,0:T(8,128)S(1)} all-to-all(f32[8,8,512]{2,1,0:T(8,128)S(1)} %get-tuple-element.833), channel_id=1, replica_groups=mesh['groups'=2,'chip'=8,'core'=2] {'chip'}, dimensions={0} | all-to-all | bytes 262144 | tf_op jit(solution)/shard_map/all_to_all | solution.py:850
  25.9 1.6 %collective-permute-start.6 = (f32[8,8,512]{2,1,0:T(8,128)S(1)}, f32[8,8,512]{2,1,0:T(8,128)S(1)}, u32[]{:S(2)}, u32[]{:S(2)}) collective-permute-start(f32[8,8,512]{2,1,0:T(8,128)S(1)} %all_to_all.10.mine_ref), channel_id=1, source_target_pairs={{0,1},{1,0},{2,3},{3,2},{4,5},{5,4},{6,7},{7,6},{8,9},{9,8},{10,11... | collective-permute-start | bytes 393224 | tf_op jit(solution)/shard_map/ppermute | solution.py:851
  27.5 1.0 %collective-permute-done.6.other_ref = f32[8,8,512]{2,1,0:T(8,128)S(1)} collective-permute-done((f32[8,8,512]{2,1,0:T(8,128)S(1)}, f32[8,8,512]{2,1,0:T(8,128)S(1)}, u32[]{:S(2)}, u32[]{:S(2)}) %collective-permute-start.6) | collective-permute-done | bytes 131104 | tf_op jit(solution)/shard_map/ppermute | solution.py:851
  28.5 4.3 %powers.1 = (f32[8,8,640]{2,1,0:T(8,128)S(1)}, f32[5,8,8192]{2,1,0:T(8,128)}) custom-call(f32[8,8,512]{2,1,0:T(8,128)S(1)} %all_to_all.10.mine_ref, f32[8,8,512]{2,1,0:T(8,128)S(1)} %collective-permute-done.6.other_ref, f32[5,8192]{1,0:T(8,128)S(1)} %get-tuple-element.444.new_low, ...), custom_call_target="tpu_custom_call", output_to_operand_aliasing={{1}: (4, {})} | custom-call | tf_op jit(solution)/shard_map/powers/pallas_call | solution.py:576
  32.9 9.0 %all_to_all.11.mine_power = f32[8,8,640]{2,1,0:T(8,128)S(1)} all-to-all(f32[8,8,640]{2,1,0:T(8,128)S(1)} %get-tuple-element.450), channel_id=1, replica_groups=mesh['groups'=2,'chip'=8,'core'=2] {'chip'}, dimensions={0} | all-to-all | bytes 327680 | tf_op jit(solution)/shard_map/all_to_all | solution.py:850
  41.8 1.8 %collective-permute-start.7 = (f32[8,8,640]{2,1,0:T(8,128)S(1)}, f32[8,8,640]{2,1,0:T(8,128)S(1)}, u32[]{:S(2)}, u32[]{:S(2)}) collective-permute-start(f32[8,8,640]{2,1,0:T(8,128)S(1)} %all_to_all.11.mine_power), channel_id=1, source_target_pairs={{0,1},{1,0},{2,3},{3,2},{4,5},{5,4},{6,7},{7,6},{8,9},{9,8},{10,11... | collective-permute-start | bytes 491528 | tf_op jit(solution)/shard_map/ppermute | solution.py:851
  43.7 0.1 copy.14.tile_ref
  43.8 0.9 %near_points.1 = (bf16[2944,48]{1,0:T(8,128)(2,1)S(1)}, bf16[48,1024]{1,0:T(8,128)(2,1)S(1)}, f32[2,8]{1,0:T(2,128)S(1)}, bf16[2,1792,128]{2,1,0:T(8,128)(2,1)S(1)}) custom-call(s32[16,4]{1,0:T(8,128)S(1)} %copy.14.tile_ref, f32[8,8,512]{2,1,0:T(8,128)S(1)} %all_to_all.10.mine_ref, f32[8,8,512]{2,1,0:T(8,128)S(1)} %collective-permute-done.6.other_ref, ...), custom_call_target="tpu_custom_call" | custom-call | flops 1000000 | bytes 1000000 | tf_op jit(solution)/shard_map/near_points/pallas_call | solution.py:727
  44.7 0.0 collective-permute-done.7.other_power
  44.7 3.6 %near_body.1 = (f32[3,512]{1,0:T(4,128)}, f32[3,1024]{1,0:T(4,128)}, f32[1,128]{1,0:T(1,128)}) custom-call(s32[16,4]{1,0:T(8,128)S(1)} %copy.14.tile_ref, s32[1,16]{1,0:T(1,128)S(1)} %bitcast.68, f32[2,8]{1,0:T(2,128)S(1)} %get-tuple-element.449.bound_ref, f32[8,8,512]{2,1,0:T(8,128)S(1)} %all_to_all.10.mine_ref, ...), custom_call_target="tpu_custom_call" | custom-call | tf_op jit(solution)/shard_map/near_body/pallas_call | solution.py:826
  48.3 0.9 %while.71 = (f32[1,128]{1,0:T(1,128)}, f32[3,512]{1,0:T(4,128)}, f32[3,1024]{1,0:T(4,128)}, f32[8,8,512]{2,1,0:T(8,128)S(1)}, bf16[512,512]{1,0:T(8,128)(2,1)S(1...) while((f32[1,128]{1,0:T(1,128)}, f32[3,512]{1,0:T(4,128)}, ...), condition=%wide.region_11.12_spmd, body=%wide.region_0.11_spmd.sunk | while | flops 78180960 | bytes 1274309 | solution.py:941
  (6 shorter events, 0.0 us)
Async XLA Ops:
  0.6 6.5 %copy-start.2 = (f32[3,512]{1,0:T(4,128)S(1)}, f32[3,512]{1,0:T(4,128)}, u32[]{:S(2)}) copy-start(f32[3,512]{1,0:T(4,128)} %base_ref.1) | copy-start | bytes 18436
  0.6 6.5 %copy-start.3 = (f32[3,512]{1,0:T(4,128)S(1)}, f32[3,512]{1,0:T(4,128)}, u32[]{:S(2)}) copy-start(f32[3,512]{1,0:T(4,128)} %normal_ref.1) | copy-start | bytes 18436
  0.7 6.5 %copy-start.4 = (f32[3,512]{1,0:T(4,128)S(1)}, f32[3,512]{1,0:T(4,128)}, u32[]{:S(2)}) copy-start(f32[3,512]{1,0:T(4,128)} %centre_ref.1) | copy-start | bytes 18436
  0.7 6.5 %copy-start.5 = (s32[512]{0:T(512)S(1)}, s32[512]{0:T(512)}, u32[]{:S(2)}) copy-start(s32[512]{0:T(512)} %param.17) | copy-start | bytes 6148
  0.7 6.5 %copy-start.6 = (f32[3,1024]{1,0:T(4,128)S(1)}, f32[3,1024]{1,0:T(4,128)}, u32[]{:S(2)}) copy-start(f32[3,1024]{1,0:T(4,128)} %nodes_ref.1) | copy-start | bytes 36868
  1.6 10.7 %collective-permute-start.4 = (f32[6,8192]{1,0:T(8,128)S(1)}, f32[6,8192]{1,0:T(8,128)S(1)}, u32[]{:S(2)}, u32[]{:S(2)}) collective-permute-start(f32[6,8192]{1,0:T(8,128)S(1)} %edge_rows.2.send_a), channel_id=1, source_target_pairs={{0,1},{1,0},{2,3},{3,2},{4,5},{5,4},{6,7},{7,6},{8,9},{9,8},{10,11... | collective-permute-start | bytes 589832 | tf_op jit(solution)/shard_map/ppermute | solution.py:918
  2.6 10.6 %collective-permute-start.5 = (f32[6,8192]{1,0:T(8,128)S(1)}, f32[6,8192]{1,0:T(8,128)S(1)}, u32[]{:S(2)}, u32[]{:S(2)}) collective-permute-start(f32[6,8192]{1,0:T(8,128)S(1)} %edge_rows.3.send_b), channel_id=1, source_target_pairs={{1,2},{3,4},{5,6},{7,8},{9,10},{11,12},{13,14},{2,1},{4,3},{6,5},{... | collective-permute-start | bytes 589832 | tf_op jit(solution)/shard_map/ppermute | solution.py:916
  7.2 2.1 %copy-start = (f32[5,8,8192]{2,1,0:T(8,128)S(1)}, f32[5,8,8192]{2,1,0:T(8,128)}, u32[]{:S(2)}) copy-start(f32[5,8,8192]{2,1,0:T(8,128)} %q_ref.5) | copy-start | bytes 3932164
  7.2 2.1 %copy-start.1 = (f32[2,8,8192]{2,1,0:T(8,128)S(1)}, f32[2,8,8192]{2,1,0:T(8,128)}, u32[]{:S(2)}) copy-start(f32[2,8,8192]{2,1,0:T(8,128)} %w_ref.5) | copy-start | bytes 1572868
  13.2 30.4 %copy-start.7 = (s32[16,4]{0,1:T(4,128)S(1)}, s32[16,4]{0,1:T(4,128)}, u32[]{:S(2)}) copy-start(s32[16,4]{0,1:T(4,128)} %param.21) | copy-start | bytes 772
  13.2 31.5 %copy-start.8 = (s32[16]{0:T(128)S(1)}, s32[16]{0:T(128)}, u32[]{:S(2)}) copy-start(s32[16]{0:T(128)} %param.22) | copy-start | bytes 196
  25.9 2.6 %collective-permute-start.6 = (f32[8,8,512]{2,1,0:T(8,128)S(1)}, f32[8,8,512]{2,1,0:T(8,128)S(1)}, u32[]{:S(2)}, u32[]{:S(2)}) collective-permute-start(f32[8,8,512]{2,1,0:T(8,128)S(1)} %all_to_all.10.mine_ref), channel_id=1, source_target_pairs={{0,1},{1,0},{2,3},{3,2},{4,5},{5,4},{6,7},{7,6},{8,9},{9,8},{10,11... | collective-permute-start | bytes 393224 | tf_op jit(solution)/shard_map/ppermute | solution.py:851
  41.8 2.9 %collective-permute-start.7 = (f32[8,8,640]{2,1,0:T(8,128)S(1)}, f32[8,8,640]{2,1,0:T(8,128)S(1)}, u32[]{:S(2)}, u32[]{:S(2)}) collective-permute-start(f32[8,8,640]{2,1,0:T(8,128)S(1)} %all_to_all.11.mine_power), channel_id=1, source_target_pairs={{0,1},{1,0},{2,3},{3,2},{4,5},{5,4},{6,7},{7,6},{8,9},{9,8},{10,11... | collective-permute-start | bytes 491528 | tf_op jit(solution)/shard_map/ppermute | solution.py:851
